TPU v7x, 256 devices: a whole 4x4x8 slice. The times are simulated.
256 devices in a mesh: grid: 64 (over z_hi, y, x, core), orb: 4 (over z_lo).
Axes of the slice: x: 4, y: 4, z: 8 (z_hi: 2, z_lo: 4; z = z_hi * 4 + z_lo), core: 2. Of those that a mesh axis runs over, the one named last changes fastest.
Arguments:
- psi_in: float32 [128, 384, 8, 128], P('orb', 'grid')
- v_local: float32 [384, 8, 128], P('grid'), may hold values from -3 to 0.5
- proj_index: int32 [192, 4, 128], P('grid'), may hold values from 0 to 6143
- proj_value: float32 [192, 4, 4, 128], P('grid'), may hold values from -1.2 to 1.2
- kb_energy: float32 [256, 4], P('grid'), may hold values from 0.5 to 3
Outputs:
- filtered: float32 [128, 384, 8, 128], P('orb', 'grid')
- gram: float32 [128, 128], P('orb', 'grid')
All inputs are finite; a program needn't handle non-finite values.
Results may differ from a plain program's by a relative error of at most 0.00005.
Values sent between devices are 32-bit elements; how exact they have to be, the bound alone decides.
No kernel may reach another device: no remote copies, remote signals or barrier semaphores. Data moves between devices by JAX's collectives and lax.ppermute only.
A program may use at most 128 MiB of HBM per device.

v0:
```python
import jax
import jax.numpy as jnp
from jax import lax
from jax.sharding import PartitionSpec as P

LAP_COEF = (
    -5369.0 / 1800.0,
    12.0 / 7.0,
    -15.0 / 56.0,
    10.0 / 189.0,
    -1.0 / 112.0,
    2.0 / 1925.0,
    -1.0 / 16632.0,
)
HIGH = lax.Precision.HIGHEST


def with_halo(cells, sides, width):
    for axis, dim in sides:
        count = lax.axis_size(axis)
        head = lax.slice_in_dim(cells, 0, width, axis=dim)
        tail = lax.slice_in_dim(cells, cells.shape[dim] - width, cells.shape[dim], axis=dim)
        cells = jnp.concatenate(
            [
                lax.ppermute(tail, axis, [(i, (i + 1) % count) for i in range(count)]),
                cells,
                lax.ppermute(head, axis, [((i + 1) % count, i) for i in range(count)]),
            ],
            axis=dim,
        )
    return cells


def nonlocal_part(field, proj_index, proj_value, kb_energy):
    orbitals = field.shape[0]
    slots = proj_index.shape[1]
    points = proj_index.shape[2]
    flattened = field.reshape(orbitals, -1)
    columns = proj_index.reshape(-1)
    picked = jnp.take(flattened, columns, axis=1).reshape(orbitals, 3, slots, points)
    partial_value = jnp.einsum("kamp,okap->kamo", proj_value, picked, precision=HIGH)
    outgoing = jnp.stack([partial_value[0], partial_value[2]])
    arrived = with_halo(outgoing, (("grid", 0),), 1)
    summed = partial_value[1] + arrived[0] + arrived[3]
    scaled = summed * kb_energy[:, :, None]
    returned = with_halo(scaled[None], (("grid", 0),), 1)
    contrib = jnp.einsum("kamp,kamo->okap", proj_value, returned, precision=HIGH).reshape(
        orbitals, -1
    )
    result = jnp.zeros_like(flattened).at[:, columns].add(contrib)
    return result.reshape(field.shape)


def hamilton(field, v_local, proj_index, proj_value, kb_energy):
    planes = field.shape[1]
    extended = with_halo(field, (("grid", 1),), 6)
    laplace = 3.0 * LAP_COEF[0] * field
    for offset in range(1, 7):
        upper = extended[:, 6 + offset : 6 + offset + planes]
        lower = extended[:, 6 - offset : 6 - offset + planes]
        laplace = laplace + LAP_COEF[offset] * (upper + lower)
        for axis in (2, 3):
            laplace = laplace + LAP_COEF[offset] * (
                jnp.roll(field, offset, axis) + jnp.roll(field, -offset, axis)
            )
    return (
        -0.5 * laplace
        + v_local[None] * field
        + nonlocal_part(field, proj_index, proj_value, kb_energy)
    )


def on_device(psi_in, v_local, proj_index, proj_value, kb_energy):
    half_width = 6.0
    centre = 8.0
    sigma = half_width / (-3.0 - centre)
    sigma_two = 1.0 / (2.0 / sigma - sigma)
    first = (hamilton(psi_in, v_local, proj_index, proj_value, kb_energy) - centre * psi_in) * (
        sigma / half_width
    )
    filtered = (hamilton(first, v_local, proj_index, proj_value, kb_energy) - centre * first) * (
        2.0 * sigma_two / half_width
    ) - sigma * sigma_two * psi_in
    orbitals = filtered.shape[0]
    flattened = filtered.reshape(orbitals, -1)
    cells_total = lax.axis_size("grid") * flattened.shape[1]
    partial_value = lax.dot_general(
        flattened,
        lax.all_gather(flattened, "orb", axis=0, tiled=True),
        (((1,), (1,)), ((), ())),
        precision=HIGH,
        preferred_element_type=jnp.float32,
    )
    owned_tile = lax.psum_scatter(partial_value, "grid", scatter_dimension=1, tiled=True)
    gram = owned_tile / cells_total
    return (filtered, gram)


def solution(mesh):
    placed = (
        P("orb", "grid", None, None),
        P("grid", None, None),
        P("grid", None, None),
        P("grid", None, None, None),
        P("grid", None),
    )
    return jax.shard_map(
        on_device,
        mesh=mesh,
        in_specs=placed,
        out_specs=(P("orb", "grid", None, None), P("orb", "grid")),
        check_vma=False,
    )
```

profile of v0, /device:TPU:1, one launch (start us, length us, event | category | flops | bytes accessed | tf_op | source)
XLA Modules:
  0.0 687.2 jit_solution(3644620892770224218)
XLA Ops:
  7.2 2.7 collective-permute-start.1
  10.7 3.1 copy.23
  13.8 4.5 gather_fusion
  20.5 8.9 %collective-permute-start.3 = (f32[1,4,4,32]{3,2,1,0:T(4,128)S(1)}, f32[1,4,4,32]{3,2,1,0:T(4,128)S(1)}, u32[]{:S(2)}, u32[]{:S(2)}) collective-permute-start(f32[1,4,4,32]{3,2,1,0:T(4,128)S(1)} %get-tuple-element.86), channel_id=1, source_target_pairs={{4,0},{8,4},{12,8},{16,12},{20,16},{24,20},{28,24},{32,28},{36,32}... | collective-permute-start | bytes 6152 | tf_op jit(solution)/shard_map/ppermute | solution.py:27
  32.0 1.4 fusion.128
  34.7 1.4 fusion.131
  40.1 1.4 fusion.136
  42.9 1.5 fusion.139
  44.4 1.4 fusion.140
  45.8 1.4 fusion.141
  48.6 1.4 fusion.143
  53.7 10.0 %collective-permute-start.5 = (f32[1,4,4,32]{3,2,1,0:T(4,128)S(1)}, f32[1,4,4,32]{3,2,1,0:T(4,128)S(1)}, u32[]{:S(2)}, u32[]{:S(2)}) collective-permute-start(f32[1,4,4,32]{3,2,1,0:T(4,128)S(1)} %fusion.100), channel_id=1, source_target_pairs={{4,0},{8,4},{12,8},{16,12},{20,16},{24,20},{28,24},{32,28},{36,32}... | collective-permute-start | bytes 6152 | tf_op jit(solution)/shard_map/ppermute | solution.py:27
  67.2 10.5 %scatter_custom_fusion = f32[32,6144]{0,1:T(8,128)} fusion(s32[1536]{0:T(1024)S(1)} %fusion.101, f32[1536,32]{1,0:T(8,128)S(1)} %copy.26, f32[]{:T(128)} %constant.11.clone.1), kind=kCustom, calls=%fused_computation.22 | custom fusion | flops 49152 | bytes 786436 | tf_op jit(solution)/shard_map/scatter-add | solution.py:50
  77.8 3.1 copy.27
  83.4 10.6 %broadcast_multiply_fusion = (f32[32,6,8,128]{3,2,1,0:T(8,128)S(1)}, f32[32,6,8,128]{3,2,1,0:T(8,128)}) fusion(f32[32,6,8,128]{3,2,1,0:T(8,128)S(1)} %copy-done.1, f32[32,6,8,128]{3,2,1,0:T(8,128)} %copy.27, f32[6,8,128]{2,1,0:T(8,128)S(1)} %copy-done.10, f32[32,6,8,6]{3,2,1,0:T(8,128)} %get-tuple-element.80, f32[32,6,8,122]{3,2,1,0:T(8,128)} %get-tuple-element.82, ...), kind=kLoop, calls=%fused_computation.142 | loop fusion | flops 15532032 | bytes 27549696 | tf_op jit(solution)/shard_map/mul | solution.py:78
  94.0 2.2 copy.28
  97.4 1.4 fusion.109
  101.4 1.4 fusion.113
  105.5 1.4 fusion.117
  106.9 1.5 fusion.119
  109.8 1.5 fusion.121
  114.0 1.4 fusion.124
  118.7 10.1 %collective-permute-start.6 = (f32[32,6,8,128]{3,2,1,0:T(8,128)S(1)}, f32[32,6,8,128]{3,2,1,0:T(8,128)}, u32[]{:S(2)}, u32[]{:S(2)}) collective-permute-start(f32[32,6,8,128]{3,2,1,0:T(8,128)S(1)} %get-tuple-element.3), channel_id=1, source_target_pairs={{4,0},{8,4},{12,8},{16,12},{20,16},{24,20},{28,24},{32,28},{36,32}... | collective-permute-start | bytes 2359304 | tf_op jit(solution)/shard_map/ppermute | solution.py:27
  128.8 4.5 gather_fusion.1
  134.5 9.9 %collective-permute-start.9 = (f32[1,4,4,32]{3,2,1,0:T(4,128)S(1)}, f32[1,4,4,32]{3,2,1,0:T(4,128)S(1)}, u32[]{:S(2)}, u32[]{:S(2)}) collective-permute-start(f32[1,4,4,32]{3,2,1,0:T(4,128)S(1)} %get-tuple-element.84), channel_id=1, source_target_pairs={{4,0},{8,4},{12,8},{16,12},{20,16},{24,20},{28,24},{32,28},{36,32}... | collective-permute-start | bytes 6152 | tf_op jit(solution)/shard_map/ppermute | solution.py:27
  145.3 15.5 %collective-permute-start.11 = (f32[1,4,4,32]{3,2,1,0:T(4,128)S(1)}, f32[1,4,4,32]{3,2,1,0:T(4,128)S(1)}, u32[]{:S(2)}, u32[]{:S(2)}) collective-permute-start(f32[1,4,4,32]{3,2,1,0:T(4,128)S(1)} %fusion.98), channel_id=1, source_target_pairs={{4,0},{8,4},{12,8},{16,12},{20,16},{24,20},{28,24},{32,28},{36,32}... | collective-permute-start | bytes 6152 | tf_op jit(solution)/shard_map/ppermute | solution.py:27
  164.2 10.5 %scatter_custom_fusion.1 = f32[32,6144]{0,1:T(8,128)} fusion(s32[1536]{0:T(1024)S(1)} %fusion.101, f32[1536,32]{1,0:T(8,128)S(1)} %copy.31, f32[]{:T(128)} %constant.11.clone.1), kind=kCustom, calls=%fused_computation.20 | custom fusion | flops 49152 | bytes 786436 | tf_op jit(solution)/shard_map/scatter-add | solution.py:50
  174.8 3.1 copy.32
  177.9 13.4 %multiply_subtract_fusion = f32[32,6,8,128]{3,2,1,0:T(8,128)S(1)} fusion(f32[32,6,8,128]{3,2,1,0:T(8,128)S(1)} %copy-done.1, f32[32,6,8,128]{3,2,1,0:T(8,128)} %get-tuple-element.4, f32[32,6,8,128]{3,2,1,0:T(8,128)} %copy.32, f32[32,6,8,6]{3,2,1,0:T(8,128)} %get-tuple-element.40, f32[32,6,8,122]{3,2,1,0:T(8,128)} %get-tuple-element.42, ...), kind=kLoop, calls=%fused_computation.139 | loop fusion | flops 17891328 | bytes 20471808 | tf_op jit(solution)/shard_map/sub | solution.py:81
  193.8 82.9 %all-gather.2.cloned.1.call-done = f32[128,6144]{1,0:T(8,128)} async-done(((f32[32,6144]{1,0:T(8,128)}), f32[128,6144]{1,0:T(8,128)}) %all-gather.2.cloned.1.call-update) | async-done | bytes 3145744 | tf_op jit(solution)/shard_map/all_gather | solution.py:89
  276.6 4.5 fusion.104
  281.1 398.7 %all-reduce = f32[32,128]{0,1:T(8,128)S(1)} all-reduce(f32[32,128]{0,1:T(8,128)S(1)} %fusion.104), channel_id=2, replica_groups=mesh['grid'=64,'orb'=4] {'grid'}, use_global_device_ids=true, to_apply=%region_2.4.clone | all-reduce | flops 4096 | bytes 32768
  (101 shorter events, 44.9 us)
Async XLA Ops:
  7.2 11.4 %copy-start = (f32[3,4,4,128]{3,2,1,0:T(4,128)S(1)}, f32[3,4,4,128]{3,2,1,0:T(4,128)}, u32[]{:S(2)}) copy-start(f32[3,4,4,128]{3,2,1,0:T(4,128)} %param.10) | copy-start | bytes 73732
  7.2 22.1 %copy-start.1 = (f32[32,6,8,128]{3,2,1,0:T(8,128)S(1)}, f32[32,6,8,128]{3,2,1,0:T(8,128)}, u32[]{:S(2)}) copy-start(f32[32,6,8,128]{3,2,1,0:T(8,128)} %param.7) | copy-start | bytes 2359300
  7.2 6.6 copy-start.11
  7.2 269.4 %all-gather.2.cloned.1.call-start = ((), (), s32[]{:S(2)}) async-start(), calls=%async_computation | async-start | bytes 3932160 | tf_op jit(solution)/shard_map/all_gather | solution.py:89
  7.2 73.6 %collective-permute-start.1 = (f32[32,6,8,128]{3,2,1,0:T(8,128)}, f32[32,6,8,128]{3,2,1,0:T(8,128)S(1)}, u32[]{:S(2)}, u32[]{:S(2)}) collective-permute-start(f32[32,6,8,128]{3,2,1,0:T(8,128)} %param.7), channel_id=1, source_target_pairs={{0,4},{4,8},{8,12},{12,16},{16,20},{20,24},{24,28},{28,32},{32,36}... | collective-permute-start | bytes 2359304 | tf_op jit(solution)/shard_map/ppermute | solution.py:25
  9.9 71.2 %collective-permute-start = (f32[32,6,8,128]{3,2,1,0:T(8,128)}, f32[32,6,8,128]{3,2,1,0:T(8,128)S(1)}, u32[]{:S(2)}, u32[]{:S(2)}) collective-permute-start(f32[32,6,8,128]{3,2,1,0:T(8,128)} %param.7), channel_id=1, source_target_pairs={{4,0},{8,4},{12,8},{16,12},{20,16},{24,20},{28,24},{32,28},{36,32}... | collective-permute-start | bytes 2359304 | tf_op jit(solution)/shard_map/ppermute | solution.py:27
  19.4 34.2 %collective-permute-start.2 = (f32[1,4,4,32]{3,2,1,0:T(4,128)S(1)}, f32[1,4,4,32]{3,2,1,0:T(4,128)S(1)}, u32[]{:S(2)}, u32[]{:S(2)}) collective-permute-start(f32[1,4,4,32]{3,2,1,0:T(4,128)S(1)} %get-tuple-element.85), channel_id=1, source_target_pairs={{0,4},{4,8},{8,12},{12,16},{16,20},{20,24},{24,28},{28,32},{32,36}... | collective-permute-start | bytes 6152 | tf_op jit(solution)/shard_map/ppermute | solution.py:25
  20.5 33.1 %collective-permute-start.3 = (f32[1,4,4,32]{3,2,1,0:T(4,128)S(1)}, f32[1,4,4,32]{3,2,1,0:T(4,128)S(1)}, u32[]{:S(2)}, u32[]{:S(2)}) collective-permute-start(f32[1,4,4,32]{3,2,1,0:T(4,128)S(1)} %get-tuple-element.86), channel_id=1, source_target_pairs={{4,0},{8,4},{12,8},{16,12},{20,16},{24,20},{28,24},{32,28},{36,32}... | collective-permute-start | bytes 6152 | tf_op jit(solution)/shard_map/ppermute | solution.py:27
  48.6 5.0 copy-start.10
  48.6 5.0 copy-start.12
  53.7 10.5 %collective-permute-start.4 = (f32[1,4,4,32]{3,2,1,0:T(4,128)S(1)}, f32[1,4,4,32]{3,2,1,0:T(4,128)S(1)}, u32[]{:S(2)}, u32[]{:S(2)}) collective-permute-start(f32[1,4,4,32]{3,2,1,0:T(4,128)S(1)} %fusion.100), channel_id=1, source_target_pairs={{0,4},{4,8},{8,12},{12,16},{16,20},{20,24},{24,28},{28,32},{32,36}... | collective-permute-start | bytes 6152 | tf_op jit(solution)/shard_map/ppermute | solution.py:25
  53.7 10.9 %collective-permute-start.5 = (f32[1,4,4,32]{3,2,1,0:T(4,128)S(1)}, f32[1,4,4,32]{3,2,1,0:T(4,128)S(1)}, u32[]{:S(2)}, u32[]{:S(2)}) collective-permute-start(f32[1,4,4,32]{3,2,1,0:T(4,128)S(1)} %fusion.100), channel_id=1, source_target_pairs={{4,0},{8,4},{12,8},{16,12},{20,16},{24,20},{28,24},{32,28},{36,32}... | collective-permute-start | bytes 6152 | tf_op jit(solution)/shard_map/ppermute | solution.py:27
  80.8 1.1 copy-start.3
  80.8 1.4 copy-start.4
  80.8 1.6 copy-start.5
  80.8 1.8 copy-start.6
  80.8 2.1 copy-start.7
  80.8 2.3 copy-start.8
  80.9 2.5 copy-start.9
  118.7 59.2 %collective-permute-start.6 = (f32[32,6,8,128]{3,2,1,0:T(8,128)S(1)}, f32[32,6,8,128]{3,2,1,0:T(8,128)}, u32[]{:S(2)}, u32[]{:S(2)}) collective-permute-start(f32[32,6,8,128]{3,2,1,0:T(8,128)S(1)} %get-tuple-element.3), channel_id=1, source_target_pairs={{4,0},{8,4},{12,8},{16,12},{20,16},{24,20},{28,24},{32,28},{36,32}... | collective-permute-start | bytes 2359304 | tf_op jit(solution)/shard_map/ppermute | solution.py:27
  128.8 49.0 %collective-permute-start.7 = (f32[32,6,8,128]{3,2,1,0:T(8,128)S(1)}, f32[32,6,8,128]{3,2,1,0:T(8,128)}, u32[]{:S(2)}, u32[]{:S(2)}) collective-permute-start(f32[32,6,8,128]{3,2,1,0:T(8,128)S(1)} %get-tuple-element.3), channel_id=1, source_target_pairs={{0,4},{4,8},{8,12},{12,16},{16,20},{20,24},{24,28},{28,32},{32,36}... | collective-permute-start | bytes 2359304 | tf_op jit(solution)/shard_map/ppermute | solution.py:25
  134.4 10.8 %collective-permute-start.8 = (f32[1,4,4,32]{3,2,1,0:T(4,128)S(1)}, f32[1,4,4,32]{3,2,1,0:T(4,128)S(1)}, u32[]{:S(2)}, u32[]{:S(2)}) collective-permute-start(f32[1,4,4,32]{3,2,1,0:T(4,128)S(1)} %get-tuple-element.83), channel_id=1, source_target_pairs={{0,4},{4,8},{8,12},{12,16},{16,20},{20,24},{24,28},{28,32},{32,36}... | collective-permute-start | bytes 6152 | tf_op jit(solution)/shard_map/ppermute | solution.py:25
  134.5 10.7 %collective-permute-start.9 = (f32[1,4,4,32]{3,2,1,0:T(4,128)S(1)}, f32[1,4,4,32]{3,2,1,0:T(4,128)S(1)}, u32[]{:S(2)}, u32[]{:S(2)}) collective-permute-start(f32[1,4,4,32]{3,2,1,0:T(4,128)S(1)} %get-tuple-element.84), channel_id=1, source_target_pairs={{4,0},{8,4},{12,8},{16,12},{20,16},{24,20},{28,24},{32,28},{36,32}... | collective-permute-start | bytes 6152 | tf_op jit(solution)/shard_map/ppermute | solution.py:27
  145.3 16.3 %collective-permute-start.10 = (f32[1,4,4,32]{3,2,1,0:T(4,128)S(1)}, f32[1,4,4,32]{3,2,1,0:T(4,128)S(1)}, u32[]{:S(2)}, u32[]{:S(2)}) collective-permute-start(f32[1,4,4,32]{3,2,1,0:T(4,128)S(1)} %fusion.98), channel_id=1, source_target_pairs={{0,4},{4,8},{8,12},{12,16},{16,20},{20,24},{24,28},{28,32},{32,36}... | collective-permute-start | bytes 6152 | tf_op jit(solution)/shard_map/ppermute | solution.py:25
  145.3 16.3 %collective-permute-start.11 = (f32[1,4,4,32]{3,2,1,0:T(4,128)S(1)}, f32[1,4,4,32]{3,2,1,0:T(4,128)S(1)}, u32[]{:S(2)}, u32[]{:S(2)}) collective-permute-start(f32[1,4,4,32]{3,2,1,0:T(4,128)S(1)} %fusion.98), channel_id=1, source_target_pairs={{4,0},{8,4},{12,8},{16,12},{20,16},{24,20},{28,24},{32,28},{36,32}... | collective-permute-start | bytes 6152 | tf_op jit(solution)/shard_map/ppermute | solution.py:27
  177.9 14.6 %copy-start.13 = (u32[256]{0:T(256)S(1)}, u32[256]{0:T(256)}, u32[]{:S(2)}) copy-start(u32[256]{0:T(256)} %constant.54) | copy-start | bytes 3076
  191.3 89.8 %copy-start.2 = (f32[32,6,8,128]{3,2,1,0:T(8,128)}, f32[32,6,8,128]{3,2,1,0:T(8,128)S(1)}, u32[]{:S(2)}) copy-start(f32[32,6,8,128]{3,2,1,0:T(8,128)S(1)} %multiply_subtract_fusion) | copy-start | bytes 2359300
Sparse Core Ops, SparseCore 0:
  192.6 83.9 all-gather.1
where the time goes:
time: 695 us; the launch traced here: 687 us
  blocking collectives  399 us (57%)
  waiting for transfers between devices  83.8 us (12%)
  local copies, waits for them, and re-layouts  77.1 us (11%)
  starting transfers between devices  59.1 us (9%)
  other arithmetic  46.4 us (7%)
  between operations  15 us (2%)
  matrix products  7.05 us (1%)
    unnamed x1, blocking collectives  399 us
    all_gather x1, waiting for transfers between devices, on_device(): lax.all_gather(flattened, 'orb', axis=0, tiled=True)  82.9 us
    ppermute x6, starting transfers between devices, with_halo(): lax.ppermute(head, axis, [((i + 1) % count, i) for i in range(count)])  55.2 us
    slice x38, local copies, waits for them, and re-layouts, hamilton(): jnp.roll(field, offset, axis) + jnp.roll(field, -offset, axis)  48.3 us
    scatter-add x2, other arithmetic, nonlocal_part(): result = jnp.zeros_like(flattened).at[:, columns].add(contrib)  21.1 us
  transfers between devices with their start and end apart: 13, of which 4 were waited for; matrix products, arithmetic and copies ran while one was open for 11% of the time, Pallas kernels for 0%

commit v1 on v0

v1 whole, which is shorter than its diff:
```python
import functools

import jax
import jax.numpy as jnp
from jax import lax
from jax.experimental import pallas as pl
from jax.experimental.pallas import tpu as pltpu
from jax.sharding import PartitionSpec as P

LAP_COEF = (
    -5369.0 / 1800.0,
    12.0 / 7.0,
    -15.0 / 56.0,
    10.0 / 189.0,
    -1.0 / 112.0,
    2.0 / 1925.0,
    -1.0 / 16632.0,
)
HALF_WIDTH = 6.0
CENTRE = 8.0
SIGMA = HALF_WIDTH / (-3.0 - CENTRE)
SIGMA_TWO = 1.0 / (2.0 / SIGMA - SIGMA)

NX = 128
NY = 8
PLANES = 6
ROWS = PLANES * NY
SLOTS = 4
PROJ = 4
OWNED = SLOTS * PROJ
KAM = 3 * OWNED
PTS = 128

F32 = jnp.float32
BF16 = jnp.bfloat16
VMEM = pl.BlockSpec(memory_space=pltpu.VMEM)
SMEM = pl.BlockSpec(memory_space=pltpu.SMEM)


def two_parts(x):
    head = x.astype(BF16)
    return head, (x - head.astype(F32)).astype(BF16)


def dot_nt(lhs, rhs):
    return lax.dot_general(lhs, rhs, (((1,), (1,)), ((), ())), preferred_element_type=F32)


def dot_nn(lhs, rhs):
    return lax.dot_general(lhs, rhs, (((1,), (0,)), ((), ())), preferred_element_type=F32)


def row_of(field_ref, row, orbitals):
    return field_ref[pl.ds(row, orbitals, stride=ROWS), :]


def project(field_ref, proj_ref, orbitals):
    def step(pair, acc):
        row = 2 * pair
        points = jnp.concatenate([row_of(field_ref, row + i, orbitals) for i in (0, 1)], axis=1)
        head, tail = two_parts(points)
        lhs = jnp.concatenate([head, tail], axis=0)
        rhs = jnp.concatenate([proj_ref[row + i, : 2 * KAM, :] for i in (0, 1)], axis=1)
        return acc + dot_nt(lhs, rhs)

    acc = lax.fori_loop(0, ROWS // 2, step, jnp.zeros((2 * orbitals, 2 * KAM), F32), unroll=4)
    acc = acc[:orbitals] + acc[orbitals:]
    return acc[:, :KAM] + acc[:, KAM:]


def projector_kernel(odd_ref, index_ref, value_ref, psi_ref, proj_ref, part_ref, lhs_ref, *, orbitals):
    even = 1 - odd_ref[0]
    slot = lax.broadcasted_iota(jnp.int32, (OWNED, PTS), 0) // PROJ
    lane_no = lax.broadcasted_iota(jnp.int32, (NX, PTS), 0)
    row_no = lax.broadcasted_iota(jnp.int32, (ROWS, OWNED, PTS), 0)
    for frame in range(3):
        piece = frame + even * (2 - 2 * frame)
        index = index_ref[piece]
        value = value_ref[piece]
        parts = [p.astype(F32) for p in two_parts(value)]
        hits = []
        for a in range(SLOTS):
            mine = index[a : a + 1, :]
            row = jnp.where(slot == a, jnp.broadcast_to(mine >> 7, (OWNED, PTS)), -1)
            here = row_no == row[None]
            for i, part in enumerate(parts):
                chosen = jnp.where(here, part[None], 0.0)
                lhs_ref[i, :, a * PTS : (a + 1) * PTS] = chosen.reshape(ROWS * OWNED, PTS).astype(BF16)
            hits.append(jnp.where(lane_no == jnp.broadcast_to(mine & (NX - 1), (NX, PTS)), 1.0, 0.0).astype(BF16))
        rhs = jnp.concatenate(hits, axis=1)
        dense = dot_nt(lhs_ref[0], rhs) + dot_nt(lhs_ref[1], rhs)
        head, tail = two_parts(dense.reshape(ROWS, OWNED, NX))
        at = frame * OWNED
        proj_ref[:, at : at + OWNED, :] = head
        proj_ref[:, KAM + at : KAM + at + OWNED, :] = tail
        proj_ref[:, 2 * KAM + at : 2 * KAM + at + OWNED, :] = head
    part_ref[...] = project(psi_ref, proj_ref, orbitals)


def hamilton_kernel(odd_ref, field_ref, mate_ref, far_ref, proj_ref, v_ref, coeff_ref, *rest, orbitals, scale, back):
    if back is None:
        out_ref, part_ref, nonlocal_ref, v_scr = rest
    else:
        start_ref, out_ref, rows_ref, nonlocal_ref, v_scr = rest
    odd = odd_ref[0]
    head, tail = two_parts(coeff_ref[...] * scale)
    lhs = jnp.concatenate([head, head, tail], axis=1)

    def spread(pair, carry):
        row = 2 * pair
        rhs = jnp.concatenate([proj_ref[row + i] for i in (0, 1)], axis=1)
        both = dot_nn(lhs, rhs)
        for i in (0, 1):
            nonlocal_ref[pl.ds(row + i, orbitals, stride=ROWS), :] = both[:, i * NX : (i + 1) * NX]
        return carry

    lax.fori_loop(0, ROWS // 2, spread, 0, unroll=4)
    v_scr[...] = (v_ref[...] - (CENTRE + 1.5 * LAP_COEF[0])) * scale

    c = [-0.5 * scale * x for x in LAP_COEF]
    place = [(NY * ((PLANES - 1 - j) + odd * (2 * j - PLANES + 1))) for j in range(PLANES)]

    def orbital(o, carry):
        base = o * ROWS
        spots = [pl.ds(pl.multiple_of(base + p, NY), NY) for p in place]
        cells = [ref[s, :] for ref in (mate_ref, field_ref, far_ref) for s in spots]
        for j in range(PLANES):
            f = cells[PLANES + j]
            total = f * v_scr[pl.ds(pl.multiple_of(place[j], NY), NY), :] + nonlocal_ref[spots[j], :]
            if back is not None:
                total = total + back * start_ref[spots[j], :]
            for k in range(1, 7):
                along = (cells[PLANES + j + k] + cells[PLANES + j - k]) + (
                    pltpu.roll(f, k, 1) + pltpu.roll(f, NX - k, 1)
                )
                total = total + c[k] * along
            for k, weight in ((1, c[1]), (2, c[2] + c[6]), (3, c[3] + c[5])):
                total = total + weight * (pltpu.roll(f, k, 0) + pltpu.roll(f, NY - k, 0))
            total = total + (2.0 * c[4]) * pltpu.roll(f, 4, 0)
            out_ref[spots[j], :] = total
        return carry

    lax.fori_loop(0, orbitals, orbital, 0)
    if back is None:
        part_ref[...] = project(out_ref, proj_ref, orbitals)
    else:
        for row in range(ROWS):
            rows_ref[row] = row_of(out_ref, row, orbitals)


def gram_kernel(rows_ref, out_ref, *, groups, rows, scale):
    acc = None
    for row in range(0, rows, 2):
        x = jnp.concatenate(
            [
                jnp.concatenate([rows_ref[g * rows + row + i] for g in range(groups)], axis=0)
                for i in (0, 1)
            ],
            axis=1,
        )
        head, tail = two_parts(x)
        term = dot_nt(jnp.concatenate([head, tail], axis=0), head)
        acc = term if acc is None else acc + term
    n = acc.shape[1]
    cross = acc[n:]
    out_ref[...] = (acc[:n] + cross + cross.T) * scale


def on_device(psi_in, v_local, proj_index, proj_value, kb_energy):
    orbitals = psi_in.shape[0]
    cells = ROWS * NX
    slabs = lax.axis_size("grid")
    groups = lax.axis_size("orb")
    mates = [(i, i ^ 1) for i in range(slabs)]
    fars = [(i, (i + 1 if i % 2 else i - 1) % slabs) for i in range(slabs)]

    def swap(x, pairs):
        return lax.ppermute(x, "grid", pairs)

    odd = (lax.axis_index("grid") % 2).astype(jnp.int32).reshape(1)
    field_shape = jax.ShapeDtypeStruct((orbitals * ROWS, NX), F32)
    part_shape = jax.ShapeDtypeStruct((orbitals, KAM), F32)
    psi = psi_in.reshape(orbitals * ROWS, NX)
    v = v_local.reshape(ROWS, NX)
    kb = jnp.broadcast_to(kb_energy.reshape(1, OWNED), (orbitals, OWNED))

    def atoms(part):
        mate = swap(part[:, :OWNED], mates)
        own = part[:, OWNED : 2 * OWNED] + mate
        far = swap(jnp.concatenate([part[:, 2 * OWNED :], own, kb], axis=1), fars)
        own = (own + far[:, :OWNED]) * kb
        beyond = (far[:, OWNED : 2 * OWNED] + part[:, 2 * OWNED :]) * far[:, 2 * OWNED :]
        return jnp.concatenate([swap(own, mates), own, beyond], axis=1)

    def hamilton(field, mate, far, proj, coeff, scale, back, *start):
        second = part_shape if back is None else jax.ShapeDtypeStruct((ROWS, orbitals, NX), F32)
        return pl.pallas_call(
            functools.partial(hamilton_kernel, orbitals=orbitals, scale=scale, back=back),
            out_shape=(field_shape, second),
            in_specs=[SMEM] + [VMEM] * (6 + len(start)),
            out_specs=(VMEM, VMEM),
            scratch_shapes=[pltpu.VMEM((orbitals * ROWS, NX), F32), pltpu.VMEM((ROWS, NX), F32)],
            cost_estimate=pl.CostEstimate(flops=10**8, bytes_accessed=6 * 10**6, transcendentals=0),
            name="hamilton",
        )(odd, field, mate, far, proj, v, coeff, *start)

    psi_far = swap(psi, fars)
    psi_mate = swap(psi, mates)
    proj, part = pl.pallas_call(
        functools.partial(projector_kernel, orbitals=orbitals),
        out_shape=(jax.ShapeDtypeStruct((ROWS, 3 * KAM, NX), BF16), part_shape),
        in_specs=[SMEM] + [VMEM] * 3,
        out_specs=(VMEM, VMEM),
        scratch_shapes=[pltpu.VMEM((2, ROWS * OWNED, SLOTS * PTS), BF16)],
        cost_estimate=pl.CostEstimate(flops=10**8, bytes_accessed=3 * 10**6, transcendentals=0),
        name="projectors",
    )(odd, proj_index, proj_value.reshape(3, OWNED, PTS), psi)
    coeff = atoms(part)
    first, part = hamilton(psi, psi_mate, psi_far, proj, coeff, SIGMA / HALF_WIDTH, None)
    first_far = swap(first, fars)
    first_mate = swap(first, mates)
    coeff = atoms(part)
    filtered, rows = hamilton(
        first, first_mate, first_far, proj, coeff, 2.0 * SIGMA_TWO / HALF_WIDTH, -SIGMA * SIGMA_TWO, psi
    )
    rows = lax.all_to_all(rows, "orb", 0, 0, tiled=True)
    n = orbitals * groups
    partial_gram = pl.pallas_call(
        functools.partial(gram_kernel, groups=groups, rows=ROWS // groups, scale=1.0 / (cells * slabs)),
        out_shape=jax.ShapeDtypeStruct((n, n), F32),
        in_specs=[VMEM],
        out_specs=VMEM,
        cost_estimate=pl.CostEstimate(flops=10**8, bytes_accessed=10**6, transcendentals=0),
        name="gram",
    )(rows)
    width = n // slabs
    tiles = partial_gram.reshape(slabs, width, groups, orbitals).transpose(0, 2, 1, 3)
    tiles = lax.all_to_all(
        tiles.reshape(slabs * groups, width * orbitals), ("grid", "orb"), 0, 0, tiled=True
    )
    gram = jnp.sum(tiles, axis=0).reshape(width, orbitals).T
    return filtered.reshape(psi_in.shape), gram


def solution(mesh):
    placed = (
        P("orb", "grid", None, None),
        P("grid", None, None),
        P("grid", None, None),
        P("grid", None, None, None),
        P("grid", None),
    )
    return jax.shard_map(
        on_device,
        mesh=mesh,
        in_specs=placed,
        out_specs=(P("orb", "grid", None, None), P("orb", "grid")),
        check_vma=False,
    )
```

time: 695 us -> 142 us (0.20)
  blocking collectives: 399 us -> 43.9 us
  waiting for transfers between devices: 83.8 us -> 10.1 us
  local copies, waits for them, and re-layouts: 77.1 us -> 7.36 us
  other arithmetic: 46.4 us -> 4.97 us
  Pallas kernels: 0 us -> 26.9 us
  between operations: 15 us -> 0.7 us
  starting transfers between devices: 59.1 us -> 46.7 us
  matrix products: 7.05 us -> 0 us
    unnamed x1 -> x0, blocking collectives: 399 us -> none
    all_gather x1 -> x0, waiting for transfers between devices: 82.9 us -> none  [on_device(): lax.all_gather(flattened, 'orb', axis=0, tiled=True)]
    slice x40 -> x2, local copies, waits for them, and re-layouts: 48.3 us -> 1.73 us  [atoms(): far = swap(jnp.concatenate([part[:, 2 * OWNED:], own, kb], axis=1), fars)]
    all_to_all x0 -> x2, blocking collectives: none -> 43.9 us  [the longest x1 24.2 us: on_device(): rows = lax.all_to_all(rows, 'orb', 0, 0, tiled=True)]
    pallas_call x0 -> x4, Pallas kernels: none -> 26.9 us  [the longest x2 19.5 us: hamilton(): pl.pallas_call(functools.partial(hamilton_kernel, orbitals=orbitals, scal...]
    scatter-add x2 -> x0, other arithmetic: 21.1 us -> none  [nonlocal_part(): result = jnp.zeros_like(flattened).at[:, columns].add(contrib)]
    sub x1 -> x0, other arithmetic: 13.4 us -> none  [on_device(): (hamilton(first, v_local, proj_index, proj_value, kb_energy) - centre * f...]
    ppermute x12 -> x10, starting transfers between devices: 59.1 us -> 46.7 us  [swap(): return lax.ppermute(x, 'grid', pairs)]
  transfers between devices with their start and end apart: 13 -> 10, of which waited for: 4 -> 6; matrix products, arithmetic and copies ran while one was open for 11% -> 5% of each run, Pallas kernels for 0% -> 4%
where the time goes in v1:
time: 142 us; the launch traced here: 141 us
  starting transfers between devices  46.7 us (33%)
  blocking collectives  43.9 us (31%)
  Pallas kernels  26.9 us (19%)
  waiting for transfers between devices  10.1 us (7%)
  local copies, waits for them, and re-layouts  7.36 us (5%)
  other arithmetic  4.97 us (4%)
    ppermute x10, starting transfers between devices, swap(): return lax.ppermute(x, 'grid', pairs)  46.7 us
    all_to_all x1, blocking collectives, on_device(): rows = lax.all_to_all(rows, 'orb', 0, 0, tiled=True)  24.2 us
    all_to_all x1, blocking collectives, on_device(): lax.all_to_all(tiles.reshape(slabs * groups, width * orbitals), ('grid',...  19.8 us
    pallas_call x2, Pallas kernels, hamilton(): pl.pallas_call(functools.partial(hamilton_kernel, orbitals=orbitals, scal...  19.5 us
    ppermute x10, waiting for transfers between devices, swap(): return lax.ppermute(x, 'grid', pairs)  10.1 us
    pallas_call x1, Pallas kernels, on_device(): pl.pallas_call(functools.partial(projector_kernel, orbitals=orbitals), ou...  5.22 us
    unnamed x8, local copies, waits for them, and re-layouts  2.9 us
  transfers between devices with their start and end apart: 10, of which 6 were waited for; matrix products, arithmetic and copies ran while one was open for 5% of the time, Pallas kernels for 4%

profile of v1, /device:TPU:1, one launch (start us, length us, event | category | flops | bytes accessed | tf_op | source)
XLA Modules:
  0.0 140.8 jit_solution(3915480297570004655)
XLA Ops:
  0.6 2.7 %collective-permute-start.1 = (f32[1536,128]{1,0:T(8,128)}, f32[1536,128]{1,0:T(8,128)S(1)}, u32[]{:S(2)}, u32[]{:S(2)}) collective-permute-start(f32[1536,128]{1,0:T(8,128)} %bitcast.8), channel_id=1, source_target_pairs={{0,252},{4,8},{8,4},{12,16},{16,12},{20,24},{24,20},{28,32},{32,28... | collective-permute-start | bytes 2359304 | tf_op jit(solution)/shard_map/ppermute | solution.py:178
  3.3 10.2 %collective-permute-start = (f32[1536,128]{1,0:T(8,128)}, f32[1536,128]{1,0:T(8,128)S(1)}, u32[]{:S(2)}, u32[]{:S(2)}) collective-permute-start(f32[1536,128]{1,0:T(8,128)} %bitcast.9), channel_id=1, source_target_pairs={{0,4},{4,0},{8,12},{12,8},{16,20},{20,16},{24,28},{28,24},{32,36},... | collective-permute-start | bytes 2359304 | tf_op jit(solution)/shard_map/ppermute | solution.py:178
  13.5 5.2 %projectors.1 = (bf16[48,144,128]{2,1,0:T(8,128)(2,1)}, f32[32,48]{1,0:T(8,128)}) custom-call(s32[1]{0:T(128)} %bitcast.odd_ref, s32[3,4,128]{2,1,0:T(4,128)} %index_ref.1, f32[3,16,128]{2,1,0:T(8,128)} %bitcast.17, f32[1536,128]{1,0:T(8,128)} %bitcast.10), custom_call_target="tpu_custom_call" | custom-call | flops 100000000 | bytes 3000000 | tf_op jit(solution)/shard_map/projectors/pallas_call | solution.py:209
  18.7 0.9 fusion.3
  19.6 0.8 broadcast_in_dim.7
  20.4 0.4 collective-permute-done.2
  20.8 0.8 slice_add_fusion.5
  21.7 3.4 %collective-permute-done.3 = f32[32,48]{1,0:T(8,128)S(1)} collective-permute-done((f32[32,48]{1,0:T(8,128)S(1)}, f32[32,48]{1,0:T(8,128)S(1)}, u32[]{:S(2)}, u32[]{:S(2)}) %collective-permute-start.3) | collective-permute-done | bytes 6176 | tf_op jit(solution)/shard_map/ppermute | solution.py:178
  25.1 0.8 fusion.1
  25.9 11.3 %collective-permute-start.4 = (f32[32,16]{1,0:T(8,128)S(1)}, f32[32,16]{1,0:T(8,128)S(1)}, u32[]{:S(2)}, u32[]{:S(2)}) collective-permute-start(f32[32,16]{1,0:T(8,128)S(1)} %get-tuple-element.18), channel_id=1, source_target_pairs={{0,4},{4,0},{8,12},{12,8},{16,20},{20,16},{24,28},{28,24},{32,36},... | collective-permute-start | bytes 6152 | tf_op jit(solution)/shard_map/ppermute | solution.py:178
  37.3 0.8 collective-permute-done.4
  38.1 0.7 pad_maximum_fusion.2.coeff_ref
  38.8 0.9 copy-done
  39.9 10.0 %hamilton.2 = (f32[1536,128]{1,0:T(8,128)}, f32[32,48]{1,0:T(8,128)}) custom-call(s32[1]{0:T(128)} %bitcast.odd_ref, f32[1536,128]{1,0:T(8,128)} %bitcast.11, f32[1536,128]{1,0:T(8,128)} %copy-done.1, f32[1536,128]{1,0:T(8,128)} %copy-done, bf16[48,144,128]{2,1,0:T(8,128)(2,1)} %get-tuple-element.8.proj_ref, f32[48,128]{1,0:T(8,128)} %bitcast.15, ...), custom_call_target="tpu_custom_call" | custom-call | flops 100000000 | bytes 6000000 | tf_op jit(solution)/shard_map/hamilton/pallas_call | solution.py:197
  49.9 5.9 %collective-permute-start.5 = (f32[1536,128]{1,0:T(8,128)}, f32[1536,128]{1,0:T(8,128)S(1)}, u32[]{:S(2)}, u32[]{:S(2)}) collective-permute-start(f32[1536,128]{1,0:T(8,128)} %get-tuple-element.10.field_ref), channel_id=1, source_target_pairs={{0,4},{4,0},{8,12},{12,8},{16,20},{20,16},{24,28},{28,24},{32,36},... | collective-permute-start | bytes 2359304 | tf_op jit(solution)/shard_map/ppermute | solution.py:178
  55.9 0.9 fusion.2
  56.7 1.2 collective-permute-done.7
  57.9 0.8 slice_add_fusion.4
  58.8 3.4 %collective-permute-done.8 = f32[32,48]{1,0:T(8,128)S(1)} collective-permute-done((f32[32,48]{1,0:T(8,128)S(1)}, f32[32,48]{1,0:T(8,128)S(1)}, u32[]{:S(2)}, u32[]{:S(2)}) %collective-permute-start.8) | collective-permute-done | bytes 6176 | tf_op jit(solution)/shard_map/ppermute | solution.py:178
  62.3 0.8 fusion
  63.1 16.5 %collective-permute-start.9 = (f32[32,16]{1,0:T(8,128)S(1)}, f32[32,16]{1,0:T(8,128)S(1)}, u32[]{:S(2)}, u32[]{:S(2)}) collective-permute-start(f32[32,16]{1,0:T(8,128)S(1)} %get-tuple-element.14), channel_id=1, source_target_pairs={{0,4},{4,0},{8,12},{12,8},{16,20},{20,16},{24,28},{28,24},{32,36},... | collective-permute-start | bytes 6152 | tf_op jit(solution)/shard_map/ppermute | solution.py:178
  79.6 0.8 collective-permute-done.9
  80.4 0.7 pad_maximum_fusion.3.coeff_ref
  81.1 0.9 copy-done.2
  82.0 0.9 copy-done.3
  82.9 9.5 %hamilton.3 = (f32[1536,128]{1,0:T(8,128)}, f32[48,32,128]{2,1,0:T(8,128)}) custom-call(s32[1]{0:T(128)} %bitcast.odd_ref, f32[1536,128]{1,0:T(8,128)} %get-tuple-element.10.field_ref, f32[1536,128]{1,0:T(8,128)} %copy-done.3, f32[1536,128]{1,0:T(8,128)} %copy-done.2, bf16[48,144,128]{2,1,0:T(8,128)(2,1)} %get-tuple-element.8.proj_ref, f32[48,128]{1,0:T(8,128)} %bitcast.16, ...), custom_call_target="tpu_custom_call" | custom-call | flops 100000000 | bytes 6000000 | tf_op jit(solution)/shard_map/hamilton/pallas_call | solution.py:197
  92.4 24.2 %all_to_all.14.rows_ref = f32[48,32,128]{2,1,0:T(8,128)} all-to-all(f32[48,32,128]{2,1,0:T(8,128)} %get-tuple-element.13), channel_id=1, replica_groups=mesh['grid'=64,'orb'=4] {'orb'}, dimensions={0} | all-to-all | bytes 1572864 | tf_op jit(solution)/shard_map/all_to_all | solution.py:226
  116.5 2.2 %gram.1 = f32[128,128]{1,0:T(8,128)} custom-call(f32[48,32,128]{2,1,0:T(8,128)} %all_to_all.14.rows_ref), custom_call_target="tpu_custom_call" | custom-call | flops 100000000 | bytes 1000000 | tf_op jit(solution)/shard_map/gram/pallas_call | solution.py:228
  118.7 1.0 reshape.36
  120.1 19.8 %all_to_all.15 = f32[256,1,64]{2,1,0:T(1,128)S(1)} all-to-all(f32[256,1,64]{2,1,0:T(1,128)S(1)} %bitcast.14), channel_id=1, replica_groups=mesh['grid'=64,'orb'=4] {'grid','orb'}, dimensions={0} | all-to-all | bytes 131072 | tf_op jit(solution)/shard_map/all_to_all | solution.py:238
  139.8 0.3 reduce_sum.9
  140.1 0.6 reshape.37
  (19 shorter events, 0.9 us)
Async XLA Ops:
  0.6 38.2 %collective-permute-start.1 = (f32[1536,128]{1,0:T(8,128)}, f32[1536,128]{1,0:T(8,128)S(1)}, u32[]{:S(2)}, u32[]{:S(2)}) collective-permute-start(f32[1536,128]{1,0:T(8,128)} %bitcast.8), channel_id=1, source_target_pairs={{0,252},{4,8},{8,4},{12,16},{16,12},{20,24},{24,20},{28,32},{32,28... | collective-permute-start | bytes 2359304 | tf_op jit(solution)/shard_map/ppermute | solution.py:178
  3.3 35.5 %collective-permute-start = (f32[1536,128]{1,0:T(8,128)}, f32[1536,128]{1,0:T(8,128)S(1)}, u32[]{:S(2)}, u32[]{:S(2)}) collective-permute-start(f32[1536,128]{1,0:T(8,128)} %bitcast.9), channel_id=1, source_target_pairs={{0,4},{4,0},{8,12},{12,8},{16,20},{20,16},{24,28},{28,24},{32,36},... | collective-permute-start | bytes 2359304 | tf_op jit(solution)/shard_map/ppermute | solution.py:178
  19.6 1.2 collective-permute-start.2
  21.6 3.5 %collective-permute-start.3 = (f32[32,48]{1,0:T(8,128)S(1)}, f32[32,48]{1,0:T(8,128)S(1)}, u32[]{:S(2)}, u32[]{:S(2)}) collective-permute-start(f32[32,48]{1,0:T(8,128)S(1)} %pad_maximum_fusion.1), channel_id=1, source_target_pairs={{0,252},{4,8},{8,4},{12,16},{16,12},{20,24},{24,20},{28,32},{32,28... | collective-permute-start | bytes 18440 | tf_op jit(solution)/shard_map/ppermute | solution.py:178
  25.9 12.2 %collective-permute-start.4 = (f32[32,16]{1,0:T(8,128)S(1)}, f32[32,16]{1,0:T(8,128)S(1)}, u32[]{:S(2)}, u32[]{:S(2)}) collective-permute-start(f32[32,16]{1,0:T(8,128)S(1)} %get-tuple-element.18), channel_id=1, source_target_pairs={{0,4},{4,0},{8,12},{12,8},{16,20},{20,16},{24,28},{28,24},{32,36},... | collective-permute-start | bytes 6152 | tf_op jit(solution)/shard_map/ppermute | solution.py:178
  38.8 0.9 copy-start
  38.8 1.1 copy-start.1
  49.9 31.1 %collective-permute-start.6 = (f32[1536,128]{1,0:T(8,128)}, f32[1536,128]{1,0:T(8,128)S(1)}, u32[]{:S(2)}, u32[]{:S(2)}) collective-permute-start(f32[1536,128]{1,0:T(8,128)} %get-tuple-element.10.field_ref), channel_id=1, source_target_pairs={{0,252},{4,8},{8,4},{12,16},{16,12},{20,24},{24,20},{28,32},{32,28... | collective-permute-start | bytes 2359304 | tf_op jit(solution)/shard_map/ppermute | solution.py:178
  49.9 31.1 %collective-permute-start.5 = (f32[1536,128]{1,0:T(8,128)}, f32[1536,128]{1,0:T(8,128)S(1)}, u32[]{:S(2)}, u32[]{:S(2)}) collective-permute-start(f32[1536,128]{1,0:T(8,128)} %get-tuple-element.10.field_ref), channel_id=1, source_target_pairs={{0,4},{4,0},{8,12},{12,8},{16,20},{20,16},{24,28},{28,24},{32,36},... | collective-permute-start | bytes 2359304 | tf_op jit(solution)/shard_map/ppermute | solution.py:178
  56.7 1.2 collective-permute-start.7
  58.8 3.5 %collective-permute-start.8 = (f32[32,48]{1,0:T(8,128)S(1)}, f32[32,48]{1,0:T(8,128)S(1)}, u32[]{:S(2)}, u32[]{:S(2)}) collective-permute-start(f32[32,48]{1,0:T(8,128)S(1)} %pad_maximum_fusion), channel_id=1, source_target_pairs={{0,252},{4,8},{8,4},{12,16},{16,12},{20,24},{24,20},{28,32},{32,28... | collective-permute-start | bytes 18440 | tf_op jit(solution)/shard_map/ppermute | solution.py:178
  63.1 17.3 %collective-permute-start.9 = (f32[32,16]{1,0:T(8,128)S(1)}, f32[32,16]{1,0:T(8,128)S(1)}, u32[]{:S(2)}, u32[]{:S(2)}) collective-permute-start(f32[32,16]{1,0:T(8,128)S(1)} %get-tuple-element.14), channel_id=1, source_target_pairs={{0,4},{4,0},{8,12},{12,8},{16,20},{20,16},{24,28},{28,24},{32,36},... | collective-permute-start | bytes 6152 | tf_op jit(solution)/shard_map/ppermute | solution.py:178
  81.1 0.9 copy-start.2
  82.0 0.9 copy-start.3

commit v2 on v1

v2 whole, which is shorter than its diff:
```python
import functools

import jax
import jax.numpy as jnp
from jax import lax
from jax.experimental import pallas as pl
from jax.experimental.pallas import tpu as pltpu
from jax.sharding import PartitionSpec as P

LAP_COEF = (
    -5369.0 / 1800.0,
    12.0 / 7.0,
    -15.0 / 56.0,
    10.0 / 189.0,
    -1.0 / 112.0,
    2.0 / 1925.0,
    -1.0 / 16632.0,
)
HALF_WIDTH = 6.0
CENTRE = 8.0
SIGMA = HALF_WIDTH / (-3.0 - CENTRE)
SIGMA_TWO = 1.0 / (2.0 / SIGMA - SIGMA)

NX = 128
NY = 8
PLANES = 6
ROWS = PLANES * NY
SLOTS = 4
PROJ = 4
OWNED = SLOTS * PROJ
KAM = 3 * OWNED
PTS = 128

F32 = jnp.float32
BF16 = jnp.bfloat16
VMEM = pl.BlockSpec(memory_space=pltpu.VMEM)
SMEM = pl.BlockSpec(memory_space=pltpu.SMEM)


def two_parts(x):
    head = x.astype(BF16)
    return head, (x - head.astype(F32)).astype(BF16)


def dot_nt(lhs, rhs):
    return lax.dot_general(lhs, rhs, (((1,), (1,)), ((), ())), preferred_element_type=F32)


def dot_nn(lhs, rhs):
    return lax.dot_general(lhs, rhs, (((1,), (0,)), ((), ())), preferred_element_type=F32)


def row_of(field_ref, row, orbitals):
    return field_ref[pl.ds(row, orbitals, stride=ROWS), :]


def lanes(shape):
    return lax.broadcasted_iota(jnp.int32, shape, 1)


def project(field_ref, proj_ref, orbitals):
    def step(pair, acc):
        row = 2 * pair
        points = jnp.concatenate([row_of(field_ref, row + i, orbitals) for i in (0, 1)], axis=1)
        head, tail = two_parts(points)
        lhs = jnp.concatenate([head, tail], axis=0)
        rhs = jnp.concatenate([proj_ref[row + i, :NX, :] for i in (0, 1)], axis=1)
        return acc + dot_nt(lhs, rhs)

    acc = lax.fori_loop(0, ROWS // 2, step, jnp.zeros((2 * orbitals, NX), F32), unroll=4)
    acc = acc[:orbitals] + acc[orbitals:]
    return jnp.where(lanes(acc.shape) < KAM, acc + pltpu.roll(acc, NX - KAM, 1), 0.0)


def put_messages(part, kb_ref, own_ref, mate_ref):
    lane = lanes(part.shape)
    kb = jnp.broadcast_to(kb_ref[...], part.shape)
    own_ref[...] = jnp.where(lane < KAM, part, jnp.where(lane < KAM + OWNED, kb, 0.0))
    mate = jnp.where(lane < 4 * OWNED, pltpu.roll(part, 3 * OWNED, 1), kb)
    mate = jnp.where(lane < 2 * OWNED, pltpu.roll(part, OWNED, 1), mate)
    mate = jnp.where(lane < 5 * OWNED, jnp.where(lane < 4 * OWNED, mate, pltpu.roll(part, 3 * OWNED, 1)), kb)
    sent = ((lane >= OWNED) & (lane < 2 * OWNED)) | ((lane >= 4 * OWNED) & (lane < 6 * OWNED))
    mate_ref[...] = jnp.where(sent, mate, 0.0)


def projector_kernel(odd_ref, index_ref, value_ref, kb_ref, psi_ref, proj_ref, own_ref, mate_ref, lhs_ref, *, orbitals):
    even = 1 - odd_ref[0]
    slot = lax.broadcasted_iota(jnp.int32, (OWNED, PTS), 0) // PROJ
    lane_no = lax.broadcasted_iota(jnp.int32, (NX, PTS), 0)
    row_no = lax.broadcasted_iota(jnp.int32, (ROWS, OWNED, PTS), 0)
    for frame in range(3):
        piece = frame + even * (2 - 2 * frame)
        index = index_ref[piece]
        value = value_ref[piece]
        parts = [p.astype(F32) for p in two_parts(value)]
        hits = []
        for a in range(SLOTS):
            mine = index[a : a + 1, :]
            row = jnp.where(slot == a, jnp.broadcast_to(mine >> 7, (OWNED, PTS)), -1)
            here = row_no == row[None]
            for i, part in enumerate(parts):
                chosen = jnp.where(here, part[None], 0.0)
                lhs_ref[i, :, a * PTS : (a + 1) * PTS] = chosen.reshape(ROWS * OWNED, PTS).astype(BF16)
            hits.append(jnp.where(lane_no == jnp.broadcast_to(mine & (NX - 1), (NX, PTS)), 1.0, 0.0).astype(BF16))
        rhs = jnp.concatenate(hits, axis=1)
        dense = dot_nt(lhs_ref[0], rhs) + dot_nt(lhs_ref[1], rhs)
        head, tail = two_parts(dense.reshape(ROWS, OWNED, NX))
        at = frame * OWNED
        proj_ref[:, at : at + OWNED, :] = head
        proj_ref[:, KAM + at : KAM + at + OWNED, :] = tail
        proj_ref[:, 2 * KAM + at : 2 * KAM + at + OWNED, :] = head
    put_messages(project(psi_ref, proj_ref, orbitals), kb_ref, own_ref, mate_ref)


def weights(scale):
    return [-0.5 * scale * x for x in LAP_COEF]


def places(odd_ref):
    odd = odd_ref[0]
    return [NY * ((PLANES - 1 - j) + odd * (2 * j - PLANES + 1)) for j in range(PLANES)]


def slab_kernel(field_ref, v_ref, *rest, orbitals, scale, back):
    start_ref = rest[0] if back is not None else None
    out_ref, v_scr = rest[-2:]
    v_scr[...] = (v_ref[...] - (CENTRE + 1.5 * LAP_COEF[0])) * scale
    c = weights(scale)

    def orbital(o, carry):
        base = o * ROWS
        spots = [pl.ds(pl.multiple_of(base + NY * j, NY), NY) for j in range(PLANES)]
        cells = [field_ref[s, :] for s in spots]
        for j in range(PLANES):
            f = cells[j]
            total = f * v_scr[NY * j : NY * j + NY, :]
            if back is not None:
                total = total + back * start_ref[spots[j], :]
            for k in range(1, 7):
                along = pltpu.roll(f, k, 1) + pltpu.roll(f, NX - k, 1)
                for other in (j - k, j + k):
                    if 0 <= other < PLANES:
                        along = along + cells[other]
                total = total + c[k] * along
            for k, weight in ((1, c[1]), (2, c[2] + c[6]), (3, c[3] + c[5])):
                total = total + weight * (pltpu.roll(f, k, 0) + pltpu.roll(f, NY - k, 0))
            total = total + (2.0 * c[4]) * pltpu.roll(f, 4, 0)
            out_ref[spots[j], :] = total
        return carry

    lax.fori_loop(0, orbitals, orbital, 0)


def finish_kernel(place_ref, slab_ref, mate_ref, far_ref, proj_ref, own_msg, far_msg, beyond_msg, *rest, orbitals, scale, last):
    if last:
        out_ref, *chunk_refs, nonlocal_ref = rest
    else:
        kb_ref, out_ref, own_out, mate_out, nonlocal_ref = rest
    own, far, beyond = own_msg[...], far_msg[...], beyond_msg[...]
    lane = lanes(own.shape)

    def shift(x, by):
        return pltpu.roll(x, NX - by, 1)

    first, second = lane < OWNED, lane < 2 * OWNED
    sums = own + jnp.where(
        first,
        shift(own, 4 * OWNED) + shift(beyond, 2 * OWNED),
        jnp.where(second, shift(far, OWNED), pltpu.roll(far, OWNED, 1)),
    )
    energy = jnp.where(
        first, shift(own, 5 * OWNED), jnp.where(second, shift(own, 2 * OWNED), shift(far, OWNED))
    )
    coeff = (sums * energy * scale)[:, :KAM]
    head, tail = two_parts(coeff)
    lhs = jnp.concatenate([head, head, tail], axis=1)

    def spread(pair, carry):
        row = 2 * pair
        rhs = jnp.concatenate([proj_ref[row + i] for i in (0, 1)], axis=1)
        both = dot_nn(lhs, rhs)
        for i in (0, 1):
            nonlocal_ref[pl.ds(row + i, orbitals, stride=ROWS), :] = both[:, i * NX : (i + 1) * NX]
        return carry

    lax.fori_loop(0, ROWS // 2, spread, 0, unroll=4)
    c = weights(scale)
    place = places(place_ref)

    def orbital(o, carry):
        base = o * ROWS
        spots = [pl.ds(pl.multiple_of(base + p, NY), NY) for p in place]
        mate = [mate_ref[s, :] for s in spots]
        beyond = [far_ref[s, :] for s in spots]
        for j in range(PLANES):
            total = slab_ref[spots[j], :] + nonlocal_ref[spots[j], :]
            for k in range(1, 7):
                terms = []
                if j - k < 0:
                    terms.append(mate[PLANES + j - k])
                if j + k >= PLANES:
                    terms.append(beyond[j + k - PLANES])
                if terms:
                    total = total + c[k] * sum(terms[1:], terms[0])
            out_ref[spots[j], :] = total
        return carry

    lax.fori_loop(0, orbitals, orbital, 0, unroll=2)
    if last:
        share = ROWS // len(chunk_refs)
        for m, chunk_ref in enumerate(chunk_refs):
            at = (place_ref[1] ^ m) * share
            for i in range(share):
                chunk_ref[i] = row_of(out_ref, at + i, orbitals)
    else:
        put_messages(project(out_ref, proj_ref, orbitals), kb_ref, own_out, mate_out)


def gram_kernel(place_ref, *refs, orbitals, width, scale):
    *block_refs, out_ref, head_ref, tail_ref, gram_ref = refs
    for m, block_ref in enumerate(block_refs):
        at = pl.ds(pl.multiple_of((place_ref[1] ^ m) * orbitals, orbitals), orbitals)
        for i in range(block_ref.shape[0]):
            head, tail = two_parts(block_ref[i])
            head_ref[at, i * NX : (i + 1) * NX] = head
            tail_ref[at, i * NX : (i + 1) * NX] = tail
    head = head_ref[...]
    cross = dot_nt(tail_ref[...], head)
    gram_ref[...] = (dot_nt(head, head) + cross + cross.T) * scale
    n = gram_ref.shape[0]
    groups = len(block_refs)
    parts = [gram_ref[pl.ds(t, n // width, stride=width), :] for t in range(width)]
    lane = lanes(parts[0].shape)
    for q in range(groups):
        row = parts[0] if q == 0 else pltpu.roll(parts[0], n - orbitals * q, 1)
        for t in range(1, width):
            by = (orbitals * (t - q)) % n
            row = jnp.where(lane < orbitals * t, row, pltpu.roll(parts[t], by, 1) if by else parts[t])
        out_ref[pl.ds(q, n // width, stride=groups), :] = row


def params(mib):
    return pltpu.CompilerParams(vmem_limit_bytes=mib * 2**20)


def on_device(psi_in, v_local, proj_index, proj_value, kb_energy):
    orbitals = psi_in.shape[0]
    slabs = lax.axis_size("grid")
    groups = lax.axis_size("orb")
    mates = [(i, i ^ 1) for i in range(slabs)]
    fars = [(i, (i + 1 if i % 2 else i - 1) % slabs) for i in range(slabs)]
    n = orbitals * groups
    width = n // slabs

    def swap(x, pairs):
        return lax.ppermute(x, "grid", pairs)

    place = jnp.stack([lax.axis_index("grid") % 2, lax.axis_index("orb")]).astype(jnp.int32)
    field_shape = jax.ShapeDtypeStruct((orbitals * ROWS, NX), F32)
    message_shape = jax.ShapeDtypeStruct((orbitals, NX), F32)
    psi = psi_in.reshape(orbitals * ROWS, NX)
    v = v_local.reshape(ROWS, NX)
    kb = kb_energy.reshape(1, OWNED)
    kb = jnp.pad(kb, ((0, 0), (KAM, 0))) + jnp.zeros((1, KAM + OWNED), F32)
    kb = jnp.pad(jnp.concatenate([kb, kb[:, 2 * OWNED :]], axis=1), ((0, 0), (0, NX - 6 * OWNED)))

    def slab(field, scale, back, *start):
        return pl.pallas_call(
            functools.partial(slab_kernel, orbitals=orbitals, scale=scale, back=back),
            out_shape=field_shape,
            in_specs=[VMEM] * (2 + len(start)),
            out_specs=VMEM,
            scratch_shapes=[pltpu.VMEM((ROWS, NX), F32)],
            compiler_params=params(8),
            cost_estimate=pl.CostEstimate(flops=10**8, bytes_accessed=10**7, transcendentals=0),
            name="slab",
        )(field, v, *start)

    def finish(operands, outs, scale, last):
        return pl.pallas_call(
            functools.partial(finish_kernel, orbitals=orbitals, scale=scale, last=last),
            out_shape=(field_shape, *outs),
            in_specs=[SMEM] + [VMEM] * len(operands),
            out_specs=(VMEM,) * (1 + len(outs)),
            scratch_shapes=[pltpu.VMEM((orbitals * ROWS, NX), F32)],
            compiler_params=params(16),
            cost_estimate=pl.CostEstimate(flops=10**8, bytes_accessed=10**7, transcendentals=0),
            name="finish",
        )(place, *operands)

    def stage(field, proj, own, to_mate, scale, back, *start):
        far = swap(field, fars)
        mate = swap(field, mates)
        own = own + swap(to_mate, mates)
        from_far = swap(own, fars)
        field, own = lax.optimization_barrier((field, own))
        local = slab(field, scale, back, *start)
        return local, mate, far, proj, own, from_far, swap(from_far, mates)

    proj, own, to_mate = pl.pallas_call(
        functools.partial(projector_kernel, orbitals=orbitals),
        out_shape=(jax.ShapeDtypeStruct((ROWS, 3 * KAM, NX), BF16), message_shape, message_shape),
        in_specs=[SMEM] + [VMEM] * 4,
        out_specs=(VMEM,) * 3,
        scratch_shapes=[pltpu.VMEM((2, ROWS * OWNED, SLOTS * PTS), BF16)],
        compiler_params=params(16),
        cost_estimate=pl.CostEstimate(flops=10**8, bytes_accessed=10**7, transcendentals=0),
        name="projectors",
    )(place, proj_index, proj_value.reshape(3, OWNED, PTS), kb, psi)
    scale = SIGMA / HALF_WIDTH
    operands = stage(psi, proj, own, to_mate, scale, None)
    first, own, to_mate = finish((*operands, kb), (message_shape,) * 2, scale, False)
    scale = 2.0 * SIGMA_TWO / HALF_WIDTH
    operands = stage(first, proj, own, to_mate, scale, -SIGMA * SIGMA_TWO, psi)
    chunk = jax.ShapeDtypeStruct((ROWS // groups, orbitals, NX), F32)
    filtered, *blocks = finish(operands, (chunk,) * groups, scale, True)
    for m in reversed(range(1, groups)):
        blocks[m] = lax.ppermute(blocks[m], "orb", [(i, i ^ m) for i in range(groups)])
    tiles = pl.pallas_call(
        functools.partial(gram_kernel, orbitals=orbitals, width=width, scale=1.0 / (slabs * ROWS * NX)),
        out_shape=jax.ShapeDtypeStruct((slabs * groups, n), F32),
        in_specs=[SMEM] + [VMEM] * groups,
        out_specs=VMEM,
        scratch_shapes=[pltpu.VMEM((n, ROWS // groups * NX), BF16)] * 2 + [pltpu.VMEM((n, n), F32)],
        compiler_params=params(8),
        cost_estimate=pl.CostEstimate(flops=10**8, bytes_accessed=10**6, transcendentals=0),
        name="gram",
    )(place, *blocks)
    tiles = lax.all_to_all(tiles, ("grid", "orb"), 0, 0, tiled=True)
    gram = jnp.sum(tiles, axis=0)[: width * orbitals].reshape(width, orbitals).T
    return filtered.reshape(psi_in.shape), gram


def solution(mesh):
    placed = (
        P("orb", "grid", None, None),
        P("grid", None, None),
        P("grid", None, None),
        P("grid", None, None, None),
        P("grid", None),
    )
    return jax.shard_map(
        on_device,
        mesh=mesh,
        in_specs=placed,
        out_specs=(P("orb", "grid", None, None), P("orb", "grid")),
        check_vma=False,
    )
```

time: 142 us -> 123 us (0.87)
  blocking collectives: 43.9 us -> 22.6 us
  waiting for transfers between devices: 10.1 us -> 23.1 us
  Pallas kernels: 26.9 us -> 21.7 us
  other arithmetic: 4.97 us -> 0.44 us
  starting transfers between devices: 46.7 us -> 49.5 us
  local copies, waits for them, and re-layouts: 7.36 us -> 4.87 us
    all_to_all x2 -> x1, blocking collectives: 43.9 us -> 22.6 us  [on_device(): tiles = lax.all_to_all(tiles, ('grid', 'orb'), 0, 0, tiled=True)]
    ppermute x0 -> x3, waiting for transfers between devices: none -> 12.4 us  [on_device(): lax.ppermute(blocks[m], 'orb', [(i, i ^ m) for i in range(groups)])]
    pallas_call x3 -> x5, Pallas kernels: 21.7 us -> 17.9 us  [the longest x2 9.61 us: slab(): pl.pallas_call(functools.partial(slab_kernel, orbitals=orbitals, scale=sc...]
    ppermute x0 -> x3, starting transfers between devices: none -> 3.55 us  [on_device(): lax.ppermute(blocks[m], 'orb', [(i, i ^ m) for i in range(groups)])]
    slice x2 -> x1, local copies, waits for them, and re-layouts: 1.73 us -> 0.07 us  [on_device(): kb[:, 2 * OWNED:]]
    mul x2 -> x0, other arithmetic: 1.59 us -> none  [atoms(): own = (own + far[:, :OWNED]) * kb]
    add x2, other arithmetic: 1.58 us -> 0.01 us  [stage(): own = own + swap(to_mate, mates)]
    pallas_call x1, Pallas kernels: 5.22 us -> 3.75 us  [on_device(): pl.pallas_call(functools.partial(projector_kernel, orbitals=orbitals), ou...]
  transfers between devices with their start and end apart: 10 -> 13, of which waited for: 6 -> 6; matrix products, arithmetic and copies ran while one was open for 5% -> 1% of each run, Pallas kernels for 4% -> 11%
where the time goes in v2:
time: 123 us
  starting transfers between devices  49.5 us (40%)
  waiting for transfers between devices  23.1 us (19%)
  blocking collectives  22.6 us (18%)
  Pallas kernels  21.7 us (18%)
  local copies, waits for them, and re-layouts  4.87 us (4%)
    ppermute x10, starting transfers between devices, swap(): return lax.ppermute(x, 'grid', pairs)  46 us
    all_to_all x1, blocking collectives, on_device(): tiles = lax.all_to_all(tiles, ('grid', 'orb'), 0, 0, tiled=True)  22.6 us
    ppermute x3, waiting for transfers between devices, on_device(): lax.ppermute(blocks[m], 'orb', [(i, i ^ m) for i in range(groups)])  12.4 us
    ppermute x10, waiting for transfers between devices, swap(): return lax.ppermute(x, 'grid', pairs)  10.8 us
    pallas_call x2, Pallas kernels, slab(): pl.pallas_call(functools.partial(slab_kernel, orbitals=orbitals, scale=sc...  9.61 us
    pallas_call x2, Pallas kernels, finish(): pl.pallas_call(functools.partial(finish_kernel, orbitals=orbitals, scale=...  7.1 us
    pallas_call x1, Pallas kernels, on_device(): pl.pallas_call(functools.partial(projector_kernel, orbitals=orbitals), ou...  3.75 us
    ppermute x3, starting transfers between devices, on_device(): lax.ppermute(blocks[m], 'orb', [(i, i ^ m) for i in range(groups)])  3.55 us
  transfers between devices with their start and end apart: 13, of which 6 were waited for; matrix products, arithmetic and copies ran while one was open for 1% of the time, Pallas kernels for 11%

profile of v2, /device:TPU:1, one launch (start us, length us, event | category | flops | bytes accessed | tf_op | source)
XLA Modules:
  0.0 123.0 jit_solution(1851410405037792360)
XLA Ops:
  0.6 2.7 %collective-permute-start.2 = (f32[1536,128]{1,0:T(8,128)}, f32[1536,128]{1,0:T(8,128)S(1)}, u32[]{:S(2)}, u32[]{:S(2)}) collective-permute-start(f32[1536,128]{1,0:T(8,128)} %bitcast.11), channel_id=1, source_target_pairs={{0,252},{4,8},{8,4},{12,16},{16,12},{20,24},{24,20},{28,32},{32,28... | collective-permute-start | bytes 2359304 | tf_op jit(solution)/shard_map/ppermute | solution.py:256
  3.3 10.2 %collective-permute-start.1 = (f32[1536,128]{1,0:T(8,128)}, f32[1536,128]{1,0:T(8,128)S(1)}, u32[]{:S(2)}, u32[]{:S(2)}) collective-permute-start(f32[1536,128]{1,0:T(8,128)} %bitcast.12), channel_id=1, source_target_pairs={{0,4},{4,0},{8,12},{12,8},{16,20},{20,16},{24,28},{28,24},{32,36},... | collective-permute-start | bytes 2359304 | tf_op jit(solution)/shard_map/ppermute | solution.py:256
  13.5 0.8 reshape.34
  14.3 0.1 pad.8
  14.3 0.1 pad_slice_fusion
  14.4 0.1 pad_add_fusion.odd_ref.place_ref
  14.5 0.1 fusion.kb_ref.rest_0_
  14.6 1.1 copy-done
  15.7 0.7 copy-done.4
  16.4 0.7 copy-done.5
  17.1 3.7 %projectors.1 = (bf16[48,144,128]{2,1,0:T(8,128)(2,1)S(1)}, f32[32,128]{1,0:T(8,128)S(1)}, f32[32,128]{1,0:T(8,128)S(1)}) custom-call(s32[2]{0:T(128)S(1)} %pad_add_fusion.odd_ref.place_ref, s32[3,4,128]{2,1,0:T(4,128)S(1)} %copy-done.5, f32[3,16,128]{2,1,0:T(8,128)S(1)} %bitcast.19, f32[1,128]{1,0:T(1,128)S(1)} %fusion.kb_ref.rest_0_, f32[1536,128]{1,0:T(8,128)S(1)} %bitcast.13), custom_call_target="tpu_custom_call" | custom-call | flops 100000000 | bytes 10000000 | tf_op jit(solution)/shard_map/projectors/pallas_call | solution.py:300
  20.9 0.1 collective-permute-start
  21.0 1.2 collective-permute-done
  22.2 3.3 %collective-permute-done.3.far_msg = f32[32,128]{1,0:T(8,128)S(1)} collective-permute-done((f32[32,128]{1,0:T(8,128)S(1)}, f32[32,128]{1,0:T(8,128)S(1)}, u32[]{:S(2)}, u32[]{:S(2)}) %collective-permute-start.3) | collective-permute-done | bytes 16416 | tf_op jit(solution)/shard_map/ppermute | solution.py:256
  25.5 11.0 %collective-permute-start.4 = (f32[32,128]{1,0:T(8,128)S(1)}, f32[32,128]{1,0:T(8,128)S(1)}, u32[]{:S(2)}, u32[]{:S(2)}) collective-permute-start(f32[32,128]{1,0:T(8,128)S(1)} %collective-permute-done.3.far_msg), channel_id=1, source_target_pairs={{0,4},{4,0},{8,12},{12,8},{16,20},{20,16},{24,28},{28,24},{32,36},... | collective-permute-start | bytes 49160 | tf_op jit(solution)/shard_map/ppermute | solution.py:256
  36.4 0.7 copy-done.2
  37.2 4.8 %slab.2.slab_ref = f32[1536,128]{1,0:T(8,128)S(1)} custom-call(f32[1536,128]{1,0:T(8,128)S(1)} %bitcast.14, f32[48,128]{1,0:T(8,128)S(1)} %bitcast.17), custom_call_target="tpu_custom_call" | custom-call | flops 100000000 | bytes 10000000 | tf_op jit(solution)/shard_map/slab/pallas_call | solution.py:268
  42.0 3.7 %finish.2 = (f32[1536,128]{1,0:T(8,128)S(1)}, f32[32,128]{1,0:T(8,128)S(1)}, f32[32,128]{1,0:T(8,128)S(1)}) custom-call(s32[2]{0:T(128)S(1)} %pad_add_fusion.odd_ref.place_ref, f32[1536,128]{1,0:T(8,128)S(1)} %slab.2.slab_ref, f32[1536,128]{1,0:T(8,128)S(1)} %collective-permute-done.1.mate_ref, f32[1536,128]{1,0:T(8,128)S(1)} %collective-permute-done.2.far_ref, ...), custom_call_target="tpu_custom_call" | custom-call | flops 100000000 | bytes 10000000 | tf_op jit(solution)/shard_map/finish/pallas_call | solution.py:280
  45.8 0.1 collective-permute-start.7
  45.9 5.6 %collective-permute-start.6 = (f32[1536,128]{1,0:T(8,128)S(1)}, f32[1536,128]{1,0:T(8,128)S(1)}, u32[]{:S(2)}, u32[]{:S(2)}) collective-permute-start(f32[1536,128]{1,0:T(8,128)S(1)} %get-tuple-element.25.field_ref), channel_id=1, source_target_pairs={{0,4},{4,0},{8,12},{12,8},{16,20},{20,16},{24,28},{28,24},{32,36},... | collective-permute-start | bytes 2359304 | tf_op jit(solution)/shard_map/ppermute | solution.py:256
  51.4 1.9 %collective-permute-done.5 = f32[32,128]{1,0:T(8,128)S(1)} collective-permute-done((f32[32,128]{1,0:T(8,128)S(1)}, f32[32,128]{1,0:T(8,128)S(1)}, u32[]{:S(2)}, u32[]{:S(2)}) %collective-permute-start.5) | collective-permute-done | bytes 16416 | tf_op jit(solution)/shard_map/ppermute | solution.py:256
  53.4 4.4 %collective-permute-done.8.far_msg = f32[32,128]{1,0:T(8,128)S(1)} collective-permute-done((f32[32,128]{1,0:T(8,128)S(1)}, f32[32,128]{1,0:T(8,128)S(1)}, u32[]{:S(2)}, u32[]{:S(2)}) %collective-permute-start.8) | collective-permute-done | bytes 16416 | tf_op jit(solution)/shard_map/ppermute | solution.py:256
  57.7 16.4 %collective-permute-start.9 = (f32[32,128]{1,0:T(8,128)S(1)}, f32[32,128]{1,0:T(8,128)S(1)}, u32[]{:S(2)}, u32[]{:S(2)}) collective-permute-start(f32[32,128]{1,0:T(8,128)S(1)} %collective-permute-done.8.far_msg), channel_id=1, source_target_pairs={{0,4},{4,0},{8,12},{12,8},{16,20},{20,16},{24,28},{28,24},{32,36},... | collective-permute-start | bytes 49160 | tf_op jit(solution)/shard_map/ppermute | solution.py:256
  74.1 4.8 %slab.3.slab_ref = f32[1536,128]{1,0:T(8,128)S(1)} custom-call(f32[1536,128]{1,0:T(8,128)S(1)} %get-tuple-element.25.field_ref, f32[48,128]{1,0:T(8,128)S(1)} %bitcast.18, f32[1536,128]{1,0:T(8,128)S(1)} %bitcast.15), custom_call_target="tpu_custom_call" | custom-call | flops 100000000 | bytes 10000000 | tf_op jit(solution)/shard_map/slab/pallas_call | solution.py:268
  79.0 3.4 %finish.3 = (f32[1536,128]{1,0:T(8,128)}, f32[12,32,128]{2,1,0:T(8,128)S(1)}, f32[12,32,128]{2,1,0:T(8,128)S(1)}, f32[12,32,128]{2,1,0:T(8,128)S(1)}, f32[12,32,128]{2,1,0:T(8,128)S(1)}) custom-call(s32[2]{0:T(128)S(1)} %pad_add_fusion.odd_ref.place_ref, f32[1536,128]{1,0:T(8,128)S(1)} %slab.3.slab_ref, f32[1536,128]{1,0:T(8,128)S(1)} %collective-permute-done.6.mate_ref, ...), custom_call_target="tpu_custom_call" | custom-call | flops 100000000 | bytes 10000000 | tf_op jit(solution)/shard_map/finish/pallas_call | solution.py:280
  82.4 3.5 %collective-permute-start.12 = (f32[12,32,128]{2,1,0:T(8,128)S(1)}, f32[12,32,128]{2,1,0:T(8,128)S(1)}, u32[]{:S(2)}, u32[]{:S(2)}) collective-permute-start(f32[12,32,128]{2,1,0:T(8,128)S(1)} %get-tuple-element.31), channel_id=1, source_target_pairs={{0,3},{1,2},{2,1},{3,0},{4,7},{5,6},{6,5},{7,4},{8,11},{9,10},{10,... | collective-permute-start | bytes 589832 | tf_op jit(solution)/shard_map/ppermute | solution.py:318
  85.9 4.2 %collective-permute-done.10.refs_1_ = f32[12,32,128]{2,1,0:T(8,128)S(1)} collective-permute-done((f32[12,32,128]{2,1,0:T(8,128)S(1)}, f32[12,32,128]{2,1,0:T(8,128)S(1)}, u32[]{:S(2)}, u32[]{:S(2)}) %collective-permute-start.10) | collective-permute-done | bytes 196640 | tf_op jit(solution)/shard_map/ppermute | solution.py:318
  90.1 8.1 %collective-permute-done.11.refs_2_ = f32[12,32,128]{2,1,0:T(8,128)S(1)} collective-permute-done((f32[12,32,128]{2,1,0:T(8,128)S(1)}, f32[12,32,128]{2,1,0:T(8,128)S(1)}, u32[]{:S(2)}, u32[]{:S(2)}) %collective-permute-start.11) | collective-permute-done | bytes 196640 | tf_op jit(solution)/shard_map/ppermute | solution.py:318
  98.3 1.2 gram.1
  99.5 22.6 %all_to_all.9 = f32[256,1,128]{2,1,0:T(1,128)S(1)} all-to-all(f32[256,1,128]{2,1,0:T(1,128)S(1)} %bitcast.16), channel_id=1, replica_groups=mesh['grid'=64,'orb'=4] {'grid','orb'}, dimensions={0} | all-to-all | bytes 262144 | tf_op jit(solution)/shard_map/all_to_all | solution.py:329
  122.1 0.3 reduce_sum.9
  122.4 0.6 reshape.37
  (22 shorter events, 0.1 us)
Async XLA Ops:
  0.6 41.4 %collective-permute-start.2 = (f32[1536,128]{1,0:T(8,128)}, f32[1536,128]{1,0:T(8,128)S(1)}, u32[]{:S(2)}, u32[]{:S(2)}) collective-permute-start(f32[1536,128]{1,0:T(8,128)} %bitcast.11), channel_id=1, source_target_pairs={{0,252},{4,8},{8,4},{12,16},{16,12},{20,24},{24,20},{28,32},{32,28... | collective-permute-start | bytes 2359304 | tf_op jit(solution)/shard_map/ppermute | solution.py:256
  3.3 38.7 %collective-permute-start.1 = (f32[1536,128]{1,0:T(8,128)}, f32[1536,128]{1,0:T(8,128)S(1)}, u32[]{:S(2)}, u32[]{:S(2)}) collective-permute-start(f32[1536,128]{1,0:T(8,128)} %bitcast.12), channel_id=1, source_target_pairs={{0,4},{4,0},{8,12},{12,8},{16,20},{20,16},{24,28},{28,24},{32,36},... | collective-permute-start | bytes 2359304 | tf_op jit(solution)/shard_map/ppermute | solution.py:256
  14.6 1.1 copy-start
  15.7 0.7 copy-start.4
  16.4 0.7 copy-start.5
  20.9 1.3 %collective-permute-start = (f32[32,128]{1,0:T(8,128)S(1)}, f32[32,128]{1,0:T(8,128)S(1)}, u32[]{:S(2)}, u32[]{:S(2)}) collective-permute-start(f32[32,128]{1,0:T(8,128)S(1)} %get-tuple-element.18), channel_id=1, source_target_pairs={{0,4},{4,0},{8,12},{12,8},{16,20},{20,16},{24,28},{28,24},{32,36},... | collective-permute-start | bytes 49160 | tf_op jit(solution)/shard_map/ppermute | solution.py:256
  22.2 3.3 %collective-permute-start.3 = (f32[32,128]{1,0:T(8,128)S(1)}, f32[32,128]{1,0:T(8,128)S(1)}, u32[]{:S(2)}, u32[]{:S(2)}) collective-permute-start(f32[32,128]{1,0:T(8,128)S(1)} %add.15.own_msg), channel_id=1, source_target_pairs={{0,252},{4,8},{8,4},{12,16},{16,12},{20,24},{24,20},{28,32},{32,28... | collective-permute-start | bytes 49160 | tf_op jit(solution)/shard_map/ppermute | solution.py:256
  25.5 16.5 %collective-permute-start.4 = (f32[32,128]{1,0:T(8,128)S(1)}, f32[32,128]{1,0:T(8,128)S(1)}, u32[]{:S(2)}, u32[]{:S(2)}) collective-permute-start(f32[32,128]{1,0:T(8,128)S(1)} %collective-permute-done.3.far_msg), channel_id=1, source_target_pairs={{0,4},{4,0},{8,12},{12,8},{16,20},{20,16},{24,28},{28,24},{32,36},... | collective-permute-start | bytes 49160 | tf_op jit(solution)/shard_map/ppermute | solution.py:256
  36.4 0.7 copy-start.2
  42.0 32.1 %copy-start.1 = (f32[32,6,8,128]{3,2,1,0:T(8,128)S(1)}, f32[32,6,8,128]{3,2,1,0:T(8,128)}, u32[]{:S(2)}) copy-start(f32[32,6,8,128]{3,2,1,0:T(8,128)} %param.5) | copy-start | bytes 2359300
  42.0 32.1 %copy-start.3 = (f32[6,8,128]{2,1,0:T(8,128)S(1)}, f32[6,8,128]{2,1,0:T(8,128)}, u32[]{:S(2)}) copy-start(f32[6,8,128]{2,1,0:T(8,128)} %param.6) | copy-start | bytes 73732
  45.8 33.2 %collective-permute-start.7 = (f32[1536,128]{1,0:T(8,128)S(1)}, f32[1536,128]{1,0:T(8,128)S(1)}, u32[]{:S(2)}, u32[]{:S(2)}) collective-permute-start(f32[1536,128]{1,0:T(8,128)S(1)} %get-tuple-element.25.field_ref), channel_id=1, source_target_pairs={{0,252},{4,8},{8,4},{12,16},{16,12},{20,24},{24,20},{28,32},{32,28... | collective-permute-start | bytes 2359304 | tf_op jit(solution)/shard_map/ppermute | solution.py:256
  45.9 33.1 %collective-permute-start.6 = (f32[1536,128]{1,0:T(8,128)S(1)}, f32[1536,128]{1,0:T(8,128)S(1)}, u32[]{:S(2)}, u32[]{:S(2)}) collective-permute-start(f32[1536,128]{1,0:T(8,128)S(1)} %get-tuple-element.25.field_ref), channel_id=1, source_target_pairs={{0,4},{4,0},{8,12},{12,8},{16,20},{20,16},{24,28},{28,24},{32,36},... | collective-permute-start | bytes 2359304 | tf_op jit(solution)/shard_map/ppermute | solution.py:256
  51.4 1.9 %collective-permute-start.5 = (f32[32,128]{1,0:T(8,128)S(1)}, f32[32,128]{1,0:T(8,128)S(1)}, u32[]{:S(2)}, u32[]{:S(2)}) collective-permute-start(f32[32,128]{1,0:T(8,128)S(1)} %get-tuple-element.24), channel_id=1, source_target_pairs={{0,4},{4,0},{8,12},{12,8},{16,20},{20,16},{24,28},{28,24},{32,36},... | collective-permute-start | bytes 49160 | tf_op jit(solution)/shard_map/ppermute | solution.py:256
  53.4 4.4 %collective-permute-start.8 = (f32[32,128]{1,0:T(8,128)S(1)}, f32[32,128]{1,0:T(8,128)S(1)}, u32[]{:S(2)}, u32[]{:S(2)}) collective-permute-start(f32[32,128]{1,0:T(8,128)S(1)} %add.16.own_msg), channel_id=1, source_target_pairs={{0,252},{4,8},{8,4},{12,16},{16,12},{20,24},{24,20},{28,32},{32,28... | collective-permute-start | bytes 49160 | tf_op jit(solution)/shard_map/ppermute | solution.py:256
  57.7 21.2 %collective-permute-start.9 = (f32[32,128]{1,0:T(8,128)S(1)}, f32[32,128]{1,0:T(8,128)S(1)}, u32[]{:S(2)}, u32[]{:S(2)}) collective-permute-start(f32[32,128]{1,0:T(8,128)S(1)} %collective-permute-done.8.far_msg), channel_id=1, source_target_pairs={{0,4},{4,0},{8,12},{12,8},{16,20},{20,16},{24,28},{28,24},{32,36},... | collective-permute-start | bytes 49160 | tf_op jit(solution)/shard_map/ppermute | solution.py:256
  82.4 7.8 %collective-permute-start.10 = (f32[12,32,128]{2,1,0:T(8,128)S(1)}, f32[12,32,128]{2,1,0:T(8,128)S(1)}, u32[]{:S(2)}, u32[]{:S(2)}) collective-permute-start(f32[12,32,128]{2,1,0:T(8,128)S(1)} %get-tuple-element.29), channel_id=1, source_target_pairs={{0,1},{1,0},{2,3},{3,2},{4,5},{5,4},{6,7},{7,6},{8,9},{9,8},{10,11... | collective-permute-start | bytes 589832 | tf_op jit(solution)/shard_map/ppermute | solution.py:318
  82.4 15.9 %collective-permute-start.11 = (f32[12,32,128]{2,1,0:T(8,128)S(1)}, f32[12,32,128]{2,1,0:T(8,128)S(1)}, u32[]{:S(2)}, u32[]{:S(2)}) collective-permute-start(f32[12,32,128]{2,1,0:T(8,128)S(1)} %get-tuple-element.30), channel_id=1, source_target_pairs={{0,2},{1,3},{2,0},{3,1},{4,6},{5,7},{6,4},{7,5},{8,10},{9,11},{10,... | collective-permute-start | bytes 589832 | tf_op jit(solution)/shard_map/ppermute | solution.py:318
  82.4 15.9 %collective-permute-start.12 = (f32[12,32,128]{2,1,0:T(8,128)S(1)}, f32[12,32,128]{2,1,0:T(8,128)S(1)}, u32[]{:S(2)}, u32[]{:S(2)}) collective-permute-start(f32[12,32,128]{2,1,0:T(8,128)S(1)} %get-tuple-element.31), channel_id=1, source_target_pairs={{0,3},{1,2},{2,1},{3,0},{4,7},{5,6},{6,5},{7,4},{8,11},{9,10},{10,... | collective-permute-start | bytes 589832 | tf_op jit(solution)/shard_map/ppermute | solution.py:318

commit v3 on v2

--- a/solution.py
+++ b/solution.py
@@ -91,7 +91,7 @@
     for frame in range(3):
         piece = frame + even * (2 - 2 * frame)
         index = index_ref[piece]
-        value = value_ref[piece]
+        value = jnp.concatenate([value_ref[piece, a] for a in range(SLOTS)], axis=0)
         parts = [p.astype(F32) for p in two_parts(value)]
         hits = []
         for a in range(SLOTS):
@@ -295,6 +295,7 @@
         from_far = swap(own, fars)
         field, own = lax.optimization_barrier((field, own))
         local = slab(field, scale, back, *start)
+        from_far, local = lax.optimization_barrier((from_far, local))
         return local, mate, far, proj, own, from_far, swap(from_far, mates)
 
     proj, own, to_mate = pl.pallas_call(
@@ -306,7 +307,7 @@
         compiler_params=params(16),
         cost_estimate=pl.CostEstimate(flops=10**8, bytes_accessed=10**7, transcendentals=0),
         name="projectors",
-    )(place, proj_index, proj_value.reshape(3, OWNED, PTS), kb, psi)
+    )(place, proj_index, proj_value, kb, psi)
     scale = SIGMA / HALF_WIDTH
     operands = stage(psi, proj, own, to_mate, scale, None)
     first, own, to_mate = finish((*operands, kb), (message_shape,) * 2, scale, False)

time: 123 us -> 115 us (0.935)
  waiting for transfers between devices: 23.1 us -> 16.8 us
  starting transfers between devices: 49.5 us -> 47.2 us
    ppermute x10, waiting for transfers between devices: 10.8 us -> 4.8 us  [swap(): return lax.ppermute(x, 'grid', pairs)]
    ppermute x10, starting transfers between devices: 46 us -> 43.6 us  [swap(): return lax.ppermute(x, 'grid', pairs)]
  transfers between devices with their start and end apart: 13 -> 13, of which waited for: 6 -> 6; matrix products, arithmetic and copies ran while one was open for 1% -> 1% of each run, Pallas kernels for 11% -> 12%
where the time goes in v3:
time: 115 us
  starting transfers between devices  47.2 us (41%)
  blocking collectives  23.3 us (20%)
  Pallas kernels  21.7 us (19%)
  waiting for transfers between devices  16.8 us (15%)
  local copies, waits for them, and re-layouts  4.86 us (4%)
    ppermute x10, starting transfers between devices, swap(): return lax.ppermute(x, 'grid', pairs)  43.6 us
    all_to_all x1, blocking collectives, on_device(): tiles = lax.all_to_all(tiles, ('grid', 'orb'), 0, 0, tiled=True)  23.3 us
    ppermute x3, waiting for transfers between devices, on_device(): lax.ppermute(blocks[m], 'orb', [(i, i ^ m) for i in range(groups)])  12 us
    pallas_call x2, Pallas kernels, slab(): pl.pallas_call(functools.partial(slab_kernel, orbitals=orbitals, scale=sc...  9.61 us
    pallas_call x2, Pallas kernels, finish(): pl.pallas_call(functools.partial(finish_kernel, orbitals=orbitals, scale=...  7.1 us
    ppermute x10, waiting for transfers between devices, swap(): return lax.ppermute(x, 'grid', pairs)  4.8 us
    pallas_call x1, Pallas kernels, on_device(): pl.pallas_call(functools.partial(projector_kernel, orbitals=orbitals), ou...  3.74 us
    ppermute x3, starting transfers between devices, on_device(): lax.ppermute(blocks[m], 'orb', [(i, i ^ m) for i in range(groups)])  3.55 us
  transfers between devices with their start and end apart: 13, of which 6 were waited for; matrix products, arithmetic and copies ran while one was open for 1% of the time, Pallas kernels for 12%

profile of v3, /device:TPU:1, one launch (start us, length us, event | category | flops | bytes accessed | tf_op | source)
XLA Modules:
  0.0 115.0 jit_solution(15859062523829577894)
XLA Ops:
  0.6 2.7 %collective-permute-start.3 = (f32[1536,128]{1,0:T(8,128)}, f32[1536,128]{1,0:T(8,128)S(1)}, u32[]{:S(2)}, u32[]{:S(2)}) collective-permute-start(f32[1536,128]{1,0:T(8,128)} %bitcast.10), channel_id=1, source_target_pairs={{0,252},{4,8},{8,4},{12,16},{16,12},{20,24},{24,20},{28,32},{32,28... | collective-permute-start | bytes 2359304 | tf_op jit(solution)/shard_map/ppermute | solution.py:256
  3.3 10.2 %collective-permute-start.2 = (f32[1536,128]{1,0:T(8,128)}, f32[1536,128]{1,0:T(8,128)S(1)}, u32[]{:S(2)}, u32[]{:S(2)}) collective-permute-start(f32[1536,128]{1,0:T(8,128)} %bitcast.11), channel_id=1, source_target_pairs={{0,4},{4,0},{8,12},{12,8},{16,20},{20,16},{24,28},{28,24},{32,36},... | collective-permute-start | bytes 2359304 | tf_op jit(solution)/shard_map/ppermute | solution.py:256
  13.5 0.8 reshape.29
  14.3 0.1 pad.8
  14.3 0.1 pad_slice_fusion
  14.4 0.1 pad_add_fusion.odd_ref.place_ref
  14.5 0.1 fusion.kb_ref.rest_0_
  14.6 1.1 copy-done
  15.7 0.7 copy-done.4
  16.4 0.7 copy-done.5
  17.1 3.7 %projectors.1 = (bf16[48,144,128]{2,1,0:T(8,128)(2,1)S(1)}, f32[32,128]{1,0:T(8,128)S(1)}, f32[32,128]{1,0:T(8,128)S(1)}) custom-call(s32[2]{0:T(128)S(1)} %pad_add_fusion.odd_ref.place_ref, s32[3,4,128]{2,1,0:T(4,128)S(1)} %copy-done.5, f32[3,4,4,128]{3,2,1,0:T(4,128)S(1)} %copy-done.4, f32[1,128]{1,0:T(1,128)S(1)} %fusion.kb_ref.rest_0_, ...), custom_call_target="tpu_custom_call" | custom-call | flops 100000000 | bytes 10000000 | tf_op jit(solution)/shard_map/projectors/pallas_call | solution.py:301
  20.9 0.1 collective-permute-start
  21.0 1.2 %collective-permute-done = f32[32,128]{1,0:T(8,128)S(1)} collective-permute-done((f32[32,128]{1,0:T(8,128)S(1)}, f32[32,128]{1,0:T(8,128)S(1)}, u32[]{:S(2)}, u32[]{:S(2)}) %collective-permute-start) | collective-permute-done | bytes 16416 | tf_op jit(solution)/shard_map/ppermute | solution.py:256
  22.2 0.7 copy-done.2
  22.9 4.8 %slab.2.slab_ref = f32[1536,128]{1,0:T(8,128)S(1)} custom-call(f32[1536,128]{1,0:T(8,128)S(1)} %bitcast.13, f32[48,128]{1,0:T(8,128)S(1)} %bitcast.16), custom_call_target="tpu_custom_call" | custom-call | flops 100000000 | bytes 10000000 | tf_op jit(solution)/shard_map/slab/pallas_call | solution.py:268
  27.7 8.7 %collective-permute-start.4 = (f32[32,128]{1,0:T(8,128)S(1)}, f32[32,128]{1,0:T(8,128)S(1)}, u32[]{:S(2)}, u32[]{:S(2)}) collective-permute-start(f32[32,128]{1,0:T(8,128)S(1)} %collective-permute-done.1.far_msg), channel_id=1, source_target_pairs={{0,4},{4,0},{8,12},{12,8},{16,20},{20,16},{24,28},{28,24},{32,36},... | collective-permute-start | bytes 49160 | tf_op jit(solution)/shard_map/ppermute | solution.py:256
  36.4 0.8 collective-permute-done.4.beyond_msg
  37.3 3.7 %finish.2 = (f32[1536,128]{1,0:T(8,128)S(1)}, f32[32,128]{1,0:T(8,128)S(1)}, f32[32,128]{1,0:T(8,128)S(1)}) custom-call(s32[2]{0:T(128)S(1)} %pad_add_fusion.odd_ref.place_ref, f32[1536,128]{1,0:T(8,128)S(1)} %slab.2.slab_ref, f32[1536,128]{1,0:T(8,128)S(1)} %collective-permute-done.2.mate_ref, f32[1536,128]{1,0:T(8,128)S(1)} %collective-permute-done.3.far_ref, ...), custom_call_target="tpu_custom_call" | custom-call | flops 100000000 | bytes 10000000 | tf_op jit(solution)/shard_map/finish/pallas_call | solution.py:280
  41.0 0.1 collective-permute-start.8
  41.1 5.9 %collective-permute-start.7 = (f32[1536,128]{1,0:T(8,128)S(1)}, f32[1536,128]{1,0:T(8,128)S(1)}, u32[]{:S(2)}, u32[]{:S(2)}) collective-permute-start(f32[1536,128]{1,0:T(8,128)S(1)} %get-tuple-element.31.field_ref), channel_id=1, source_target_pairs={{0,4},{4,0},{8,12},{12,8},{16,20},{20,16},{24,28},{28,24},{32,36},... | collective-permute-start | bytes 2359304 | tf_op jit(solution)/shard_map/ppermute | solution.py:256
  47.0 1.9 %collective-permute-done.5 = f32[32,128]{1,0:T(8,128)S(1)} collective-permute-done((f32[32,128]{1,0:T(8,128)S(1)}, f32[32,128]{1,0:T(8,128)S(1)}, u32[]{:S(2)}, u32[]{:S(2)}) %collective-permute-start.5) | collective-permute-done | bytes 16416 | tf_op jit(solution)/shard_map/ppermute | solution.py:256
  49.0 4.8 %slab.3.slab_ref = f32[1536,128]{1,0:T(8,128)S(1)} custom-call(f32[1536,128]{1,0:T(8,128)S(1)} %get-tuple-element.31.field_ref, f32[48,128]{1,0:T(8,128)S(1)} %bitcast.17, f32[1536,128]{1,0:T(8,128)S(1)} %bitcast.14), custom_call_target="tpu_custom_call" | custom-call | flops 100000000 | bytes 10000000 | tf_op jit(solution)/shard_map/slab/pallas_call | solution.py:268
  53.8 15.9 %collective-permute-start.9 = (f32[32,128]{1,0:T(8,128)S(1)}, f32[32,128]{1,0:T(8,128)S(1)}, u32[]{:S(2)}, u32[]{:S(2)}) collective-permute-start(f32[32,128]{1,0:T(8,128)S(1)} %collective-permute-done.6.far_msg), channel_id=1, source_target_pairs={{0,4},{4,0},{8,12},{12,8},{16,20},{20,16},{24,28},{28,24},{32,36},... | collective-permute-start | bytes 49160 | tf_op jit(solution)/shard_map/ppermute | solution.py:256
  69.7 0.8 collective-permute-done.9.beyond_msg
  70.6 3.4 %finish.3 = (f32[1536,128]{1,0:T(8,128)}, f32[12,32,128]{2,1,0:T(8,128)S(1)}, f32[12,32,128]{2,1,0:T(8,128)S(1)}, f32[12,32,128]{2,1,0:T(8,128)S(1)}, f32[12,32,128]{2,1,0:T(8,128)S(1)}) custom-call(s32[2]{0:T(128)S(1)} %pad_add_fusion.odd_ref.place_ref, f32[1536,128]{1,0:T(8,128)S(1)} %slab.3.slab_ref, f32[1536,128]{1,0:T(8,128)S(1)} %collective-permute-done.7.mate_ref, ...), custom_call_target="tpu_custom_call" | custom-call | flops 100000000 | bytes 10000000 | tf_op jit(solution)/shard_map/finish/pallas_call | solution.py:280
  74.0 3.5 %collective-permute-start.12 = (f32[12,32,128]{2,1,0:T(8,128)S(1)}, f32[12,32,128]{2,1,0:T(8,128)S(1)}, u32[]{:S(2)}, u32[]{:S(2)}) collective-permute-start(f32[12,32,128]{2,1,0:T(8,128)S(1)} %get-tuple-element.39), channel_id=1, source_target_pairs={{0,3},{1,2},{2,1},{3,0},{4,7},{5,6},{6,5},{7,4},{8,11},{9,10},{10,... | collective-permute-start | bytes 589832 | tf_op jit(solution)/shard_map/ppermute | solution.py:319
  77.5 3.8 %collective-permute-done.10.refs_1_ = f32[12,32,128]{2,1,0:T(8,128)S(1)} collective-permute-done((f32[12,32,128]{2,1,0:T(8,128)S(1)}, f32[12,32,128]{2,1,0:T(8,128)S(1)}, u32[]{:S(2)}, u32[]{:S(2)}) %collective-permute-start.10) | collective-permute-done | bytes 196640 | tf_op jit(solution)/shard_map/ppermute | solution.py:319
  81.4 8.1 %collective-permute-done.11.refs_2_ = f32[12,32,128]{2,1,0:T(8,128)S(1)} collective-permute-done((f32[12,32,128]{2,1,0:T(8,128)S(1)}, f32[12,32,128]{2,1,0:T(8,128)S(1)}, u32[]{:S(2)}, u32[]{:S(2)}) %collective-permute-start.11) | collective-permute-done | bytes 196640 | tf_op jit(solution)/shard_map/ppermute | solution.py:319
  89.5 1.2 %gram.1 = f32[256,128]{1,0:T(8,128)S(1)} custom-call(s32[2]{0:T(128)S(1)} %pad_add_fusion.odd_ref.place_ref, f32[12,32,128]{2,1,0:T(8,128)S(1)} %get-tuple-element.36.refs_0_, f32[12,32,128]{2,1,0:T(8,128)S(1)} %collective-permute-done.10.refs_1_, f32[12,32,128]{2,1,0:T(8,128)S(1)} %collective-permute-done.11.refs_2_, ...), custom_call_target="tpu_custom_call" | custom-call | flops 100000000 | bytes 1000000 | tf_op jit(solution)/shard_map/gram/pallas_call | solution.py:320
  90.7 23.3 %all_to_all.9 = f32[256,1,128]{2,1,0:T(1,128)S(1)} all-to-all(f32[256,1,128]{2,1,0:T(1,128)S(1)} %bitcast.15), channel_id=1, replica_groups=mesh['grid'=64,'orb'=4] {'grid','orb'}, dimensions={0} | all-to-all | bytes 262144 | tf_op jit(solution)/shard_map/all_to_all | solution.py:330
  114.0 0.3 reduce_sum.9
  114.3 0.6 reshape.33
  (22 shorter events, 0.1 us)
Async XLA Ops:
  0.6 36.7 %collective-permute-start.3 = (f32[1536,128]{1,0:T(8,128)}, f32[1536,128]{1,0:T(8,128)S(1)}, u32[]{:S(2)}, u32[]{:S(2)}) collective-permute-start(f32[1536,128]{1,0:T(8,128)} %bitcast.10), channel_id=1, source_target_pairs={{0,252},{4,8},{8,4},{12,16},{16,12},{20,24},{24,20},{28,32},{32,28... | collective-permute-start | bytes 2359304 | tf_op jit(solution)/shard_map/ppermute | solution.py:256
  3.3 34.0 %collective-permute-start.2 = (f32[1536,128]{1,0:T(8,128)}, f32[1536,128]{1,0:T(8,128)S(1)}, u32[]{:S(2)}, u32[]{:S(2)}) collective-permute-start(f32[1536,128]{1,0:T(8,128)} %bitcast.11), channel_id=1, source_target_pairs={{0,4},{4,0},{8,12},{12,8},{16,20},{20,16},{24,28},{28,24},{32,36},... | collective-permute-start | bytes 2359304 | tf_op jit(solution)/shard_map/ppermute | solution.py:256
  14.6 1.1 copy-start
  15.7 0.7 copy-start.4
  16.4 0.7 copy-start.5
  20.9 1.3 %collective-permute-start = (f32[32,128]{1,0:T(8,128)S(1)}, f32[32,128]{1,0:T(8,128)S(1)}, u32[]{:S(2)}, u32[]{:S(2)}) collective-permute-start(f32[32,128]{1,0:T(8,128)S(1)} %get-tuple-element.22), channel_id=1, source_target_pairs={{0,4},{4,0},{8,12},{12,8},{16,20},{20,16},{24,28},{28,24},{32,36},... | collective-permute-start | bytes 49160 | tf_op jit(solution)/shard_map/ppermute | solution.py:256
  22.1 5.6 %collective-permute-start.1 = (f32[32,128]{1,0:T(8,128)S(1)}, f32[32,128]{1,0:T(8,128)S(1)}, u32[]{:S(2)}, u32[]{:S(2)}) collective-permute-start(f32[32,128]{1,0:T(8,128)S(1)} %add.15.own_msg), channel_id=1, source_target_pairs={{0,252},{4,8},{8,4},{12,16},{16,12},{20,24},{24,20},{28,32},{32,28... | collective-permute-start | bytes 49160 | tf_op jit(solution)/shard_map/ppermute | solution.py:256
  22.1 0.7 copy-start.2
  27.7 9.6 %collective-permute-start.4 = (f32[32,128]{1,0:T(8,128)S(1)}, f32[32,128]{1,0:T(8,128)S(1)}, u32[]{:S(2)}, u32[]{:S(2)}) collective-permute-start(f32[32,128]{1,0:T(8,128)S(1)} %collective-permute-done.1.far_msg), channel_id=1, source_target_pairs={{0,4},{4,0},{8,12},{12,8},{16,20},{20,16},{24,28},{28,24},{32,36},... | collective-permute-start | bytes 49160 | tf_op jit(solution)/shard_map/ppermute | solution.py:256
  37.3 11.7 %copy-start.1 = (f32[32,6,8,128]{3,2,1,0:T(8,128)S(1)}, f32[32,6,8,128]{3,2,1,0:T(8,128)}, u32[]{:S(2)}) copy-start(f32[32,6,8,128]{3,2,1,0:T(8,128)} %param.5) | copy-start | bytes 2359300
  37.3 11.7 %copy-start.3 = (f32[6,8,128]{2,1,0:T(8,128)S(1)}, f32[6,8,128]{2,1,0:T(8,128)}, u32[]{:S(2)}) copy-start(f32[6,8,128]{2,1,0:T(8,128)} %param.6) | copy-start | bytes 73732
  41.0 29.6 %collective-permute-start.8 = (f32[1536,128]{1,0:T(8,128)S(1)}, f32[1536,128]{1,0:T(8,128)S(1)}, u32[]{:S(2)}, u32[]{:S(2)}) collective-permute-start(f32[1536,128]{1,0:T(8,128)S(1)} %get-tuple-element.31.field_ref), channel_id=1, source_target_pairs={{0,252},{4,8},{8,4},{12,16},{16,12},{20,24},{24,20},{28,32},{32,28... | collective-permute-start | bytes 2359304 | tf_op jit(solution)/shard_map/ppermute | solution.py:256
  41.1 29.5 %collective-permute-start.7 = (f32[1536,128]{1,0:T(8,128)S(1)}, f32[1536,128]{1,0:T(8,128)S(1)}, u32[]{:S(2)}, u32[]{:S(2)}) collective-permute-start(f32[1536,128]{1,0:T(8,128)S(1)} %get-tuple-element.31.field_ref), channel_id=1, source_target_pairs={{0,4},{4,0},{8,12},{12,8},{16,20},{20,16},{24,28},{28,24},{32,36},... | collective-permute-start | bytes 2359304 | tf_op jit(solution)/shard_map/ppermute | solution.py:256
  47.0 1.9 %collective-permute-start.5 = (f32[32,128]{1,0:T(8,128)S(1)}, f32[32,128]{1,0:T(8,128)S(1)}, u32[]{:S(2)}, u32[]{:S(2)}) collective-permute-start(f32[32,128]{1,0:T(8,128)S(1)} %get-tuple-element.29), channel_id=1, source_target_pairs={{0,4},{4,0},{8,12},{12,8},{16,20},{20,16},{24,28},{28,24},{32,36},... | collective-permute-start | bytes 49160 | tf_op jit(solution)/shard_map/ppermute | solution.py:256
  49.0 4.8 %collective-permute-start.6 = (f32[32,128]{1,0:T(8,128)S(1)}, f32[32,128]{1,0:T(8,128)S(1)}, u32[]{:S(2)}, u32[]{:S(2)}) collective-permute-start(f32[32,128]{1,0:T(8,128)S(1)} %add.16.own_msg), channel_id=1, source_target_pairs={{0,252},{4,8},{8,4},{12,16},{16,12},{20,24},{24,20},{28,32},{32,28... | collective-permute-start | bytes 49160 | tf_op jit(solution)/shard_map/ppermute | solution.py:256
  53.8 16.8 %collective-permute-start.9 = (f32[32,128]{1,0:T(8,128)S(1)}, f32[32,128]{1,0:T(8,128)S(1)}, u32[]{:S(2)}, u32[]{:S(2)}) collective-permute-start(f32[32,128]{1,0:T(8,128)S(1)} %collective-permute-done.6.far_msg), channel_id=1, source_target_pairs={{0,4},{4,0},{8,12},{12,8},{16,20},{20,16},{24,28},{28,24},{32,36},... | collective-permute-start | bytes 49160 | tf_op jit(solution)/shard_map/ppermute | solution.py:256
  74.0 7.4 %collective-permute-start.10 = (f32[12,32,128]{2,1,0:T(8,128)S(1)}, f32[12,32,128]{2,1,0:T(8,128)S(1)}, u32[]{:S(2)}, u32[]{:S(2)}) collective-permute-start(f32[12,32,128]{2,1,0:T(8,128)S(1)} %get-tuple-element.37), channel_id=1, source_target_pairs={{0,1},{1,0},{2,3},{3,2},{4,5},{5,4},{6,7},{7,6},{8,9},{9,8},{10,11... | collective-permute-start | bytes 589832 | tf_op jit(solution)/shard_map/ppermute | solution.py:319
  74.0 15.5 %collective-permute-start.11 = (f32[12,32,128]{2,1,0:T(8,128)S(1)}, f32[12,32,128]{2,1,0:T(8,128)S(1)}, u32[]{:S(2)}, u32[]{:S(2)}) collective-permute-start(f32[12,32,128]{2,1,0:T(8,128)S(1)} %get-tuple-element.38), channel_id=1, source_target_pairs={{0,2},{1,3},{2,0},{3,1},{4,6},{5,7},{6,4},{7,5},{8,10},{9,11},{10,... | collective-permute-start | bytes 589832 | tf_op jit(solution)/shard_map/ppermute | solution.py:319
  74.0 15.5 %collective-permute-start.12 = (f32[12,32,128]{2,1,0:T(8,128)S(1)}, f32[12,32,128]{2,1,0:T(8,128)S(1)}, u32[]{:S(2)}, u32[]{:S(2)}) collective-permute-start(f32[12,32,128]{2,1,0:T(8,128)S(1)} %get-tuple-element.39), channel_id=1, source_target_pairs={{0,3},{1,2},{2,1},{3,0},{4,7},{5,6},{6,5},{7,4},{8,11},{9,10},{10,... | collective-permute-start | bytes 589832 | tf_op jit(solution)/shard_map/ppermute | solution.py:319

commit v4 on v2

--- a/solution.py
+++ b/solution.py
@@ -83,15 +83,14 @@
     mate_ref[...] = jnp.where(sent, mate, 0.0)
 
 
-def projector_kernel(odd_ref, index_ref, value_ref, kb_ref, psi_ref, proj_ref, own_ref, mate_ref, lhs_ref, *, orbitals):
-    even = 1 - odd_ref[0]
+def fill_projectors(even, index_of, value_of, proj_ref, lhs_ref):
     slot = lax.broadcasted_iota(jnp.int32, (OWNED, PTS), 0) // PROJ
     lane_no = lax.broadcasted_iota(jnp.int32, (NX, PTS), 0)
     row_no = lax.broadcasted_iota(jnp.int32, (ROWS, OWNED, PTS), 0)
     for frame in range(3):
         piece = frame + even * (2 - 2 * frame)
-        index = index_ref[piece]
-        value = value_ref[piece]
+        index = index_of(piece)
+        value = value_of(piece)
         parts = [p.astype(F32) for p in two_parts(value)]
         hits = []
         for a in range(SLOTS):
@@ -109,59 +108,90 @@
         proj_ref[:, at : at + OWNED, :] = head
         proj_ref[:, KAM + at : KAM + at + OWNED, :] = tail
         proj_ref[:, 2 * KAM + at : 2 * KAM + at + OWNED, :] = head
+
+
+def projector_kernel(place_ref, index_ref, value_ref, kb_ref, psi_ref, proj_ref, own_ref, mate_ref, lhs_ref, *, orbitals):
+    def value_of(piece):
+        return jnp.concatenate([value_ref[piece, a] for a in range(SLOTS)], axis=0)
+
+    fill_projectors(1 - place_ref[0], lambda piece: index_ref[piece], value_of, proj_ref, lhs_ref)
     put_messages(project(psi_ref, proj_ref, orbitals), kb_ref, own_ref, mate_ref)
+
+
+def far_projector_kernel(place_ref, message_ref, proj_ref, lhs_ref, *, index_at, value_at):
+    def index_of(piece):
+        return message_ref[pl.ds(index_at + piece * SLOTS, SLOTS), :].astype(jnp.int32)
+
+    def value_of(piece):
+        return message_ref[pl.ds(pl.multiple_of(value_at + piece * OWNED, 8), OWNED), :]
+
+    fill_projectors(place_ref[0], index_of, value_of, proj_ref, lhs_ref)
 
 
 def weights(scale):
     return [-0.5 * scale * x for x in LAP_COEF]
 
 
-def places(odd_ref):
-    odd = odd_ref[0]
+def places(odd):
     return [NY * ((PLANES - 1 - j) + odd * (2 * j - PLANES + 1)) for j in range(PLANES)]
+
+
+def banded(size, period, c):
+    i, j = (lax.broadcasted_iota(jnp.int32, (size, size), d) for d in (0, 1))
+    ahead = (j - i) & (period - 1)
+    matrix = jnp.zeros((size, size), F32)
+    for k in range(1, 7):
+        for by in (k, -k):
+            matrix = matrix + jnp.where(ahead == by % period, c[k], 0.0)
+    return two_parts(jnp.where(i // period == j // period, matrix, 0.0))
 
 
 def slab_kernel(field_ref, v_ref, *rest, orbitals, scale, back):
     start_ref = rest[0] if back is not None else None
-    out_ref, v_scr = rest[-2:]
+    out_ref, v_scr, planar_ref = rest[-3:]
     v_scr[...] = (v_ref[...] - (CENTRE + 1.5 * LAP_COEF[0])) * scale
     c = weights(scale)
+    head, tail = banded(NX, NX, c)
+    along_x = jnp.concatenate(
+        [jnp.concatenate([head, tail], axis=1), jnp.concatenate([head, jnp.zeros_like(tail)], axis=1)], axis=0
+    )
+    head, tail = banded(NX, NY, c)
+    along_y = jnp.concatenate([head, head, tail], axis=1)
+
+    def block(i, carry):
+        at = pl.ds(pl.multiple_of(i * NX, NX), NX)
+        head, tail = two_parts(field_ref[at, :])
+        both = dot_nn(jnp.concatenate([head, tail], axis=1), along_x)
+        across = dot_nn(along_y, jnp.concatenate([head, tail, head], axis=0))
+        planar_ref[at, :] = both[:, :NX] + both[:, NX:] + across
+        return carry
+
+    lax.fori_loop(0, orbitals * ROWS // NX, block, 0, unroll=4)
 
     def orbital(o, carry):
         base = o * ROWS
         spots = [pl.ds(pl.multiple_of(base + NY * j, NY), NY) for j in range(PLANES)]
         cells = [field_ref[s, :] for s in spots]
         for j in range(PLANES):
-            f = cells[j]
-            total = f * v_scr[NY * j : NY * j + NY, :]
+            total = planar_ref[spots[j], :] + cells[j] * v_scr[NY * j : NY * j + NY, :]
             if back is not None:
                 total = total + back * start_ref[spots[j], :]
-            for k in range(1, 7):
-                along = pltpu.roll(f, k, 1) + pltpu.roll(f, NX - k, 1)
-                for other in (j - k, j + k):
-                    if 0 <= other < PLANES:
-                        along = along + cells[other]
-                total = total + c[k] * along
-            for k, weight in ((1, c[1]), (2, c[2] + c[6]), (3, c[3] + c[5])):
-                total = total + weight * (pltpu.roll(f, k, 0) + pltpu.roll(f, NY - k, 0))
-            total = total + (2.0 * c[4]) * pltpu.roll(f, 4, 0)
+            for k in range(1, PLANES):
+                others = [cells[i] for i in (j - k, j + k) if 0 <= i < PLANES]
+                if others:
+                    total = total + c[k] * sum(others[1:], others[0])
             out_ref[spots[j], :] = total
         return carry
 
-    lax.fori_loop(0, orbitals, orbital, 0)
-
-
-def finish_kernel(place_ref, slab_ref, mate_ref, far_ref, proj_ref, own_msg, far_msg, beyond_msg, *rest, orbitals, scale, last):
-    if last:
-        out_ref, *chunk_refs, nonlocal_ref = rest
-    else:
-        kb_ref, out_ref, own_out, mate_out, nonlocal_ref = rest
-    own, far, beyond = own_msg[...], far_msg[...], beyond_msg[...]
+    lax.fori_loop(0, orbitals, orbital, 0, unroll=2)
+
+
+def shift(x, by):
+    return pltpu.roll(x, NX - by, 1)
+
+
+def atom_sums(own, far, beyond):
     lane = lanes(own.shape)
-
-    def shift(x, by):
-        return pltpu.roll(x, NX - by, 1)
-
     first, second = lane < OWNED, lane < 2 * OWNED
     sums = own + jnp.where(
         first,
@@ -171,8 +201,11 @@
     energy = jnp.where(
         first, shift(own, 5 * OWNED), jnp.where(second, shift(own, 2 * OWNED), shift(far, OWNED))
     )
-    coeff = (sums * energy * scale)[:, :KAM]
-    head, tail = two_parts(coeff)
+    return jnp.where(lane < KAM, sums * energy, 0.0)
+
+
+def add_rest(out_ref, slab_ref, mate_ref, far_ref, proj_ref, coeff, nonlocal_ref, odd, scale, orbitals):
+    head, tail = two_parts((coeff * scale)[:, :KAM])
     lhs = jnp.concatenate([head, head, tail], axis=1)
 
     def spread(pair, carry):
@@ -185,7 +218,7 @@
 
     lax.fori_loop(0, ROWS // 2, spread, 0, unroll=4)
     c = weights(scale)
-    place = places(place_ref)
+    place = places(odd)
 
     def orbital(o, carry):
         base = o * ROWS
@@ -206,14 +239,42 @@
         return carry
 
     lax.fori_loop(0, orbitals, orbital, 0, unroll=2)
-    if last:
-        share = ROWS // len(chunk_refs)
-        for m, chunk_ref in enumerate(chunk_refs):
-            at = (place_ref[1] ^ m) * share
-            for i in range(share):
-                chunk_ref[i] = row_of(out_ref, at + i, orbitals)
-    else:
-        put_messages(project(out_ref, proj_ref, orbitals), kb_ref, own_out, mate_out)
+
+
+def first_kernel(
+    place_ref, slab_ref, mate_ref, far_ref, proj_ref, own_msg, far_msg, beyond_msg, kb_ref,
+    out_ref, own_out, mate_out, sums_ref, nonlocal_ref, *, orbitals, scale,
+):
+    sums = atom_sums(own_msg[...], far_msg[:orbitals, :], beyond_msg[:orbitals, :])
+    sums_ref[...] = sums
+    add_rest(out_ref, slab_ref, mate_ref, far_ref, proj_ref, sums, nonlocal_ref, place_ref[0], scale, orbitals)
+    put_messages(project(out_ref, proj_ref, orbitals), kb_ref, own_out, mate_out)
+    lane = lanes(sums.shape)
+    own_out[...] = jnp.where(lane < 6 * OWNED, own_out[...], jnp.where(lane < 7 * OWNED, pltpu.roll(sums, 6 * OWNED, 1), 0.0))
+
+
+def far_first_kernel(
+    place_ref, slab_ref, mate_ref, psi_ref, proj_ref, sums_ref, far_msg, out_ref, nonlocal_ref, *, orbitals, scale
+):
+    sums, far = sums_ref[...], far_msg[...]
+    lane = lanes(sums.shape)
+    far_sums = jnp.where(
+        lane < OWNED, shift(far, 6 * OWNED), jnp.where(lane < 2 * OWNED, shift(sums, OWNED), pltpu.roll(sums, OWNED, 1))
+    )
+    add_rest(out_ref, slab_ref, mate_ref, psi_ref, proj_ref, far_sums, nonlocal_ref, 1 - place_ref[0], scale, orbitals)
+
+
+def second_kernel(
+    place_ref, slab_ref, mate_ref, far_ref, proj_ref, own_msg, far_msg, beyond_msg, out_ref, *rest, orbitals, scale
+):
+    *chunk_refs, nonlocal_ref = rest
+    coeff = atom_sums(own_msg[...], far_msg[...], beyond_msg[...])
+    add_rest(out_ref, slab_ref, mate_ref, far_ref, proj_ref, coeff, nonlocal_ref, place_ref[0], scale, orbitals)
+    share = ROWS // len(chunk_refs)
+    for m, chunk_ref in enumerate(chunk_refs):
+        at = (place_ref[1] ^ m) * share
+        for i in range(share):
+            chunk_ref[i] = row_of(out_ref, at + i, orbitals)
 
 
 def gram_kernel(place_ref, *refs, orbitals, width, scale):
@@ -264,56 +325,75 @@
     kb = jnp.pad(kb, ((0, 0), (KAM, 0))) + jnp.zeros((1, KAM + OWNED), F32)
     kb = jnp.pad(jnp.concatenate([kb, kb[:, 2 * OWNED :]], axis=1), ((0, 0), (0, NX - 6 * OWNED)))
 
-    def slab(field, scale, back, *start):
+    def kernel(body, name, outs, scratch, mib, *operands, scalars=True, **statics):
         return pl.pallas_call(
-            functools.partial(slab_kernel, orbitals=orbitals, scale=scale, back=back),
-            out_shape=field_shape,
-            in_specs=[VMEM] * (2 + len(start)),
-            out_specs=VMEM,
-            scratch_shapes=[pltpu.VMEM((ROWS, NX), F32)],
-            compiler_params=params(8),
-            cost_estimate=pl.CostEstimate(flops=10**8, bytes_accessed=10**7, transcendentals=0),
-            name="slab",
-        )(field, v, *start)
-
-    def finish(operands, outs, scale, last):
-        return pl.pallas_call(
-            functools.partial(finish_kernel, orbitals=orbitals, scale=scale, last=last),
-            out_shape=(field_shape, *outs),
-            in_specs=[SMEM] + [VMEM] * len(operands),
-            out_specs=(VMEM,) * (1 + len(outs)),
-            scratch_shapes=[pltpu.VMEM((orbitals * ROWS, NX), F32)],
-            compiler_params=params(16),
-            cost_estimate=pl.CostEstimate(flops=10**8, bytes_accessed=10**7, transcendentals=0),
-            name="finish",
-        )(place, *operands)
-
-    def stage(field, proj, own, to_mate, scale, back, *start):
-        far = swap(field, fars)
-        mate = swap(field, mates)
-        own = own + swap(to_mate, mates)
-        from_far = swap(own, fars)
-        field, own = lax.optimization_barrier((field, own))
-        local = slab(field, scale, back, *start)
-        return local, mate, far, proj, own, from_far, swap(from_far, mates)
-
-    proj, own, to_mate = pl.pallas_call(
-        functools.partial(projector_kernel, orbitals=orbitals),
-        out_shape=(jax.ShapeDtypeStruct((ROWS, 3 * KAM, NX), BF16), message_shape, message_shape),
-        in_specs=[SMEM] + [VMEM] * 4,
-        out_specs=(VMEM,) * 3,
-        scratch_shapes=[pltpu.VMEM((2, ROWS * OWNED, SLOTS * PTS), BF16)],
-        compiler_params=params(16),
-        cost_estimate=pl.CostEstimate(flops=10**8, bytes_accessed=10**7, transcendentals=0),
-        name="projectors",
-    )(place, proj_index, proj_value.reshape(3, OWNED, PTS), kb, psi)
-    scale = SIGMA / HALF_WIDTH
-    operands = stage(psi, proj, own, to_mate, scale, None)
-    first, own, to_mate = finish((*operands, kb), (message_shape,) * 2, scale, False)
-    scale = 2.0 * SIGMA_TWO / HALF_WIDTH
-    operands = stage(first, proj, own, to_mate, scale, -SIGMA * SIGMA_TWO, psi)
+            functools.partial(body, **statics),
+            out_shape=outs,
+            in_specs=[SMEM] * scalars + [VMEM] * len(operands),
+            out_specs=jax.tree.map(lambda _: VMEM, outs),
+            scratch_shapes=scratch,
+            compiler_params=params(mib),
+            cost_estimate=pl.CostEstimate(flops=10**9, bytes_accessed=10**7, transcendentals=0),
+            name=name,
+        )(*([place] * scalars), *operands)
+
+    field_scratch = pltpu.VMEM((orbitals * ROWS, NX), F32)
+    proj_shape = jax.ShapeDtypeStruct((ROWS, 3 * KAM, NX), BF16)
+    proj_scratch = [pltpu.VMEM((2, ROWS * OWNED, SLOTS * PTS), BF16)]
+
+    def slab(field, potential, scale, back, *start):
+        scratch = [pltpu.VMEM((ROWS, NX), F32), field_scratch]
+        return kernel(
+            slab_kernel, "slab", field_shape, scratch, 8, field, potential, *start,
+            scalars=False, orbitals=orbitals, scale=scale, back=back,
+        )
+
+    first_scale, scale = SIGMA / HALF_WIDTH, 2.0 * SIGMA_TWO / HALF_WIDTH
+    far = swap(psi, fars)
+    mate = swap(psi, mates)
+    proj, own, to_mate = kernel(
+        projector_kernel, "projectors", (proj_shape, message_shape, message_shape), proj_scratch, 16,
+        proj_index, proj_value, kb, psi, orbitals=orbitals,
+    )
+    own = own + swap(to_mate, mates)
+    values = proj_value.reshape(3 * OWNED, PTS)
+    indices = proj_index.astype(F32).reshape(3 * SLOTS, PTS)
+    value_at = orbitals + ROWS
+    index_at = value_at + 3 * OWNED
+    message = jnp.concatenate([own, v, values, indices], axis=0)
+    from_far = swap(message, fars)
+    message, field = lax.optimization_barrier((message, psi))
+    local = slab(field, v, first_scale, None)
+    local, mate = lax.optimization_barrier((local, mate))
+    far_mate = swap(mate, fars)
+    from_far, local = lax.optimization_barrier((from_far, local))
+    from_beyond = swap(from_far, mates)
+    first, own, to_mate, sums = kernel(
+        first_kernel, "first", (field_shape, message_shape, message_shape, message_shape), [field_scratch], 16,
+        local, mate, far, proj, message[:orbitals], from_far, from_beyond, kb, orbitals=orbitals, scale=first_scale,
+    )
+    first_mate = swap(first, mates)
+    own = own + swap(to_mate, mates)
+    far_again = swap(own, fars)
+    own, from_far, far, first = lax.optimization_barrier((own, from_far, far, first))
+    far_proj = kernel(
+        far_projector_kernel, "far_projectors", proj_shape, proj_scratch, 16, from_far,
+        index_at=index_at, value_at=value_at,
+    )
+    far_local = slab(far, from_far[orbitals:value_at], first_scale, None)
+    far_again, far_proj, far_local = lax.optimization_barrier((far_again, far_proj, far_local))
+    beyond_again = swap(far_again, mates)
+    first, far_mate = lax.optimization_barrier((first, far_mate))
+    local = slab(first, v, scale, -SIGMA * SIGMA_TWO, psi)
+    first_far = kernel(
+        far_first_kernel, "far_first", field_shape, [field_scratch], 16,
+        far_local, far_mate, psi, far_proj, sums, far_again, orbitals=orbitals, scale=first_scale,
+    )
     chunk = jax.ShapeDtypeStruct((ROWS // groups, orbitals, NX), F32)
-    filtered, *blocks = finish(operands, (chunk,) * groups, scale, True)
+    filtered, *blocks = kernel(
+        second_kernel, "second", (field_shape,) + (chunk,) * groups, [field_scratch], 16,
+        local, first_mate, first_far, proj, own, far_again, beyond_again, orbitals=orbitals, scale=scale,
+    )
     for m in reversed(range(1, groups)):
         blocks[m] = lax.ppermute(blocks[m], "orb", [(i, i ^ m) for i in range(groups)])
     tiles = pl.pallas_call(

time: 123 us -> 108 us (0.88)
  starting transfers between devices: 49.5 us -> 37.6 us
  waiting for transfers between devices: 23.1 us -> 16.8 us
  blocking collectives: 22.6 us -> 24.9 us
  Pallas kernels: 21.7 us -> 23.2 us
    ppermute x10, starting transfers between devices: 46 us -> 34.1 us  [swap(): return lax.ppermute(x, 'grid', pairs)]
    ppermute x10, waiting for transfers between devices: 10.8 us -> 3.91 us  [swap(): return lax.ppermute(x, 'grid', pairs)]
    all_to_all x1, blocking collectives: 22.6 us -> 24.9 us  [on_device(): tiles = lax.all_to_all(tiles, ('grid', 'orb'), 0, 0, tiled=True)]
    pallas_call x5 -> x8, Pallas kernels: 20.5 us -> 22 us  [kernel(): pl.pallas_call(functools.partial(body, **statics), out_shape=outs, in_spe...]
  transfers between devices with their start and end apart: 13 -> 13, of which waited for: 6 -> 6; matrix products, arithmetic and copies ran while one was open for 1% -> 1% of each run, Pallas kernels for 11% -> 17%
where the time goes in v4:
time: 108 us
  starting transfers between devices  37.6 us (35%)
  blocking collectives  24.9 us (23%)
  Pallas kernels  23.2 us (21%)
  waiting for transfers between devices  16.8 us (16%)
  local copies, waits for them, and re-layouts  4.15 us (4%)
    ppermute x10, starting transfers between devices, swap(): return lax.ppermute(x, 'grid', pairs)  34.1 us
    all_to_all x1, blocking collectives, on_device(): tiles = lax.all_to_all(tiles, ('grid', 'orb'), 0, 0, tiled=True)  24.9 us
    pallas_call x8, Pallas kernels, kernel(): pl.pallas_call(functools.partial(body, **statics), out_shape=outs, in_spe...  22 us
    ppermute x3, waiting for transfers between devices, on_device(): lax.ppermute(blocks[m], 'orb', [(i, i ^ m) for i in range(groups)])  12.9 us
    ppermute x10, waiting for transfers between devices, swap(): return lax.ppermute(x, 'grid', pairs)  3.91 us
    ppermute x3, starting transfers between devices, on_device(): lax.ppermute(blocks[m], 'orb', [(i, i ^ m) for i in range(groups)])  3.55 us
    unnamed x12, local copies, waits for them, and re-layouts  2.57 us
  transfers between devices with their start and end apart: 13, of which 6 were waited for; matrix products, arithmetic and copies ran while one was open for 1% of the time, Pallas kernels for 17%

profile of v4, /device:TPU:1, one launch (start us, length us, event | category | flops | bytes accessed | tf_op | source)
XLA Modules:
  0.0 107.9 jit_solution(15893306767971298594)
XLA Ops:
  0.6 3.3 %collective-permute-start.2 = (f32[1536,128]{1,0:T(8,128)}, f32[1536,128]{1,0:T(8,128)S(1)}, u32[]{:S(2)}, u32[]{:S(2)}) collective-permute-start(f32[1536,128]{1,0:T(8,128)} %bitcast.11), channel_id=1, source_target_pairs={{0,4},{4,0},{8,12},{12,8},{16,20},{20,16},{24,28},{28,24},{32,36},... | collective-permute-start | bytes 2359304 | tf_op jit(solution)/shard_map/ppermute | solution.py:317
  4.0 0.8 reshape.35
  5.0 1.1 %copy-done = f32[32,6,8,128]{3,2,1,0:T(8,128)S(1)} copy-done((f32[32,6,8,128]{3,2,1,0:T(8,128)S(1)}, f32[32,6,8,128]{3,2,1,0:T(8,128)}, u32[]{:S(2)}) %copy-start) | copy-done | bytes 786456
  6.2 0.7 copy-done.2
  6.9 0.7 copy-done.5
  7.6 3.7 %projectors.1 = (bf16[48,144,128]{2,1,0:T(8,128)(2,1)S(1)}, f32[32,128]{1,0:T(8,128)S(1)}, f32[32,128]{1,0:T(8,128)S(1)}) custom-call(s32[2]{0:T(128)S(1)} %pad_add_fusion.place_ref, s32[3,4,128]{2,1,0:T(4,128)S(1)} %copy-done.5, f32[3,4,4,128]{3,2,1,0:T(4,128)S(1)} %copy-done.2, f32[1,128]{1,0:T(1,128)S(1)} %fusion.kb_ref, f32[1536,128]{1,0:T(8,128)S(1)} %bitcast.13), custom_call_target="tpu_custom_call" | custom-call | flops 1000000000 | bytes 10000000 | tf_op jit(solution)/shard_map/projectors/pallas_call | solution.py:329
  11.3 10.3 %collective-permute-start = (f32[32,128]{1,0:T(8,128)S(1)}, f32[32,128]{1,0:T(8,128)S(1)}, u32[]{:S(2)}, u32[]{:S(2)}) collective-permute-start(f32[32,128]{1,0:T(8,128)S(1)} %get-tuple-element.30), channel_id=1, source_target_pairs={{0,4},{4,0},{8,12},{12,8},{16,20},{20,16},{24,28},{28,24},{32,36},... | collective-permute-start | bytes 49160 | tf_op jit(solution)/shard_map/ppermute | solution.py:317
  21.7 0.8 collective-permute-done
  22.6 1.6 %slab.3.slab_ref = f32[1536,128]{1,0:T(8,128)S(1)} custom-call(f32[1536,128]{1,0:T(8,128)S(1)} %bitcast.14, f32[48,128]{1,0:T(8,128)S(1)} %bitcast.20), custom_call_target="tpu_custom_call" | custom-call | flops 1000000000 | bytes 10000000 | tf_op jit(solution)/shard_map/slab/pallas_call | solution.py:329
  24.2 1.8 %collective-permute-start.6 = (f32[1536,128]{1,0:T(8,128)S(1)}, f32[1536,128]{1,0:T(8,128)S(1)}, u32[]{:S(2)}, u32[]{:S(2)}) collective-permute-start(f32[1536,128]{1,0:T(8,128)S(1)} %collective-permute-done.2.mate_ref), channel_id=1, source_target_pairs={{0,252},{4,8},{8,4},{12,16},{16,12},{20,24},{24,20},{28,32},{32,28... | collective-permute-start | bytes 2359304 | tf_op jit(solution)/shard_map/ppermute | solution.py:317
  26.0 0.4 collective-permute-done.1.far_msg.message_ref
  26.4 11.2 %collective-permute-start.4 = (f32[140,128]{1,0:T(8,128)S(1)}, f32[140,128]{1,0:T(8,128)S(1)}, u32[]{:S(2)}, u32[]{:S(2)}) collective-permute-start(f32[140,128]{1,0:T(8,128)S(1)} %collective-permute-done.1.far_msg.message_ref), channel_id=1, source_target_pairs={{0,4},{4,0},{8,12},{12,8},{16,20},{20,16},{24,28},{28,24},{32,36},... | collective-permute-start | bytes 215048 | tf_op jit(solution)/shard_map/ppermute | solution.py:317
  37.6 0.9 collective-permute-done.4.beyond_msg
  38.5 4.3 %first.1 = (f32[1536,128]{1,0:T(8,128)S(1)}, f32[32,128]{1,0:T(8,128)S(1)}, f32[32,128]{1,0:T(8,128)S(1)}, f32[32,128]{1,0:T(8,128)S(1)}) custom-call(s32[2]{0:T(128)S(1)} %pad_add_fusion.place_ref, f32[1536,128]{1,0:T(8,128)S(1)} %slab.3.slab_ref, f32[1536,128]{1,0:T(8,128)S(1)} %collective-permute-done.2.mate_ref, ...), custom_call_target="tpu_custom_call" | custom-call | flops 1000000000 | bytes 10000000 | tf_op jit(solution)/shard_map/first/pallas_call | solution.py:329
  42.7 0.4 collective-permute-start.7
  43.2 0.2 collective-permute-start.5
  43.3 1.8 %collective-permute-done.5 = f32[32,128]{1,0:T(8,128)S(1)} collective-permute-done((f32[32,128]{1,0:T(8,128)S(1)}, f32[32,128]{1,0:T(8,128)S(1)}, u32[]{:S(2)}, u32[]{:S(2)}) %collective-permute-start.5) | collective-permute-done | bytes 16416 | tf_op jit(solution)/shard_map/ppermute | solution.py:317
  45.1 2.3 %far_projectors.1.proj_ref = bf16[48,144,128]{2,1,0:T(8,128)(2,1)S(1)} custom-call(s32[2]{0:T(128)S(1)} %pad_add_fusion.place_ref, f32[140,128]{1,0:T(8,128)S(1)} %collective-permute-done.1.far_msg.message_ref), custom_call_target="tpu_custom_call" | custom-call | flops 1000000000 | bytes 10000000 | tf_op jit(solution)/shard_map/far_projectors/pallas_call | solution.py:329
  47.5 2.7 %slab.5.slab_ref = f32[1536,128]{1,0:T(8,128)S(1)} custom-call(f32[1536,128]{1,0:T(8,128)} %collective-permute-done.3.far_ref.field_ref, f32[48,128]{1,0:T(8,128)S(1)} %slice.22.v_ref), custom_call_target="tpu_custom_call" | custom-call | flops 1000000000 | bytes 10000000 | tf_op jit(solution)/shard_map/slab/pallas_call | solution.py:329
  50.2 6.8 %collective-permute-start.9 = (f32[32,128]{1,0:T(8,128)S(1)}, f32[32,128]{1,0:T(8,128)S(1)}, u32[]{:S(2)}, u32[]{:S(2)}) collective-permute-start(f32[32,128]{1,0:T(8,128)S(1)} %collective-permute-done.8.far_msg), channel_id=1, source_target_pairs={{0,4},{4,0},{8,12},{12,8},{16,20},{20,16},{24,28},{28,24},{32,36},... | collective-permute-start | bytes 49160 | tf_op jit(solution)/shard_map/ppermute | solution.py:317
  57.0 1.7 %slab.4.slab_ref = f32[1536,128]{1,0:T(8,128)S(1)} custom-call(f32[1536,128]{1,0:T(8,128)S(1)} %get-tuple-element.42.field_ref, f32[48,128]{1,0:T(8,128)S(1)} %bitcast.21, f32[1536,128]{1,0:T(8,128)S(1)} %bitcast.15), custom_call_target="tpu_custom_call" | custom-call | flops 1000000000 | bytes 10000000 | tf_op jit(solution)/shard_map/slab/pallas_call | solution.py:329
  58.7 2.3 %far_first.1.far_ref = f32[1536,128]{1,0:T(8,128)S(1)} custom-call(s32[2]{0:T(128)S(1)} %pad_add_fusion.place_ref, f32[1536,128]{1,0:T(8,128)S(1)} %slab.5.slab_ref, f32[1536,128]{1,0:T(8,128)S(1)} %collective-permute-done.6.mate_ref, f32[1536,128]{1,0:T(8,128)S(1)} %bitcast.16, bf16[48,144,128]{2,1,0:T(8,128)(2,1)S(1)} %far_projectors.1.proj_ref, ...), custom_call_target="tpu_custom_call" | custom-call | flops 1000000000 | bytes 10000000 | tf_op jit(solution)/shard_map/far_first/pallas_call | solution.py:329
  61.0 3.4 %second.1 = (f32[1536,128]{1,0:T(8,128)}, f32[12,32,128]{2,1,0:T(8,128)S(1)}, f32[12,32,128]{2,1,0:T(8,128)S(1)}, f32[12,32,128]{2,1,0:T(8,128)S(1)}, f32[12,32,128]{2,1,0:T(8,128)S(1)}) custom-call(s32[2]{0:T(128)S(1)} %pad_add_fusion.place_ref, f32[1536,128]{1,0:T(8,128)S(1)} %slab.4.slab_ref, f32[1536,128]{1,0:T(8,128)S(1)} %collective-permute-done.7.mate_ref, ...), custom_call_target="tpu_custom_call" | custom-call | flops 1000000000 | bytes 10000000 | tf_op jit(solution)/shard_map/second/pallas_call | solution.py:329
  64.4 0.8 collective-permute-start.10
  65.3 0.8 collective-permute-start.11
  66.0 2.0 %collective-permute-start.12 = (f32[12,32,128]{2,1,0:T(8,128)S(1)}, f32[12,32,128]{2,1,0:T(8,128)S(1)}, u32[]{:S(2)}, u32[]{:S(2)}) collective-permute-start(f32[12,32,128]{2,1,0:T(8,128)S(1)} %get-tuple-element.55), channel_id=1, source_target_pairs={{0,3},{1,2},{2,1},{3,0},{4,7},{5,6},{6,5},{7,4},{8,11},{9,10},{10,... | collective-permute-start | bytes 589832 | tf_op jit(solution)/shard_map/ppermute | solution.py:398
  68.0 5.3 %collective-permute-done.10.refs_1_ = f32[12,32,128]{2,1,0:T(8,128)S(1)} collective-permute-done((f32[12,32,128]{2,1,0:T(8,128)S(1)}, f32[12,32,128]{2,1,0:T(8,128)S(1)}, u32[]{:S(2)}, u32[]{:S(2)}) %collective-permute-start.10) | collective-permute-done | bytes 196640 | tf_op jit(solution)/shard_map/ppermute | solution.py:398
  73.3 7.5 %collective-permute-done.11.refs_2_ = f32[12,32,128]{2,1,0:T(8,128)S(1)} collective-permute-done((f32[12,32,128]{2,1,0:T(8,128)S(1)}, f32[12,32,128]{2,1,0:T(8,128)S(1)}, u32[]{:S(2)}, u32[]{:S(2)}) %collective-permute-start.11) | collective-permute-done | bytes 196640 | tf_op jit(solution)/shard_map/ppermute | solution.py:398
  80.8 1.2 %gram.1 = f32[256,128]{1,0:T(8,128)S(1)} custom-call(s32[2]{0:T(128)S(1)} %pad_add_fusion.place_ref, f32[12,32,128]{2,1,0:T(8,128)S(1)} %get-tuple-element.52.refs_0_, f32[12,32,128]{2,1,0:T(8,128)S(1)} %collective-permute-done.10.refs_1_, f32[12,32,128]{2,1,0:T(8,128)S(1)} %collective-permute-done.11.refs_2_, f32[12,32,128]{2,1,0:T(8,128)S(1)} %collective-permute-done.12.refs_3_), custom_call_target="tpu_custom_call" | custom-call | flops 100000000 | bytes 1000000 | tf_op jit(solution)/shard_map/gram/pallas_call | solution.py:399
  82.0 24.9 %all_to_all.9 = f32[256,1,128]{2,1,0:T(1,128)S(1)} all-to-all(f32[256,1,128]{2,1,0:T(1,128)S(1)} %bitcast.17), channel_id=1, replica_groups=mesh['grid'=64,'orb'=4] {'grid','orb'}, dimensions={0} | all-to-all | bytes 262144 | tf_op jit(solution)/shard_map/all_to_all | solution.py:409
  106.9 0.3 reduce_sum.9
  107.2 0.6 reshape.41
  (30 shorter events, 0.5 us)
Async XLA Ops:
  0.6 23.6 %collective-permute-start.2 = (f32[1536,128]{1,0:T(8,128)}, f32[1536,128]{1,0:T(8,128)S(1)}, u32[]{:S(2)}, u32[]{:S(2)}) collective-permute-start(f32[1536,128]{1,0:T(8,128)} %bitcast.11), channel_id=1, source_target_pairs={{0,4},{4,0},{8,12},{12,8},{16,20},{20,16},{24,28},{28,24},{32,36},... | collective-permute-start | bytes 2359304 | tf_op jit(solution)/shard_map/ppermute | solution.py:317
  4.0 33.6 %collective-permute-start.3 = (f32[1536,128]{1,0:T(8,128)}, f32[1536,128]{1,0:T(8,128)}, u32[]{:S(2)}, u32[]{:S(2)}) collective-permute-start(f32[1536,128]{1,0:T(8,128)} %bitcast.12), channel_id=1, source_target_pairs={{0,252},{4,8},{8,4},{12,16},{16,12},{20,24},{24,20},{28,32},{32,28... | collective-permute-start | bytes 2359304 | tf_op jit(solution)/shard_map/ppermute | solution.py:317
  5.0 1.1 %copy-start = (f32[32,6,8,128]{3,2,1,0:T(8,128)S(1)}, f32[32,6,8,128]{3,2,1,0:T(8,128)}, u32[]{:S(2)}) copy-start(f32[32,6,8,128]{3,2,1,0:T(8,128)} %param.5) | copy-start | bytes 2359300
  6.2 0.7 copy-start.2
  6.9 0.7 copy-start.5
  7.6 14.9 %copy-start.3 = (f32[3,4,4,128]{3,2,1,0:T(4,128)S(1)}, f32[3,4,4,128]{3,2,1,0:T(4,128)}, u32[]{:S(2)}) copy-start(f32[3,4,4,128]{3,2,1,0:T(4,128)} %value_ref.1) | copy-start | bytes 73732
  7.6 14.9 %copy-start.4 = (f32[6,8,128]{2,1,0:T(8,128)S(1)}, f32[6,8,128]{2,1,0:T(8,128)}, u32[]{:S(2)}) copy-start(f32[6,8,128]{2,1,0:T(8,128)} %param.6) | copy-start | bytes 73732
  7.6 15.0 %copy-start.1 = (f32[32,6,8,128]{3,2,1,0:T(8,128)S(1)}, f32[32,6,8,128]{3,2,1,0:T(8,128)}, u32[]{:S(2)}) copy-start(f32[32,6,8,128]{3,2,1,0:T(8,128)} %param.5) | copy-start | bytes 2359300
  11.3 11.1 %collective-permute-start = (f32[32,128]{1,0:T(8,128)S(1)}, f32[32,128]{1,0:T(8,128)S(1)}, u32[]{:S(2)}, u32[]{:S(2)}) collective-permute-start(f32[32,128]{1,0:T(8,128)S(1)} %get-tuple-element.30), channel_id=1, source_target_pairs={{0,4},{4,0},{8,12},{12,8},{16,20},{20,16},{24,28},{28,24},{32,36},... | collective-permute-start | bytes 49160 | tf_op jit(solution)/shard_map/ppermute | solution.py:317
  22.5 3.9 %collective-permute-start.1 = (f32[140,128]{1,0:T(8,128)S(1)}, f32[140,128]{1,0:T(8,128)S(1)}, u32[]{:S(2)}, u32[]{:S(2)}) collective-permute-start(f32[140,128]{1,0:T(8,128)S(1)} %pad_maximum_fusion), channel_id=1, source_target_pairs={{0,252},{4,8},{8,4},{12,16},{16,12},{20,24},{24,20},{28,32},{32,28... | collective-permute-start | bytes 215048 | tf_op jit(solution)/shard_map/ppermute | solution.py:317
  24.2 32.8 %collective-permute-start.6 = (f32[1536,128]{1,0:T(8,128)S(1)}, f32[1536,128]{1,0:T(8,128)S(1)}, u32[]{:S(2)}, u32[]{:S(2)}) collective-permute-start(f32[1536,128]{1,0:T(8,128)S(1)} %collective-permute-done.2.mate_ref), channel_id=1, source_target_pairs={{0,252},{4,8},{8,4},{12,16},{16,12},{20,24},{24,20},{28,32},{32,28... | collective-permute-start | bytes 2359304 | tf_op jit(solution)/shard_map/ppermute | solution.py:317
  26.4 12.1 %collective-permute-start.4 = (f32[140,128]{1,0:T(8,128)S(1)}, f32[140,128]{1,0:T(8,128)S(1)}, u32[]{:S(2)}, u32[]{:S(2)}) collective-permute-start(f32[140,128]{1,0:T(8,128)S(1)} %collective-permute-done.1.far_msg.message_ref), channel_id=1, source_target_pairs={{0,4},{4,0},{8,12},{12,8},{16,20},{20,16},{24,28},{28,24},{32,36},... | collective-permute-start | bytes 215048 | tf_op jit(solution)/shard_map/ppermute | solution.py:317
  42.7 18.3 %collective-permute-start.7 = (f32[1536,128]{1,0:T(8,128)S(1)}, f32[1536,128]{1,0:T(8,128)S(1)}, u32[]{:S(2)}, u32[]{:S(2)}) collective-permute-start(f32[1536,128]{1,0:T(8,128)S(1)} %get-tuple-element.42.field_ref), channel_id=1, source_target_pairs={{0,4},{4,0},{8,12},{12,8},{16,20},{20,16},{24,28},{28,24},{32,36},... | collective-permute-start | bytes 2359304 | tf_op jit(solution)/shard_map/ppermute | solution.py:317
  43.2 2.0 %collective-permute-start.5 = (f32[32,128]{1,0:T(8,128)S(1)}, f32[32,128]{1,0:T(8,128)S(1)}, u32[]{:S(2)}, u32[]{:S(2)}) collective-permute-start(f32[32,128]{1,0:T(8,128)S(1)} %get-tuple-element.39), channel_id=1, source_target_pairs={{0,4},{4,0},{8,12},{12,8},{16,20},{20,16},{24,28},{28,24},{32,36},... | collective-permute-start | bytes 49160 | tf_op jit(solution)/shard_map/ppermute | solution.py:317
  45.1 5.1 %collective-permute-start.8 = (f32[32,128]{1,0:T(8,128)S(1)}, f32[32,128]{1,0:T(8,128)S(1)}, u32[]{:S(2)}, u32[]{:S(2)}) collective-permute-start(f32[32,128]{1,0:T(8,128)S(1)} %add.16.own_msg), channel_id=1, source_target_pairs={{0,252},{4,8},{8,4},{12,16},{16,12},{20,24},{24,20},{28,32},{32,28... | collective-permute-start | bytes 49160 | tf_op jit(solution)/shard_map/ppermute | solution.py:317
  50.2 10.8 %collective-permute-start.9 = (f32[32,128]{1,0:T(8,128)S(1)}, f32[32,128]{1,0:T(8,128)S(1)}, u32[]{:S(2)}, u32[]{:S(2)}) collective-permute-start(f32[32,128]{1,0:T(8,128)S(1)} %collective-permute-done.8.far_msg), channel_id=1, source_target_pairs={{0,4},{4,0},{8,12},{12,8},{16,20},{20,16},{24,28},{28,24},{32,36},... | collective-permute-start | bytes 49160 | tf_op jit(solution)/shard_map/ppermute | solution.py:317
  64.4 8.9 %collective-permute-start.10 = (f32[12,32,128]{2,1,0:T(8,128)S(1)}, f32[12,32,128]{2,1,0:T(8,128)S(1)}, u32[]{:S(2)}, u32[]{:S(2)}) collective-permute-start(f32[12,32,128]{2,1,0:T(8,128)S(1)} %get-tuple-element.53), channel_id=1, source_target_pairs={{0,1},{1,0},{2,3},{3,2},{4,5},{5,4},{6,7},{7,6},{8,9},{9,8},{10,11... | collective-permute-start | bytes 589832 | tf_op jit(solution)/shard_map/ppermute | solution.py:398
  65.3 15.6 %collective-permute-start.11 = (f32[12,32,128]{2,1,0:T(8,128)S(1)}, f32[12,32,128]{2,1,0:T(8,128)S(1)}, u32[]{:S(2)}, u32[]{:S(2)}) collective-permute-start(f32[12,32,128]{2,1,0:T(8,128)S(1)} %get-tuple-element.54), channel_id=1, source_target_pairs={{0,2},{1,3},{2,0},{3,1},{4,6},{5,7},{6,4},{7,5},{8,10},{9,11},{10,... | collective-permute-start | bytes 589832 | tf_op jit(solution)/shard_map/ppermute | solution.py:398
  66.0 14.8 %collective-permute-start.12 = (f32[12,32,128]{2,1,0:T(8,128)S(1)}, f32[12,32,128]{2,1,0:T(8,128)S(1)}, u32[]{:S(2)}, u32[]{:S(2)}) collective-permute-start(f32[12,32,128]{2,1,0:T(8,128)S(1)} %get-tuple-element.55), channel_id=1, source_target_pairs={{0,3},{1,2},{2,1},{3,0},{4,7},{5,6},{6,5},{7,4},{8,11},{9,10},{10,... | collective-permute-start | bytes 589832 | tf_op jit(solution)/shard_map/ppermute | solution.py:398

commit v5 on v4

--- a/solution.py
+++ b/solution.py
@@ -35,6 +35,7 @@
 BF16 = jnp.bfloat16
 VMEM = pl.BlockSpec(memory_space=pltpu.VMEM)
 SMEM = pl.BlockSpec(memory_space=pltpu.SMEM)
+ANY = pl.BlockSpec(memory_space=pl.ANY)
 
 
 def two_parts(x):
@@ -204,7 +205,9 @@
     return jnp.where(lane < KAM, sums * energy, 0.0)
 
 
-def add_rest(out_ref, slab_ref, mate_ref, far_ref, proj_ref, coeff, nonlocal_ref, odd, scale, orbitals):
+def add_rest(
+    out_ref, slab_ref, mate_ref, far_ref, proj_ref, coeff, nonlocal_ref, odd, scale, orbitals, until_here=None
+):
     head, tail = two_parts((coeff * scale)[:, :KAM])
     lhs = jnp.concatenate([head, head, tail], axis=1)
 
@@ -217,6 +220,8 @@
         return carry
 
     lax.fori_loop(0, ROWS // 2, spread, 0, unroll=4)
+    if until_here is not None:
+        until_here()
     c = weights(scale)
     place = places(odd)
 
@@ -242,12 +247,16 @@
 
 
 def first_kernel(
-    place_ref, slab_ref, mate_ref, far_ref, proj_ref, own_msg, far_msg, beyond_msg, kb_ref,
-    out_ref, own_out, mate_out, sums_ref, nonlocal_ref, *, orbitals, scale,
+    place_ref, slab_ref, mate_ref, far_arrived, proj_ref, own_msg, far_msg, beyond_msg, kb_ref,
+    out_ref, own_out, mate_out, sums_ref, far_ref, nonlocal_ref, arrival, *, orbitals, scale,
 ):
+    fetch = pltpu.make_async_copy(far_arrived, far_ref, arrival)
+    fetch.start()
     sums = atom_sums(own_msg[...], far_msg[:orbitals, :], beyond_msg[:orbitals, :])
     sums_ref[...] = sums
-    add_rest(out_ref, slab_ref, mate_ref, far_ref, proj_ref, sums, nonlocal_ref, place_ref[0], scale, orbitals)
+    add_rest(
+        out_ref, slab_ref, mate_ref, far_ref, proj_ref, sums, nonlocal_ref, place_ref[0], scale, orbitals, fetch.wait
+    )
     put_messages(project(out_ref, proj_ref, orbitals), kb_ref, own_out, mate_out)
     lane = lanes(sums.shape)
     own_out[...] = jnp.where(lane < 6 * OWNED, own_out[...], jnp.where(lane < 7 * OWNED, pltpu.roll(sums, 6 * OWNED, 1), 0.0))
@@ -325,15 +334,15 @@
     kb = jnp.pad(kb, ((0, 0), (KAM, 0))) + jnp.zeros((1, KAM + OWNED), F32)
     kb = jnp.pad(jnp.concatenate([kb, kb[:, 2 * OWNED :]], axis=1), ((0, 0), (0, NX - 6 * OWNED)))
 
-    def kernel(body, name, outs, scratch, mib, *operands, scalars=True, **statics):
+    def kernel(body, name, outs, scratch, mib, *operands, scalars=True, left=(), flops=10**9, **statics):
         return pl.pallas_call(
             functools.partial(body, **statics),
             out_shape=outs,
-            in_specs=[SMEM] * scalars + [VMEM] * len(operands),
+            in_specs=[SMEM] * scalars + [ANY if i in left else VMEM for i in range(len(operands))],
             out_specs=jax.tree.map(lambda _: VMEM, outs),
             scratch_shapes=scratch,
             compiler_params=params(mib),
-            cost_estimate=pl.CostEstimate(flops=10**9, bytes_accessed=10**7, transcendentals=0),
+            cost_estimate=pl.CostEstimate(flops=flops, bytes_accessed=10**7, transcendentals=0),
             name=name,
         )(*([place] * scalars), *operands)
 
@@ -368,9 +377,11 @@
     far_mate = swap(mate, fars)
     from_far, local = lax.optimization_barrier((from_far, local))
     from_beyond = swap(from_far, mates)
-    first, own, to_mate, sums = kernel(
-        first_kernel, "first", (field_shape, message_shape, message_shape, message_shape), [field_scratch], 16,
-        local, mate, far, proj, message[:orbitals], from_far, from_beyond, kb, orbitals=orbitals, scale=first_scale,
+    first, own, to_mate, sums, far = kernel(
+        first_kernel, "first", (field_shape, message_shape, message_shape, message_shape, field_shape),
+        [field_scratch, pltpu.SemaphoreType.DMA(())], 16,
+        local, mate, far, proj, message[:orbitals], from_far, from_beyond, kb,
+        left=(2,), orbitals=orbitals, scale=first_scale,
     )
     first_mate = swap(first, mates)
     own = own + swap(to_mate, mates)
@@ -381,13 +392,13 @@
         index_at=index_at, value_at=value_at,
     )
     far_local = slab(far, from_far[orbitals:value_at], first_scale, None)
-    far_again, far_proj, far_local = lax.optimization_barrier((far_again, far_proj, far_local))
+    local = slab(first, v, scale, -SIGMA * SIGMA_TWO, psi)
+    far_again, far_proj, far_local, local = lax.optimization_barrier((far_again, far_proj, far_local, local))
     beyond_again = swap(far_again, mates)
-    first, far_mate = lax.optimization_barrier((first, far_mate))
-    local = slab(first, v, scale, -SIGMA * SIGMA_TWO, psi)
     first_far = kernel(
         far_first_kernel, "far_first", field_shape, [field_scratch], 16,
-        far_local, far_mate, psi, far_proj, sums, far_again, orbitals=orbitals, scale=first_scale,
+        far_local, far_mate, psi, far_proj, sums, far_again, flops=20 * 10**8,
+        orbitals=orbitals, scale=first_scale,
     )
     chunk = jax.ShapeDtypeStruct((ROWS // groups, orbitals, NX), F32)
     filtered, *blocks = kernel(

time: 108 us -> 107 us (level)
  Pallas kernels: 23.2 us -> 21.5 us
  waiting for transfers between devices: 16.8 us -> 15.4 us
  local copies, waits for them, and re-layouts: 4.15 us -> 5.28 us
    pallas_call x8, Pallas kernels: 22 us -> 20.3 us  [kernel(): pl.pallas_call(functools.partial(body, **statics), out_shape=outs, in_spe...]
    unnamed x12 -> x14, local copies, waits for them, and re-layouts: 2.57 us -> 3.7 us
  transfers between devices with their start and end apart: 13 -> 13, of which waited for: 6 -> 5; matrix products, arithmetic and copies ran while one was open for 1% -> 1% of each run, Pallas kernels for 17% -> 16%
where the time goes in v5:
time: 107 us
  starting transfers between devices  37.6 us (35%)
  blocking collectives  25.8 us (24%)
  Pallas kernels  21.5 us (20%)
  waiting for transfers between devices  15.4 us (14%)
  local copies, waits for them, and re-layouts  5.28 us (5%)
    ppermute x10, starting transfers between devices, swap(): return lax.ppermute(x, 'grid', pairs)  34.1 us
    all_to_all x1, blocking collectives, on_device(): tiles = lax.all_to_all(tiles, ('grid', 'orb'), 0, 0, tiled=True)  25.8 us
    pallas_call x8, Pallas kernels, kernel(): pl.pallas_call(functools.partial(body, **statics), out_shape=outs, in_spe...  20.3 us
    ppermute x3, waiting for transfers between devices, on_device(): lax.ppermute(blocks[m], 'orb', [(i, i ^ m) for i in range(groups)])  11.8 us
    unnamed x14, local copies, waits for them, and re-layouts  3.7 us
    ppermute x3, starting transfers between devices, on_device(): lax.ppermute(blocks[m], 'orb', [(i, i ^ m) for i in range(groups)])  3.55 us
    ppermute x10, waiting for transfers between devices, swap(): return lax.ppermute(x, 'grid', pairs)  3.55 us
  transfers between devices with their start and end apart: 13, of which 5 were waited for; matrix products, arithmetic and copies ran while one was open for 1% of the time, Pallas kernels for 16%

profile of v5, /device:TPU:1, one launch (start us, length us, event | category | flops | bytes accessed | tf_op | source)
XLA Modules:
  0.0 106.9 jit_solution(11107335142763128293)
XLA Ops:
  0.6 3.3 %collective-permute-start.2 = (f32[1536,128]{1,0:T(8,128)}, f32[1536,128]{1,0:T(8,128)S(1)}, u32[]{:S(2)}, u32[]{:S(2)}) collective-permute-start(f32[1536,128]{1,0:T(8,128)} %bitcast.16), channel_id=1, source_target_pairs={{0,4},{4,0},{8,12},{12,8},{16,20},{20,16},{24,28},{28,24},{32,36},... | collective-permute-start | bytes 2359304 | tf_op jit(solution)/shard_map/ppermute | solution.py:326
  4.0 0.8 reshape.35
  5.0 0.7 copy-done
  5.8 0.7 copy-done.3
  6.5 1.1 %copy-done.4 = f32[32,6,8,128]{3,2,1,0:T(8,128)S(1)} copy-done((f32[32,6,8,128]{3,2,1,0:T(8,128)S(1)}, f32[32,6,8,128]{3,2,1,0:T(8,128)}, u32[]{:S(2)}) %copy-start.4) | copy-done | bytes 786456
  7.6 3.7 %projectors.1 = (bf16[48,144,128]{2,1,0:T(8,128)(2,1)S(1)}, f32[32,128]{1,0:T(8,128)S(1)}, f32[32,128]{1,0:T(8,128)S(1)}) custom-call(s32[2]{0:T(128)S(1)} %pad_add_fusion.place_ref, s32[3,4,128]{2,1,0:T(4,128)S(1)} %copy-done.3, f32[3,4,4,128]{3,2,1,0:T(4,128)S(1)} %copy-done, f32[1,128]{1,0:T(1,128)S(1)} %fusion.kb_ref, f32[1536,128]{1,0:T(8,128)S(1)} %bitcast.18), custom_call_target="tpu_custom_call" | custom-call | flops 1000000000 | bytes 10000000 | tf_op jit(solution)/shard_map/projectors/pallas_call | solution.py:338
  11.3 10.3 %collective-permute-start = (f32[32,128]{1,0:T(8,128)S(1)}, f32[32,128]{1,0:T(8,128)S(1)}, u32[]{:S(2)}, u32[]{:S(2)}) collective-permute-start(f32[32,128]{1,0:T(8,128)S(1)} %get-tuple-element.30), channel_id=1, source_target_pairs={{0,4},{4,0},{8,12},{12,8},{16,20},{20,16},{24,28},{28,24},{32,36},... | collective-permute-start | bytes 49160 | tf_op jit(solution)/shard_map/ppermute | solution.py:326
  21.7 0.8 collective-permute-done
  22.5 0.1 collective-permute-start.1
  22.6 1.1 %copy-done.5 = f32[32,6,8,128]{3,2,1,0:T(8,128)S(1)} copy-done((f32[32,6,8,128]{3,2,1,0:T(8,128)S(1)}, f32[32,6,8,128]{3,2,1,0:T(8,128)}, u32[]{:S(2)}) %copy-start.5) | copy-done | bytes 786456
  23.7 1.6 %slab.3.slab_ref = f32[1536,128]{1,0:T(8,128)S(1)} custom-call(f32[1536,128]{1,0:T(8,128)S(1)} %bitcast.19, f32[48,128]{1,0:T(8,128)S(1)} %bitcast.14), custom_call_target="tpu_custom_call" | custom-call | flops 1000000000 | bytes 10000000 | tf_op jit(solution)/shard_map/slab/pallas_call | solution.py:338
  25.3 1.8 %collective-permute-start.8 = (f32[1536,128]{1,0:T(8,128)S(1)}, f32[1536,128]{1,0:T(8,128)S(1)}, u32[]{:S(2)}, u32[]{:S(2)}) collective-permute-start(f32[1536,128]{1,0:T(8,128)S(1)} %collective-permute-done.2.mate_ref), channel_id=1, source_target_pairs={{0,252},{4,8},{8,4},{12,16},{16,12},{20,24},{24,20},{28,32},{32,28... | collective-permute-start | bytes 2359304 | tf_op jit(solution)/shard_map/ppermute | solution.py:326
  27.2 10.4 %collective-permute-start.4 = (f32[140,128]{1,0:T(8,128)S(1)}, f32[140,128]{1,0:T(8,128)S(1)}, u32[]{:S(2)}, u32[]{:S(2)}) collective-permute-start(f32[140,128]{1,0:T(8,128)S(1)} %collective-permute-done.1.far_msg.message_ref), channel_id=1, source_target_pairs={{0,4},{4,0},{8,12},{12,8},{16,20},{20,16},{24,28},{28,24},{32,36},... | collective-permute-start | bytes 215048 | tf_op jit(solution)/shard_map/ppermute | solution.py:326
  37.6 0.9 collective-permute-done.4.beyond_msg
  38.5 3.8 %first.1 = (f32[1536,128]{1,0:T(8,128)S(1)}, f32[32,128]{1,0:T(8,128)S(1)}, f32[32,128]{1,0:T(8,128)S(1)}, f32[32,128]{1,0:T(8,128)S(1)}, f32[1536,128]{1,0:T(8,128)S(1)}) custom-call(s32[2]{0:T(128)S(1)} %pad_add_fusion.place_ref, f32[1536,128]{1,0:T(8,128)S(1)} %slab.3.slab_ref, f32[1536,128]{1,0:T(8,128)S(1)} %collective-permute-done.2.mate_ref, ...), custom_call_target="tpu_custom_call" | custom-call | flops 1000000000 | bytes 10000000 | tf_op jit(solution)/shard_map/first/pallas_call | solution.py:338
  42.2 0.4 collective-permute-start.7
  42.7 0.2 collective-permute-start.5
  42.8 1.8 %collective-permute-done.5 = f32[32,128]{1,0:T(8,128)S(1)} collective-permute-done((f32[32,128]{1,0:T(8,128)S(1)}, f32[32,128]{1,0:T(8,128)S(1)}, u32[]{:S(2)}, u32[]{:S(2)}) %collective-permute-start.5) | collective-permute-done | bytes 16416 | tf_op jit(solution)/shard_map/ppermute | solution.py:326
  44.7 2.3 %far_projectors.1.proj_ref = bf16[48,144,128]{2,1,0:T(8,128)(2,1)S(1)} custom-call(s32[2]{0:T(128)S(1)} %pad_add_fusion.place_ref, f32[140,128]{1,0:T(8,128)S(1)} %collective-permute-done.1.far_msg.message_ref), custom_call_target="tpu_custom_call" | custom-call | flops 1000000000 | bytes 10000000 | tf_op jit(solution)/shard_map/far_projectors/pallas_call | solution.py:338
  47.0 1.7 %slab.5.slab_ref = f32[1536,128]{1,0:T(8,128)S(1)} custom-call(f32[1536,128]{1,0:T(8,128)S(1)} %get-tuple-element.44.field_ref, f32[48,128]{1,0:T(8,128)S(1)} %bitcast.15, f32[1536,128]{1,0:T(8,128)S(1)} %bitcast.20), custom_call_target="tpu_custom_call" | custom-call | flops 1000000000 | bytes 10000000 | tf_op jit(solution)/shard_map/slab/pallas_call | solution.py:338
  48.7 1.6 %slab.4.slab_ref = f32[1536,128]{1,0:T(8,128)S(1)} custom-call(f32[1536,128]{1,0:T(8,128)S(1)} %get-tuple-element.43.field_ref, f32[48,128]{1,0:T(8,128)S(1)} %slice.22.v_ref), custom_call_target="tpu_custom_call" | custom-call | flops 1000000000 | bytes 10000000 | tf_op jit(solution)/shard_map/slab/pallas_call | solution.py:338
  50.3 7.6 %collective-permute-start.9 = (f32[32,128]{1,0:T(8,128)S(1)}, f32[32,128]{1,0:T(8,128)S(1)}, u32[]{:S(2)}, u32[]{:S(2)}) collective-permute-start(f32[32,128]{1,0:T(8,128)S(1)} %collective-permute-done.6.far_msg), channel_id=1, source_target_pairs={{0,4},{4,0},{8,12},{12,8},{16,20},{20,16},{24,28},{28,24},{32,36},... | collective-permute-start | bytes 49160 | tf_op jit(solution)/shard_map/ppermute | solution.py:326
  57.8 2.3 %far_first.1.far_ref = f32[1536,128]{1,0:T(8,128)S(1)} custom-call(s32[2]{0:T(128)S(1)} %pad_add_fusion.place_ref, f32[1536,128]{1,0:T(8,128)S(1)} %slab.4.slab_ref, f32[1536,128]{1,0:T(8,128)S(1)} %collective-permute-done.8.mate_ref, f32[1536,128]{1,0:T(8,128)S(1)} %bitcast.21, bf16[48,144,128]{2,1,0:T(8,128)(2,1)S(1)} %far_projectors.1.proj_ref, ...), custom_call_target="tpu_custom_call" | custom-call | flops 2000000000 | bytes 10000000 | tf_op jit(solution)/shard_map/far_first/pallas_call | solution.py:338
  60.1 3.4 %second.1 = (f32[1536,128]{1,0:T(8,128)}, f32[12,32,128]{2,1,0:T(8,128)S(1)}, f32[12,32,128]{2,1,0:T(8,128)S(1)}, f32[12,32,128]{2,1,0:T(8,128)S(1)}, f32[12,32,128]{2,1,0:T(8,128)S(1)}) custom-call(s32[2]{0:T(128)S(1)} %pad_add_fusion.place_ref, f32[1536,128]{1,0:T(8,128)S(1)} %slab.5.slab_ref, f32[1536,128]{1,0:T(8,128)S(1)} %collective-permute-done.7.mate_ref, ...), custom_call_target="tpu_custom_call" | custom-call | flops 1000000000 | bytes 10000000 | tf_op jit(solution)/shard_map/second/pallas_call | solution.py:338
  63.6 1.9 %collective-permute-start.11 = (f32[12,32,128]{2,1,0:T(8,128)S(1)}, f32[12,32,128]{2,1,0:T(8,128)S(1)}, u32[]{:S(2)}, u32[]{:S(2)}) collective-permute-start(f32[12,32,128]{2,1,0:T(8,128)S(1)} %get-tuple-element.54), channel_id=1, source_target_pairs={{0,2},{1,3},{2,0},{3,1},{4,6},{5,7},{6,4},{7,5},{8,10},{9,11},{10,... | collective-permute-start | bytes 589832 | tf_op jit(solution)/shard_map/ppermute | solution.py:409
  65.5 1.6 %collective-permute-start.12 = (f32[12,32,128]{2,1,0:T(8,128)S(1)}, f32[12,32,128]{2,1,0:T(8,128)S(1)}, u32[]{:S(2)}, u32[]{:S(2)}) collective-permute-start(f32[12,32,128]{2,1,0:T(8,128)S(1)} %get-tuple-element.55), channel_id=1, source_target_pairs={{0,3},{1,2},{2,1},{3,0},{4,7},{5,6},{6,5},{7,4},{8,11},{9,10},{10,... | collective-permute-start | bytes 589832 | tf_op jit(solution)/shard_map/ppermute | solution.py:409
  67.1 6.5 %collective-permute-done.10.refs_1_ = f32[12,32,128]{2,1,0:T(8,128)S(1)} collective-permute-done((f32[12,32,128]{2,1,0:T(8,128)S(1)}, f32[12,32,128]{2,1,0:T(8,128)S(1)}, u32[]{:S(2)}, u32[]{:S(2)}) %collective-permute-start.10) | collective-permute-done | bytes 196640 | tf_op jit(solution)/shard_map/ppermute | solution.py:409
  73.6 5.3 %collective-permute-done.12.refs_3_ = f32[12,32,128]{2,1,0:T(8,128)S(1)} collective-permute-done((f32[12,32,128]{2,1,0:T(8,128)S(1)}, f32[12,32,128]{2,1,0:T(8,128)S(1)}, u32[]{:S(2)}, u32[]{:S(2)}) %collective-permute-start.12) | collective-permute-done | bytes 196640 | tf_op jit(solution)/shard_map/ppermute | solution.py:409
  78.9 1.2 %gram.1 = f32[256,128]{1,0:T(8,128)S(1)} custom-call(s32[2]{0:T(128)S(1)} %pad_add_fusion.place_ref, f32[12,32,128]{2,1,0:T(8,128)S(1)} %get-tuple-element.52.refs_0_, f32[12,32,128]{2,1,0:T(8,128)S(1)} %collective-permute-done.10.refs_1_, f32[12,32,128]{2,1,0:T(8,128)S(1)} %collective-permute-done.11.refs_2_, f32[12,32,128]{2,1,0:T(8,128)S(1)} %collective-permute-done.12.refs_3_), custom_call_target="tpu_custom_call" | custom-call | flops 100000000 | bytes 1000000 | tf_op jit(solution)/shard_map/gram/pallas_call | solution.py:410
  80.1 25.8 %all_to_all.9 = f32[256,1,128]{2,1,0:T(1,128)S(1)} all-to-all(f32[256,1,128]{2,1,0:T(1,128)S(1)} %bitcast.11), channel_id=1, replica_groups=mesh['grid'=64,'orb'=4] {'grid','orb'}, dimensions={0} | all-to-all | bytes 262144 | tf_op jit(solution)/shard_map/all_to_all | solution.py:420
  106.0 0.3 reduce_sum.9
  106.3 0.6 reshape.41
  (32 shorter events, 0.4 us)
Async XLA Ops:
  0.6 24.7 %collective-permute-start.2 = (f32[1536,128]{1,0:T(8,128)}, f32[1536,128]{1,0:T(8,128)S(1)}, u32[]{:S(2)}, u32[]{:S(2)}) collective-permute-start(f32[1536,128]{1,0:T(8,128)} %bitcast.16), channel_id=1, source_target_pairs={{0,4},{4,0},{8,12},{12,8},{16,20},{20,16},{24,28},{28,24},{32,36},... | collective-permute-start | bytes 2359304 | tf_op jit(solution)/shard_map/ppermute | solution.py:326
  4.0 33.6 %collective-permute-start.3 = (f32[1536,128]{1,0:T(8,128)}, f32[1536,128]{1,0:T(8,128)S(1)}, u32[]{:S(2)}, u32[]{:S(2)}) collective-permute-start(f32[1536,128]{1,0:T(8,128)} %bitcast.17), channel_id=1, source_target_pairs={{0,252},{4,8},{8,4},{12,16},{16,12},{20,24},{24,20},{28,32},{32,28... | collective-permute-start | bytes 2359304 | tf_op jit(solution)/shard_map/ppermute | solution.py:326
  5.0 0.7 copy-start
  5.8 0.7 copy-start.3
  6.5 1.1 %copy-start.4 = (f32[32,6,8,128]{3,2,1,0:T(8,128)S(1)}, f32[32,6,8,128]{3,2,1,0:T(8,128)}, u32[]{:S(2)}) copy-start(f32[32,6,8,128]{3,2,1,0:T(8,128)} %param.5) | copy-start | bytes 2359300
  7.6 14.9 %copy-start.1 = (f32[3,4,4,128]{3,2,1,0:T(4,128)S(1)}, f32[3,4,4,128]{3,2,1,0:T(4,128)}, u32[]{:S(2)}) copy-start(f32[3,4,4,128]{3,2,1,0:T(4,128)} %value_ref.1) | copy-start | bytes 73732
  7.6 14.9 %copy-start.2 = (f32[6,8,128]{2,1,0:T(8,128)S(1)}, f32[6,8,128]{2,1,0:T(8,128)}, u32[]{:S(2)}) copy-start(f32[6,8,128]{2,1,0:T(8,128)} %param.6) | copy-start | bytes 73732
  11.3 11.1 %collective-permute-start = (f32[32,128]{1,0:T(8,128)S(1)}, f32[32,128]{1,0:T(8,128)S(1)}, u32[]{:S(2)}, u32[]{:S(2)}) collective-permute-start(f32[32,128]{1,0:T(8,128)S(1)} %get-tuple-element.30), channel_id=1, source_target_pairs={{0,4},{4,0},{8,12},{12,8},{16,20},{20,16},{24,28},{28,24},{32,36},... | collective-permute-start | bytes 49160 | tf_op jit(solution)/shard_map/ppermute | solution.py:326
  22.5 4.7 %collective-permute-start.1 = (f32[140,128]{1,0:T(8,128)S(1)}, f32[140,128]{1,0:T(8,128)S(1)}, u32[]{:S(2)}, u32[]{:S(2)}) collective-permute-start(f32[140,128]{1,0:T(8,128)S(1)} %pad_maximum_fusion), channel_id=1, source_target_pairs={{0,252},{4,8},{8,4},{12,16},{16,12},{20,24},{24,20},{28,32},{32,28... | collective-permute-start | bytes 215048 | tf_op jit(solution)/shard_map/ppermute | solution.py:326
  22.6 1.1 %copy-start.5 = (f32[32,6,8,128]{3,2,1,0:T(8,128)S(1)}, f32[32,6,8,128]{3,2,1,0:T(8,128)}, u32[]{:S(2)}) copy-start(f32[32,6,8,128]{3,2,1,0:T(8,128)} %param.5) | copy-start | bytes 2359300
  25.3 32.5 %collective-permute-start.8 = (f32[1536,128]{1,0:T(8,128)S(1)}, f32[1536,128]{1,0:T(8,128)S(1)}, u32[]{:S(2)}, u32[]{:S(2)}) collective-permute-start(f32[1536,128]{1,0:T(8,128)S(1)} %collective-permute-done.2.mate_ref), channel_id=1, source_target_pairs={{0,252},{4,8},{8,4},{12,16},{16,12},{20,24},{24,20},{28,32},{32,28... | collective-permute-start | bytes 2359304 | tf_op jit(solution)/shard_map/ppermute | solution.py:326
  27.2 11.3 %collective-permute-start.4 = (f32[140,128]{1,0:T(8,128)S(1)}, f32[140,128]{1,0:T(8,128)S(1)}, u32[]{:S(2)}, u32[]{:S(2)}) collective-permute-start(f32[140,128]{1,0:T(8,128)S(1)} %collective-permute-done.1.far_msg.message_ref), channel_id=1, source_target_pairs={{0,4},{4,0},{8,12},{12,8},{16,20},{20,16},{24,28},{28,24},{32,36},... | collective-permute-start | bytes 215048 | tf_op jit(solution)/shard_map/ppermute | solution.py:326
  42.2 17.9 %collective-permute-start.7 = (f32[1536,128]{1,0:T(8,128)S(1)}, f32[1536,128]{1,0:T(8,128)S(1)}, u32[]{:S(2)}, u32[]{:S(2)}) collective-permute-start(f32[1536,128]{1,0:T(8,128)S(1)} %get-tuple-element.44.field_ref), channel_id=1, source_target_pairs={{0,4},{4,0},{8,12},{12,8},{16,20},{20,16},{24,28},{28,24},{32,36},... | collective-permute-start | bytes 2359304 | tf_op jit(solution)/shard_map/ppermute | solution.py:326
  42.7 2.0 %collective-permute-start.5 = (f32[32,128]{1,0:T(8,128)S(1)}, f32[32,128]{1,0:T(8,128)S(1)}, u32[]{:S(2)}, u32[]{:S(2)}) collective-permute-start(f32[32,128]{1,0:T(8,128)S(1)} %get-tuple-element.39), channel_id=1, source_target_pairs={{0,4},{4,0},{8,12},{12,8},{16,20},{20,16},{24,28},{28,24},{32,36},... | collective-permute-start | bytes 49160 | tf_op jit(solution)/shard_map/ppermute | solution.py:326
  44.6 5.6 %collective-permute-start.6 = (f32[32,128]{1,0:T(8,128)S(1)}, f32[32,128]{1,0:T(8,128)S(1)}, u32[]{:S(2)}, u32[]{:S(2)}) collective-permute-start(f32[32,128]{1,0:T(8,128)S(1)} %add.16.own_msg), channel_id=1, source_target_pairs={{0,252},{4,8},{8,4},{12,16},{16,12},{20,24},{24,20},{28,32},{32,28... | collective-permute-start | bytes 49160 | tf_op jit(solution)/shard_map/ppermute | solution.py:326
  44.6 2.4 %copy-start.6 = (f32[32,6,8,128]{3,2,1,0:T(8,128)S(1)}, f32[32,6,8,128]{3,2,1,0:T(8,128)}, u32[]{:S(2)}) copy-start(f32[32,6,8,128]{3,2,1,0:T(8,128)} %param.5) | copy-start | bytes 2359300
  50.3 9.8 %collective-permute-start.9 = (f32[32,128]{1,0:T(8,128)S(1)}, f32[32,128]{1,0:T(8,128)S(1)}, u32[]{:S(2)}, u32[]{:S(2)}) collective-permute-start(f32[32,128]{1,0:T(8,128)S(1)} %collective-permute-done.6.far_msg), channel_id=1, source_target_pairs={{0,4},{4,0},{8,12},{12,8},{16,20},{20,16},{24,28},{28,24},{32,36},... | collective-permute-start | bytes 49160 | tf_op jit(solution)/shard_map/ppermute | solution.py:326
  63.6 10.0 %collective-permute-start.10 = (f32[12,32,128]{2,1,0:T(8,128)S(1)}, f32[12,32,128]{2,1,0:T(8,128)S(1)}, u32[]{:S(2)}, u32[]{:S(2)}) collective-permute-start(f32[12,32,128]{2,1,0:T(8,128)S(1)} %get-tuple-element.53), channel_id=1, source_target_pairs={{0,1},{1,0},{2,3},{3,2},{4,5},{5,4},{6,7},{7,6},{8,9},{9,8},{10,11... | collective-permute-start | bytes 589832 | tf_op jit(solution)/shard_map/ppermute | solution.py:409
  63.6 10.0 %collective-permute-start.11 = (f32[12,32,128]{2,1,0:T(8,128)S(1)}, f32[12,32,128]{2,1,0:T(8,128)S(1)}, u32[]{:S(2)}, u32[]{:S(2)}) collective-permute-start(f32[12,32,128]{2,1,0:T(8,128)S(1)} %get-tuple-element.54), channel_id=1, source_target_pairs={{0,2},{1,3},{2,0},{3,1},{4,6},{5,7},{6,4},{7,5},{8,10},{9,11},{10,... | collective-permute-start | bytes 589832 | tf_op jit(solution)/shard_map/ppermute | solution.py:409
  65.5 13.5 %collective-permute-start.12 = (f32[12,32,128]{2,1,0:T(8,128)S(1)}, f32[12,32,128]{2,1,0:T(8,128)S(1)}, u32[]{:S(2)}, u32[]{:S(2)}) collective-permute-start(f32[12,32,128]{2,1,0:T(8,128)S(1)} %get-tuple-element.55), channel_id=1, source_target_pairs={{0,3},{1,2},{2,1},{3,0},{4,7},{5,6},{6,5},{7,4},{8,11},{9,10},{10,... | collective-permute-start | bytes 589832 | tf_op jit(solution)/shard_map/ppermute | solution.py:409

commit v6 on v5

--- a/solution.py
+++ b/solution.py
@@ -68,7 +68,7 @@
         rhs = jnp.concatenate([proj_ref[row + i, :NX, :] for i in (0, 1)], axis=1)
         return acc + dot_nt(lhs, rhs)
 
-    acc = lax.fori_loop(0, ROWS // 2, step, jnp.zeros((2 * orbitals, NX), F32), unroll=4)
+    acc = lax.fori_loop(0, ROWS // 2, step, jnp.zeros((2 * orbitals, NX), F32), unroll=12)
     acc = acc[:orbitals] + acc[orbitals:]
     return jnp.where(lanes(acc.shape) < KAM, acc + pltpu.roll(acc, NX - KAM, 1), 0.0)
 
@@ -184,7 +184,7 @@
             out_ref[spots[j], :] = total
         return carry
 
-    lax.fori_loop(0, orbitals, orbital, 0, unroll=2)
+    lax.fori_loop(0, orbitals, orbital, 0, unroll=4)
 
 
 def shift(x, by):
@@ -219,7 +219,7 @@
             nonlocal_ref[pl.ds(row + i, orbitals, stride=ROWS), :] = both[:, i * NX : (i + 1) * NX]
         return carry
 
-    lax.fori_loop(0, ROWS // 2, spread, 0, unroll=4)
+    lax.fori_loop(0, ROWS // 2, spread, 0, unroll=12)
     if until_here is not None:
         until_here()
     c = weights(scale)
@@ -243,7 +243,7 @@
             out_ref[spots[j], :] = total
         return carry
 
-    lax.fori_loop(0, orbitals, orbital, 0, unroll=2)
+    lax.fori_loop(0, orbitals, orbital, 0, unroll=4)
 
 
 def first_kernel(

time: 107 us -> 106 us (level)
  Pallas kernels: 21.5 us -> 18.7 us
  starting transfers between devices: 37.6 us -> 38.8 us
    pallas_call x8, Pallas kernels: 20.3 us -> 17.5 us  [kernel(): pl.pallas_call(functools.partial(body, **statics), out_shape=outs, in_spe...]
    ppermute x10, starting transfers between devices: 34.1 us -> 35.3 us  [swap(): return lax.ppermute(x, 'grid', pairs)]
  transfers between devices with their start and end apart: 13 -> 13, of which waited for: 5 -> 5; matrix products, arithmetic and copies ran while one was open for 1% -> 1% of each run, Pallas kernels for 16% -> 14%
where the time goes in v6:
time: 106 us; the launch traced here: 105 us
  starting transfers between devices  38.8 us (37%)
  blocking collectives  25.3 us (24%)
  Pallas kernels  18.7 us (18%)
  waiting for transfers between devices  15.9 us (15%)
  local copies, waits for them, and re-layouts  5.28 us (5%)
    ppermute x10, starting transfers between devices, swap(): return lax.ppermute(x, 'grid', pairs)  35.3 us
    all_to_all x1, blocking collectives, on_device(): tiles = lax.all_to_all(tiles, ('grid', 'orb'), 0, 0, tiled=True)  25.3 us
    pallas_call x8, Pallas kernels, kernel(): pl.pallas_call(functools.partial(body, **statics), out_shape=outs, in_spe...  17.5 us
    ppermute x3, waiting for transfers between devices, on_device(): lax.ppermute(blocks[m], 'orb', [(i, i ^ m) for i in range(groups)])  12.4 us
    unnamed x14, local copies, waits for them, and re-layouts  3.7 us
    ppermute x3, starting transfers between devices, on_device(): lax.ppermute(blocks[m], 'orb', [(i, i ^ m) for i in range(groups)])  3.55 us
    ppermute x10, waiting for transfers between devices, swap(): return lax.ppermute(x, 'grid', pairs)  3.55 us
  transfers between devices with their start and end apart: 13, of which 5 were waited for; matrix products, arithmetic and copies ran while one was open for 1% of the time, Pallas kernels for 14%

profile of v6, /device:TPU:1, one launch (start us, length us, event | category | flops | bytes accessed | tf_op | source)
XLA Modules:
  0.0 105.3 jit_solution(16745087402599088402)
XLA Ops:
  0.6 3.3 %collective-permute-start.2 = (f32[1536,128]{1,0:T(8,128)}, f32[1536,128]{1,0:T(8,128)S(1)}, u32[]{:S(2)}, u32[]{:S(2)}) collective-permute-start(f32[1536,128]{1,0:T(8,128)} %bitcast.16), channel_id=1, source_target_pairs={{0,4},{4,0},{8,12},{12,8},{16,20},{20,16},{24,28},{28,24},{32,36},... | collective-permute-start | bytes 2359304 | tf_op jit(solution)/shard_map/ppermute | solution.py:326
  4.0 0.8 reshape.35
  5.0 0.7 copy-done
  5.8 0.7 copy-done.3
  6.5 1.1 %copy-done.4 = f32[32,6,8,128]{3,2,1,0:T(8,128)S(1)} copy-done((f32[32,6,8,128]{3,2,1,0:T(8,128)S(1)}, f32[32,6,8,128]{3,2,1,0:T(8,128)}, u32[]{:S(2)}) %copy-start.4) | copy-done | bytes 786456
  7.6 3.3 %projectors.1 = (bf16[48,144,128]{2,1,0:T(8,128)(2,1)S(1)}, f32[32,128]{1,0:T(8,128)S(1)}, f32[32,128]{1,0:T(8,128)S(1)}) custom-call(s32[2]{0:T(128)S(1)} %pad_add_fusion.place_ref, s32[3,4,128]{2,1,0:T(4,128)S(1)} %copy-done.3, f32[3,4,4,128]{3,2,1,0:T(4,128)S(1)} %copy-done, f32[1,128]{1,0:T(1,128)S(1)} %fusion.kb_ref, f32[1536,128]{1,0:T(8,128)S(1)} %bitcast.18), custom_call_target="tpu_custom_call" | custom-call | flops 1000000000 | bytes 10000000 | tf_op jit(solution)/shard_map/projectors/pallas_call | solution.py:338
  10.9 10.3 %collective-permute-start = (f32[32,128]{1,0:T(8,128)S(1)}, f32[32,128]{1,0:T(8,128)S(1)}, u32[]{:S(2)}, u32[]{:S(2)}) collective-permute-start(f32[32,128]{1,0:T(8,128)S(1)} %get-tuple-element.30), channel_id=1, source_target_pairs={{0,4},{4,0},{8,12},{12,8},{16,20},{20,16},{24,28},{28,24},{32,36},... | collective-permute-start | bytes 49160 | tf_op jit(solution)/shard_map/ppermute | solution.py:326
  21.2 0.8 collective-permute-done
  22.0 0.1 collective-permute-start.1
  22.1 1.1 %copy-done.5 = f32[32,6,8,128]{3,2,1,0:T(8,128)S(1)} copy-done((f32[32,6,8,128]{3,2,1,0:T(8,128)S(1)}, f32[32,6,8,128]{3,2,1,0:T(8,128)}, u32[]{:S(2)}) %copy-start.5) | copy-done | bytes 786456
  23.3 1.5 %slab.3.slab_ref = f32[1536,128]{1,0:T(8,128)S(1)} custom-call(f32[1536,128]{1,0:T(8,128)S(1)} %bitcast.19, f32[48,128]{1,0:T(8,128)S(1)} %bitcast.14), custom_call_target="tpu_custom_call" | custom-call | flops 1000000000 | bytes 10000000 | tf_op jit(solution)/shard_map/slab/pallas_call | solution.py:338
  24.8 1.8 %collective-permute-start.8 = (f32[1536,128]{1,0:T(8,128)S(1)}, f32[1536,128]{1,0:T(8,128)S(1)}, u32[]{:S(2)}, u32[]{:S(2)}) collective-permute-start(f32[1536,128]{1,0:T(8,128)S(1)} %collective-permute-done.2.mate_ref), channel_id=1, source_target_pairs={{0,252},{4,8},{8,4},{12,16},{16,12},{20,24},{24,20},{28,32},{32,28... | collective-permute-start | bytes 2359304 | tf_op jit(solution)/shard_map/ppermute | solution.py:326
  26.6 10.9 %collective-permute-start.4 = (f32[140,128]{1,0:T(8,128)S(1)}, f32[140,128]{1,0:T(8,128)S(1)}, u32[]{:S(2)}, u32[]{:S(2)}) collective-permute-start(f32[140,128]{1,0:T(8,128)S(1)} %collective-permute-done.1.far_msg.message_ref), channel_id=1, source_target_pairs={{0,4},{4,0},{8,12},{12,8},{16,20},{20,16},{24,28},{28,24},{32,36},... | collective-permute-start | bytes 215048 | tf_op jit(solution)/shard_map/ppermute | solution.py:326
  37.6 0.9 collective-permute-done.4.beyond_msg
  38.5 2.7 %first.1 = (f32[1536,128]{1,0:T(8,128)S(1)}, f32[32,128]{1,0:T(8,128)S(1)}, f32[32,128]{1,0:T(8,128)S(1)}, f32[32,128]{1,0:T(8,128)S(1)}, f32[1536,128]{1,0:T(8,128)S(1)}) custom-call(s32[2]{0:T(128)S(1)} %pad_add_fusion.place_ref, f32[1536,128]{1,0:T(8,128)S(1)} %slab.3.slab_ref, f32[1536,128]{1,0:T(8,128)S(1)} %collective-permute-done.2.mate_ref, ...), custom_call_target="tpu_custom_call" | custom-call | flops 1000000000 | bytes 10000000 | tf_op jit(solution)/shard_map/first/pallas_call | solution.py:338
  41.2 0.4 collective-permute-start.7
  41.6 0.2 collective-permute-start.5
  41.8 1.8 %collective-permute-done.5 = f32[32,128]{1,0:T(8,128)S(1)} collective-permute-done((f32[32,128]{1,0:T(8,128)S(1)}, f32[32,128]{1,0:T(8,128)S(1)}, u32[]{:S(2)}, u32[]{:S(2)}) %collective-permute-start.5) | collective-permute-done | bytes 16416 | tf_op jit(solution)/shard_map/ppermute | solution.py:326
  43.6 2.3 %far_projectors.1.proj_ref = bf16[48,144,128]{2,1,0:T(8,128)(2,1)S(1)} custom-call(s32[2]{0:T(128)S(1)} %pad_add_fusion.place_ref, f32[140,128]{1,0:T(8,128)S(1)} %collective-permute-done.1.far_msg.message_ref), custom_call_target="tpu_custom_call" | custom-call | flops 1000000000 | bytes 10000000 | tf_op jit(solution)/shard_map/far_projectors/pallas_call | solution.py:338
  45.9 1.6 %slab.5.slab_ref = f32[1536,128]{1,0:T(8,128)S(1)} custom-call(f32[1536,128]{1,0:T(8,128)S(1)} %get-tuple-element.44.field_ref, f32[48,128]{1,0:T(8,128)S(1)} %bitcast.15, f32[1536,128]{1,0:T(8,128)S(1)} %bitcast.20), custom_call_target="tpu_custom_call" | custom-call | flops 1000000000 | bytes 10000000 | tf_op jit(solution)/shard_map/slab/pallas_call | solution.py:338
  47.6 1.5 %slab.4.slab_ref = f32[1536,128]{1,0:T(8,128)S(1)} custom-call(f32[1536,128]{1,0:T(8,128)S(1)} %get-tuple-element.43.field_ref, f32[48,128]{1,0:T(8,128)S(1)} %slice.22.v_ref), custom_call_target="tpu_custom_call" | custom-call | flops 1000000000 | bytes 10000000 | tf_op jit(solution)/shard_map/slab/pallas_call | solution.py:338
  49.1 8.2 %collective-permute-start.9 = (f32[32,128]{1,0:T(8,128)S(1)}, f32[32,128]{1,0:T(8,128)S(1)}, u32[]{:S(2)}, u32[]{:S(2)}) collective-permute-start(f32[32,128]{1,0:T(8,128)S(1)} %collective-permute-done.6.far_msg), channel_id=1, source_target_pairs={{0,4},{4,0},{8,12},{12,8},{16,20},{20,16},{24,28},{28,24},{32,36},... | collective-permute-start | bytes 49160 | tf_op jit(solution)/shard_map/ppermute | solution.py:326
  57.3 1.7 %far_first.1.far_ref = f32[1536,128]{1,0:T(8,128)S(1)} custom-call(s32[2]{0:T(128)S(1)} %pad_add_fusion.place_ref, f32[1536,128]{1,0:T(8,128)S(1)} %slab.4.slab_ref, f32[1536,128]{1,0:T(8,128)S(1)} %collective-permute-done.8.mate_ref, f32[1536,128]{1,0:T(8,128)S(1)} %bitcast.21, bf16[48,144,128]{2,1,0:T(8,128)(2,1)S(1)} %far_projectors.1.proj_ref, ...), custom_call_target="tpu_custom_call" | custom-call | flops 2000000000 | bytes 10000000 | tf_op jit(solution)/shard_map/far_first/pallas_call | solution.py:338
  59.0 2.8 %second.1 = (f32[1536,128]{1,0:T(8,128)}, f32[12,32,128]{2,1,0:T(8,128)S(1)}, f32[12,32,128]{2,1,0:T(8,128)S(1)}, f32[12,32,128]{2,1,0:T(8,128)S(1)}, f32[12,32,128]{2,1,0:T(8,128)S(1)}) custom-call(s32[2]{0:T(128)S(1)} %pad_add_fusion.place_ref, f32[1536,128]{1,0:T(8,128)S(1)} %slab.5.slab_ref, f32[1536,128]{1,0:T(8,128)S(1)} %collective-permute-done.7.mate_ref, ...), custom_call_target="tpu_custom_call" | custom-call | flops 1000000000 | bytes 10000000 | tf_op jit(solution)/shard_map/second/pallas_call | solution.py:338
  61.9 1.9 %collective-permute-start.11 = (f32[12,32,128]{2,1,0:T(8,128)S(1)}, f32[12,32,128]{2,1,0:T(8,128)S(1)}, u32[]{:S(2)}, u32[]{:S(2)}) collective-permute-start(f32[12,32,128]{2,1,0:T(8,128)S(1)} %get-tuple-element.54), channel_id=1, source_target_pairs={{0,2},{1,3},{2,0},{3,1},{4,6},{5,7},{6,4},{7,5},{8,10},{9,11},{10,... | collective-permute-start | bytes 589832 | tf_op jit(solution)/shard_map/ppermute | solution.py:409
  63.8 1.7 %collective-permute-start.12 = (f32[12,32,128]{2,1,0:T(8,128)S(1)}, f32[12,32,128]{2,1,0:T(8,128)S(1)}, u32[]{:S(2)}, u32[]{:S(2)}) collective-permute-start(f32[12,32,128]{2,1,0:T(8,128)S(1)} %get-tuple-element.55), channel_id=1, source_target_pairs={{0,3},{1,2},{2,1},{3,0},{4,7},{5,6},{6,5},{7,4},{8,11},{9,10},{10,... | collective-permute-start | bytes 589832 | tf_op jit(solution)/shard_map/ppermute | solution.py:409
  65.4 6.5 %collective-permute-done.10.refs_1_ = f32[12,32,128]{2,1,0:T(8,128)S(1)} collective-permute-done((f32[12,32,128]{2,1,0:T(8,128)S(1)}, f32[12,32,128]{2,1,0:T(8,128)S(1)}, u32[]{:S(2)}, u32[]{:S(2)}) %collective-permute-start.10) | collective-permute-done | bytes 196640 | tf_op jit(solution)/shard_map/ppermute | solution.py:409
  71.9 5.9 %collective-permute-done.11.refs_2_ = f32[12,32,128]{2,1,0:T(8,128)S(1)} collective-permute-done((f32[12,32,128]{2,1,0:T(8,128)S(1)}, f32[12,32,128]{2,1,0:T(8,128)S(1)}, u32[]{:S(2)}, u32[]{:S(2)}) %collective-permute-start.11) | collective-permute-done | bytes 196640 | tf_op jit(solution)/shard_map/ppermute | solution.py:409
  77.8 1.2 %gram.1 = f32[256,128]{1,0:T(8,128)S(1)} custom-call(s32[2]{0:T(128)S(1)} %pad_add_fusion.place_ref, f32[12,32,128]{2,1,0:T(8,128)S(1)} %get-tuple-element.52.refs_0_, f32[12,32,128]{2,1,0:T(8,128)S(1)} %collective-permute-done.10.refs_1_, f32[12,32,128]{2,1,0:T(8,128)S(1)} %collective-permute-done.11.refs_2_, f32[12,32,128]{2,1,0:T(8,128)S(1)} %collective-permute-done.12.refs_3_), custom_call_target="tpu_custom_call" | custom-call | flops 100000000 | bytes 1000000 | tf_op jit(solution)/shard_map/gram/pallas_call | solution.py:410
  79.0 25.3 %all_to_all.9 = f32[256,1,128]{2,1,0:T(1,128)S(1)} all-to-all(f32[256,1,128]{2,1,0:T(1,128)S(1)} %bitcast.11), channel_id=1, replica_groups=mesh['grid'=64,'orb'=4] {'grid','orb'}, dimensions={0} | all-to-all | bytes 262144 | tf_op jit(solution)/shard_map/all_to_all | solution.py:420
  104.4 0.3 reduce_sum.9
  104.6 0.6 reshape.41
  (32 shorter events, 0.4 us)
Async XLA Ops:
  0.6 24.2 %collective-permute-start.2 = (f32[1536,128]{1,0:T(8,128)}, f32[1536,128]{1,0:T(8,128)S(1)}, u32[]{:S(2)}, u32[]{:S(2)}) collective-permute-start(f32[1536,128]{1,0:T(8,128)} %bitcast.16), channel_id=1, source_target_pairs={{0,4},{4,0},{8,12},{12,8},{16,20},{20,16},{24,28},{28,24},{32,36},... | collective-permute-start | bytes 2359304 | tf_op jit(solution)/shard_map/ppermute | solution.py:326
  4.0 33.6 %collective-permute-start.3 = (f32[1536,128]{1,0:T(8,128)}, f32[1536,128]{1,0:T(8,128)S(1)}, u32[]{:S(2)}, u32[]{:S(2)}) collective-permute-start(f32[1536,128]{1,0:T(8,128)} %bitcast.17), channel_id=1, source_target_pairs={{0,252},{4,8},{8,4},{12,16},{16,12},{20,24},{24,20},{28,32},{32,28... | collective-permute-start | bytes 2359304 | tf_op jit(solution)/shard_map/ppermute | solution.py:326
  5.0 0.7 copy-start
  5.8 0.7 copy-start.3
  6.5 1.1 %copy-start.4 = (f32[32,6,8,128]{3,2,1,0:T(8,128)S(1)}, f32[32,6,8,128]{3,2,1,0:T(8,128)}, u32[]{:S(2)}) copy-start(f32[32,6,8,128]{3,2,1,0:T(8,128)} %param.5) | copy-start | bytes 2359300
  7.6 14.4 %copy-start.1 = (f32[3,4,4,128]{3,2,1,0:T(4,128)S(1)}, f32[3,4,4,128]{3,2,1,0:T(4,128)}, u32[]{:S(2)}) copy-start(f32[3,4,4,128]{3,2,1,0:T(4,128)} %value_ref.1) | copy-start | bytes 73732
  7.6 14.4 %copy-start.2 = (f32[6,8,128]{2,1,0:T(8,128)S(1)}, f32[6,8,128]{2,1,0:T(8,128)}, u32[]{:S(2)}) copy-start(f32[6,8,128]{2,1,0:T(8,128)} %param.6) | copy-start | bytes 73732
  10.9 11.1 %collective-permute-start = (f32[32,128]{1,0:T(8,128)S(1)}, f32[32,128]{1,0:T(8,128)S(1)}, u32[]{:S(2)}, u32[]{:S(2)}) collective-permute-start(f32[32,128]{1,0:T(8,128)S(1)} %get-tuple-element.30), channel_id=1, source_target_pairs={{0,4},{4,0},{8,12},{12,8},{16,20},{20,16},{24,28},{28,24},{32,36},... | collective-permute-start | bytes 49160 | tf_op jit(solution)/shard_map/ppermute | solution.py:326
  22.0 4.6 %collective-permute-start.1 = (f32[140,128]{1,0:T(8,128)S(1)}, f32[140,128]{1,0:T(8,128)S(1)}, u32[]{:S(2)}, u32[]{:S(2)}) collective-permute-start(f32[140,128]{1,0:T(8,128)S(1)} %pad_maximum_fusion), channel_id=1, source_target_pairs={{0,252},{4,8},{8,4},{12,16},{16,12},{20,24},{24,20},{28,32},{32,28... | collective-permute-start | bytes 215048 | tf_op jit(solution)/shard_map/ppermute | solution.py:326
  22.1 1.1 %copy-start.5 = (f32[32,6,8,128]{3,2,1,0:T(8,128)S(1)}, f32[32,6,8,128]{3,2,1,0:T(8,128)}, u32[]{:S(2)}) copy-start(f32[32,6,8,128]{3,2,1,0:T(8,128)} %param.5) | copy-start | bytes 2359300
  24.8 32.5 %collective-permute-start.8 = (f32[1536,128]{1,0:T(8,128)S(1)}, f32[1536,128]{1,0:T(8,128)S(1)}, u32[]{:S(2)}, u32[]{:S(2)}) collective-permute-start(f32[1536,128]{1,0:T(8,128)S(1)} %collective-permute-done.2.mate_ref), channel_id=1, source_target_pairs={{0,252},{4,8},{8,4},{12,16},{16,12},{20,24},{24,20},{28,32},{32,28... | collective-permute-start | bytes 2359304 | tf_op jit(solution)/shard_map/ppermute | solution.py:326
  26.6 11.8 %collective-permute-start.4 = (f32[140,128]{1,0:T(8,128)S(1)}, f32[140,128]{1,0:T(8,128)S(1)}, u32[]{:S(2)}, u32[]{:S(2)}) collective-permute-start(f32[140,128]{1,0:T(8,128)S(1)} %collective-permute-done.1.far_msg.message_ref), channel_id=1, source_target_pairs={{0,4},{4,0},{8,12},{12,8},{16,20},{20,16},{24,28},{28,24},{32,36},... | collective-permute-start | bytes 215048 | tf_op jit(solution)/shard_map/ppermute | solution.py:326
  41.2 17.9 %collective-permute-start.7 = (f32[1536,128]{1,0:T(8,128)S(1)}, f32[1536,128]{1,0:T(8,128)S(1)}, u32[]{:S(2)}, u32[]{:S(2)}) collective-permute-start(f32[1536,128]{1,0:T(8,128)S(1)} %get-tuple-element.44.field_ref), channel_id=1, source_target_pairs={{0,4},{4,0},{8,12},{12,8},{16,20},{20,16},{24,28},{28,24},{32,36},... | collective-permute-start | bytes 2359304 | tf_op jit(solution)/shard_map/ppermute | solution.py:326
  41.6 2.0 %collective-permute-start.5 = (f32[32,128]{1,0:T(8,128)S(1)}, f32[32,128]{1,0:T(8,128)S(1)}, u32[]{:S(2)}, u32[]{:S(2)}) collective-permute-start(f32[32,128]{1,0:T(8,128)S(1)} %get-tuple-element.39), channel_id=1, source_target_pairs={{0,4},{4,0},{8,12},{12,8},{16,20},{20,16},{24,28},{28,24},{32,36},... | collective-permute-start | bytes 49160 | tf_op jit(solution)/shard_map/ppermute | solution.py:326
  43.6 5.5 %collective-permute-start.6 = (f32[32,128]{1,0:T(8,128)S(1)}, f32[32,128]{1,0:T(8,128)S(1)}, u32[]{:S(2)}, u32[]{:S(2)}) collective-permute-start(f32[32,128]{1,0:T(8,128)S(1)} %add.16.own_msg), channel_id=1, source_target_pairs={{0,252},{4,8},{8,4},{12,16},{16,12},{20,24},{24,20},{28,32},{32,28... | collective-permute-start | bytes 49160 | tf_op jit(solution)/shard_map/ppermute | solution.py:326
  43.6 2.4 %copy-start.6 = (f32[32,6,8,128]{3,2,1,0:T(8,128)S(1)}, f32[32,6,8,128]{3,2,1,0:T(8,128)}, u32[]{:S(2)}) copy-start(f32[32,6,8,128]{3,2,1,0:T(8,128)} %param.5) | copy-start | bytes 2359300
  49.1 9.9 %collective-permute-start.9 = (f32[32,128]{1,0:T(8,128)S(1)}, f32[32,128]{1,0:T(8,128)S(1)}, u32[]{:S(2)}, u32[]{:S(2)}) collective-permute-start(f32[32,128]{1,0:T(8,128)S(1)} %collective-permute-done.6.far_msg), channel_id=1, source_target_pairs={{0,4},{4,0},{8,12},{12,8},{16,20},{20,16},{24,28},{28,24},{32,36},... | collective-permute-start | bytes 49160 | tf_op jit(solution)/shard_map/ppermute | solution.py:326
  61.9 10.0 %collective-permute-start.10 = (f32[12,32,128]{2,1,0:T(8,128)S(1)}, f32[12,32,128]{2,1,0:T(8,128)S(1)}, u32[]{:S(2)}, u32[]{:S(2)}) collective-permute-start(f32[12,32,128]{2,1,0:T(8,128)S(1)} %get-tuple-element.53), channel_id=1, source_target_pairs={{0,1},{1,0},{2,3},{3,2},{4,5},{5,4},{6,7},{7,6},{8,9},{9,8},{10,11... | collective-permute-start | bytes 589832 | tf_op jit(solution)/shard_map/ppermute | solution.py:409
  61.9 15.9 %collective-permute-start.11 = (f32[12,32,128]{2,1,0:T(8,128)S(1)}, f32[12,32,128]{2,1,0:T(8,128)S(1)}, u32[]{:S(2)}, u32[]{:S(2)}) collective-permute-start(f32[12,32,128]{2,1,0:T(8,128)S(1)} %get-tuple-element.54), channel_id=1, source_target_pairs={{0,2},{1,3},{2,0},{3,1},{4,6},{5,7},{6,4},{7,5},{8,10},{9,11},{10,... | collective-permute-start | bytes 589832 | tf_op jit(solution)/shard_map/ppermute | solution.py:409
  63.8 14.0 %collective-permute-start.12 = (f32[12,32,128]{2,1,0:T(8,128)S(1)}, f32[12,32,128]{2,1,0:T(8,128)S(1)}, u32[]{:S(2)}, u32[]{:S(2)}) collective-permute-start(f32[12,32,128]{2,1,0:T(8,128)S(1)} %get-tuple-element.55), channel_id=1, source_target_pairs={{0,3},{1,2},{2,1},{3,0},{4,7},{5,6},{6,5},{7,4},{8,11},{9,10},{10,... | collective-permute-start | bytes 589832 | tf_op jit(solution)/shard_map/ppermute | solution.py:409

commit v7 on v6

--- a/solution.py
+++ b/solution.py
@@ -68,7 +68,7 @@
         rhs = jnp.concatenate([proj_ref[row + i, :NX, :] for i in (0, 1)], axis=1)
         return acc + dot_nt(lhs, rhs)
 
-    acc = lax.fori_loop(0, ROWS // 2, step, jnp.zeros((2 * orbitals, NX), F32), unroll=12)
+    acc = lax.fori_loop(0, ROWS // 2, step, jnp.zeros((2 * orbitals, NX), F32), unroll=24)
     acc = acc[:orbitals] + acc[orbitals:]
     return jnp.where(lanes(acc.shape) < KAM, acc + pltpu.roll(acc, NX - KAM, 1), 0.0)
 
@@ -167,7 +167,7 @@
         planar_ref[at, :] = both[:, :NX] + both[:, NX:] + across
         return carry
 
-    lax.fori_loop(0, orbitals * ROWS // NX, block, 0, unroll=4)
+    lax.fori_loop(0, orbitals * ROWS // NX, block, 0, unroll=12)
 
     def orbital(o, carry):
         base = o * ROWS
@@ -184,7 +184,7 @@
             out_ref[spots[j], :] = total
         return carry
 
-    lax.fori_loop(0, orbitals, orbital, 0, unroll=4)
+    lax.fori_loop(0, orbitals, orbital, 0, unroll=8)
 
 
 def shift(x, by):
@@ -219,7 +219,7 @@
             nonlocal_ref[pl.ds(row + i, orbitals, stride=ROWS), :] = both[:, i * NX : (i + 1) * NX]
         return carry
 
-    lax.fori_loop(0, ROWS // 2, spread, 0, unroll=12)
+    lax.fori_loop(0, ROWS // 2, spread, 0, unroll=24)
     if until_here is not None:
         until_here()
     c = weights(scale)
@@ -243,7 +243,7 @@
             out_ref[spots[j], :] = total
         return carry
 
-    lax.fori_loop(0, orbitals, orbital, 0, unroll=4)
+    lax.fori_loop(0, orbitals, orbital, 0, unroll=8)
 
 
 def first_kernel(

time: 106 us -> 105 us (level)
  Pallas kernels: 18.7 us -> 17.4 us
  starting transfers between devices: 38.8 us -> 39.9 us
    pallas_call x8, Pallas kernels: 17.5 us -> 16.2 us  [kernel(): pl.pallas_call(functools.partial(body, **statics), out_shape=outs, in_spe...]
    ppermute x10, starting transfers between devices: 35.3 us -> 36.4 us  [swap(): return lax.ppermute(x, 'grid', pairs)]
  transfers between devices with their start and end apart: 13 -> 13, of which waited for: 5 -> 5; matrix products, arithmetic and copies ran while one was open for 1% -> 1% of each run, Pallas kernels for 14% -> 13%
where the time goes in v7:
time: 105 us
  starting transfers between devices  39.9 us (38%)
  blocking collectives  25.3 us (24%)
  Pallas kernels  17.4 us (17%)
  waiting for transfers between devices  15.9 us (15%)
  local copies, waits for them, and re-layouts  5.28 us (5%)
    ppermute x10, starting transfers between devices, swap(): return lax.ppermute(x, 'grid', pairs)  36.4 us
    all_to_all x1, blocking collectives, on_device(): tiles = lax.all_to_all(tiles, ('grid', 'orb'), 0, 0, tiled=True)  25.3 us
    pallas_call x8, Pallas kernels, kernel(): pl.pallas_call(functools.partial(body, **statics), out_shape=outs, in_spe...  16.2 us
    ppermute x3, waiting for transfers between devices, on_device(): lax.ppermute(blocks[m], 'orb', [(i, i ^ m) for i in range(groups)])  12.4 us
    unnamed x14, local copies, waits for them, and re-layouts  3.7 us
    ppermute x3, starting transfers between devices, on_device(): lax.ppermute(blocks[m], 'orb', [(i, i ^ m) for i in range(groups)])  3.55 us
    ppermute x10, waiting for transfers between devices, swap(): return lax.ppermute(x, 'grid', pairs)  3.55 us
  transfers between devices with their start and end apart: 13, of which 5 were waited for; matrix products, arithmetic and copies ran while one was open for 1% of the time, Pallas kernels for 13%

profile of v7, /device:TPU:1, one launch (start us, length us, event | category | flops | bytes accessed | tf_op | source)
XLA Modules:
  0.0 105.1 jit_solution(15522934449902219251)
XLA Ops:
  0.6 3.3 %collective-permute-start.2 = (f32[1536,128]{1,0:T(8,128)}, f32[1536,128]{1,0:T(8,128)S(1)}, u32[]{:S(2)}, u32[]{:S(2)}) collective-permute-start(f32[1536,128]{1,0:T(8,128)} %bitcast.16), channel_id=1, source_target_pairs={{0,4},{4,0},{8,12},{12,8},{16,20},{20,16},{24,28},{28,24},{32,36},... | collective-permute-start | bytes 2359304 | tf_op jit(solution)/shard_map/ppermute | solution.py:326
  4.0 0.8 reshape.35
  5.0 0.7 copy-done
  5.8 0.7 copy-done.3
  6.5 1.1 %copy-done.4 = f32[32,6,8,128]{3,2,1,0:T(8,128)S(1)} copy-done((f32[32,6,8,128]{3,2,1,0:T(8,128)S(1)}, f32[32,6,8,128]{3,2,1,0:T(8,128)}, u32[]{:S(2)}) %copy-start.4) | copy-done | bytes 786456
  7.6 3.7 %projectors.1 = (bf16[48,144,128]{2,1,0:T(8,128)(2,1)S(1)}, f32[32,128]{1,0:T(8,128)S(1)}, f32[32,128]{1,0:T(8,128)S(1)}) custom-call(s32[2]{0:T(128)S(1)} %pad_add_fusion.place_ref, s32[3,4,128]{2,1,0:T(4,128)S(1)} %copy-done.3, f32[3,4,4,128]{3,2,1,0:T(4,128)S(1)} %copy-done, f32[1,128]{1,0:T(1,128)S(1)} %fusion.kb_ref, f32[1536,128]{1,0:T(8,128)S(1)} %bitcast.18), custom_call_target="tpu_custom_call" | custom-call | flops 1000000000 | bytes 10000000 | tf_op jit(solution)/shard_map/projectors/pallas_call | solution.py:338
  11.3 10.3 %collective-permute-start = (f32[32,128]{1,0:T(8,128)S(1)}, f32[32,128]{1,0:T(8,128)S(1)}, u32[]{:S(2)}, u32[]{:S(2)}) collective-permute-start(f32[32,128]{1,0:T(8,128)S(1)} %get-tuple-element.30), channel_id=1, source_target_pairs={{0,4},{4,0},{8,12},{12,8},{16,20},{20,16},{24,28},{28,24},{32,36},... | collective-permute-start | bytes 49160 | tf_op jit(solution)/shard_map/ppermute | solution.py:326
  21.6 0.8 collective-permute-done
  22.5 0.1 collective-permute-start.1
  22.6 1.1 %copy-done.5 = f32[32,6,8,128]{3,2,1,0:T(8,128)S(1)} copy-done((f32[32,6,8,128]{3,2,1,0:T(8,128)S(1)}, f32[32,6,8,128]{3,2,1,0:T(8,128)}, u32[]{:S(2)}) %copy-start.5) | copy-done | bytes 786456
  23.7 1.1 %slab.3.slab_ref = f32[1536,128]{1,0:T(8,128)S(1)} custom-call(f32[1536,128]{1,0:T(8,128)S(1)} %bitcast.19, f32[48,128]{1,0:T(8,128)S(1)} %bitcast.14), custom_call_target="tpu_custom_call" | custom-call | flops 1000000000 | bytes 10000000 | tf_op jit(solution)/shard_map/slab/pallas_call | solution.py:338
  24.9 1.8 %collective-permute-start.8 = (f32[1536,128]{1,0:T(8,128)S(1)}, f32[1536,128]{1,0:T(8,128)S(1)}, u32[]{:S(2)}, u32[]{:S(2)}) collective-permute-start(f32[1536,128]{1,0:T(8,128)S(1)} %collective-permute-done.2.mate_ref), channel_id=1, source_target_pairs={{0,252},{4,8},{8,4},{12,16},{16,12},{20,24},{24,20},{28,32},{32,28... | collective-permute-start | bytes 2359304 | tf_op jit(solution)/shard_map/ppermute | solution.py:326
  26.7 10.8 %collective-permute-start.4 = (f32[140,128]{1,0:T(8,128)S(1)}, f32[140,128]{1,0:T(8,128)S(1)}, u32[]{:S(2)}, u32[]{:S(2)}) collective-permute-start(f32[140,128]{1,0:T(8,128)S(1)} %collective-permute-done.1.far_msg.message_ref), channel_id=1, source_target_pairs={{0,4},{4,0},{8,12},{12,8},{16,20},{20,16},{24,28},{28,24},{32,36},... | collective-permute-start | bytes 215048 | tf_op jit(solution)/shard_map/ppermute | solution.py:326
  37.6 0.9 collective-permute-done.4.beyond_msg
  38.5 2.4 %first.1 = (f32[1536,128]{1,0:T(8,128)S(1)}, f32[32,128]{1,0:T(8,128)S(1)}, f32[32,128]{1,0:T(8,128)S(1)}, f32[32,128]{1,0:T(8,128)S(1)}, f32[1536,128]{1,0:T(8,128)S(1)}) custom-call(s32[2]{0:T(128)S(1)} %pad_add_fusion.place_ref, f32[1536,128]{1,0:T(8,128)S(1)} %slab.3.slab_ref, f32[1536,128]{1,0:T(8,128)S(1)} %collective-permute-done.2.mate_ref, ...), custom_call_target="tpu_custom_call" | custom-call | flops 1000000000 | bytes 10000000 | tf_op jit(solution)/shard_map/first/pallas_call | solution.py:338
  40.9 0.4 collective-permute-start.7
  41.3 0.2 collective-permute-start.5
  41.5 1.8 %collective-permute-done.5 = f32[32,128]{1,0:T(8,128)S(1)} collective-permute-done((f32[32,128]{1,0:T(8,128)S(1)}, f32[32,128]{1,0:T(8,128)S(1)}, u32[]{:S(2)}, u32[]{:S(2)}) %collective-permute-start.5) | collective-permute-done | bytes 16416 | tf_op jit(solution)/shard_map/ppermute | solution.py:326
  43.3 2.3 %far_projectors.1.proj_ref = bf16[48,144,128]{2,1,0:T(8,128)(2,1)S(1)} custom-call(s32[2]{0:T(128)S(1)} %pad_add_fusion.place_ref, f32[140,128]{1,0:T(8,128)S(1)} %collective-permute-done.1.far_msg.message_ref), custom_call_target="tpu_custom_call" | custom-call | flops 1000000000 | bytes 10000000 | tf_op jit(solution)/shard_map/far_projectors/pallas_call | solution.py:338
  45.7 1.2 %slab.5.slab_ref = f32[1536,128]{1,0:T(8,128)S(1)} custom-call(f32[1536,128]{1,0:T(8,128)S(1)} %get-tuple-element.44.field_ref, f32[48,128]{1,0:T(8,128)S(1)} %bitcast.15, f32[1536,128]{1,0:T(8,128)S(1)} %bitcast.20), custom_call_target="tpu_custom_call" | custom-call | flops 1000000000 | bytes 10000000 | tf_op jit(solution)/shard_map/slab/pallas_call | solution.py:338
  46.9 1.1 %slab.4.slab_ref = f32[1536,128]{1,0:T(8,128)S(1)} custom-call(f32[1536,128]{1,0:T(8,128)S(1)} %get-tuple-element.43.field_ref, f32[48,128]{1,0:T(8,128)S(1)} %slice.22.v_ref), custom_call_target="tpu_custom_call" | custom-call | flops 1000000000 | bytes 10000000 | tf_op jit(solution)/shard_map/slab/pallas_call | solution.py:338
  48.1 9.4 %collective-permute-start.9 = (f32[32,128]{1,0:T(8,128)S(1)}, f32[32,128]{1,0:T(8,128)S(1)}, u32[]{:S(2)}, u32[]{:S(2)}) collective-permute-start(f32[32,128]{1,0:T(8,128)S(1)} %collective-permute-done.6.far_msg), channel_id=1, source_target_pairs={{0,4},{4,0},{8,12},{12,8},{16,20},{20,16},{24,28},{28,24},{32,36},... | collective-permute-start | bytes 49160 | tf_op jit(solution)/shard_map/ppermute | solution.py:326
  57.5 1.6 %far_first.1.far_ref = f32[1536,128]{1,0:T(8,128)S(1)} custom-call(s32[2]{0:T(128)S(1)} %pad_add_fusion.place_ref, f32[1536,128]{1,0:T(8,128)S(1)} %slab.4.slab_ref, f32[1536,128]{1,0:T(8,128)S(1)} %collective-permute-done.8.mate_ref, f32[1536,128]{1,0:T(8,128)S(1)} %bitcast.21, bf16[48,144,128]{2,1,0:T(8,128)(2,1)S(1)} %far_projectors.1.proj_ref, ...), custom_call_target="tpu_custom_call" | custom-call | flops 2000000000 | bytes 10000000 | tf_op jit(solution)/shard_map/far_first/pallas_call | solution.py:338
  59.0 2.7 %second.1 = (f32[1536,128]{1,0:T(8,128)}, f32[12,32,128]{2,1,0:T(8,128)S(1)}, f32[12,32,128]{2,1,0:T(8,128)S(1)}, f32[12,32,128]{2,1,0:T(8,128)S(1)}, f32[12,32,128]{2,1,0:T(8,128)S(1)}) custom-call(s32[2]{0:T(128)S(1)} %pad_add_fusion.place_ref, f32[1536,128]{1,0:T(8,128)S(1)} %slab.5.slab_ref, f32[1536,128]{1,0:T(8,128)S(1)} %collective-permute-done.7.mate_ref, ...), custom_call_target="tpu_custom_call" | custom-call | flops 1000000000 | bytes 10000000 | tf_op jit(solution)/shard_map/second/pallas_call | solution.py:338
  61.7 1.8 %collective-permute-start.11 = (f32[12,32,128]{2,1,0:T(8,128)S(1)}, f32[12,32,128]{2,1,0:T(8,128)S(1)}, u32[]{:S(2)}, u32[]{:S(2)}) collective-permute-start(f32[12,32,128]{2,1,0:T(8,128)S(1)} %get-tuple-element.54), channel_id=1, source_target_pairs={{0,2},{1,3},{2,0},{3,1},{4,6},{5,7},{6,4},{7,5},{8,10},{9,11},{10,... | collective-permute-start | bytes 589832 | tf_op jit(solution)/shard_map/ppermute | solution.py:409
  63.6 1.7 %collective-permute-start.12 = (f32[12,32,128]{2,1,0:T(8,128)S(1)}, f32[12,32,128]{2,1,0:T(8,128)S(1)}, u32[]{:S(2)}, u32[]{:S(2)}) collective-permute-start(f32[12,32,128]{2,1,0:T(8,128)S(1)} %get-tuple-element.55), channel_id=1, source_target_pairs={{0,3},{1,2},{2,1},{3,0},{4,7},{5,6},{6,5},{7,4},{8,11},{9,10},{10,... | collective-permute-start | bytes 589832 | tf_op jit(solution)/shard_map/ppermute | solution.py:409
  65.3 6.5 %collective-permute-done.10.refs_1_ = f32[12,32,128]{2,1,0:T(8,128)S(1)} collective-permute-done((f32[12,32,128]{2,1,0:T(8,128)S(1)}, f32[12,32,128]{2,1,0:T(8,128)S(1)}, u32[]{:S(2)}, u32[]{:S(2)}) %collective-permute-start.10) | collective-permute-done | bytes 196640 | tf_op jit(solution)/shard_map/ppermute | solution.py:409
  71.7 5.9 %collective-permute-done.11.refs_2_ = f32[12,32,128]{2,1,0:T(8,128)S(1)} collective-permute-done((f32[12,32,128]{2,1,0:T(8,128)S(1)}, f32[12,32,128]{2,1,0:T(8,128)S(1)}, u32[]{:S(2)}, u32[]{:S(2)}) %collective-permute-start.11) | collective-permute-done | bytes 196640 | tf_op jit(solution)/shard_map/ppermute | solution.py:409
  77.7 1.2 %gram.1 = f32[256,128]{1,0:T(8,128)S(1)} custom-call(s32[2]{0:T(128)S(1)} %pad_add_fusion.place_ref, f32[12,32,128]{2,1,0:T(8,128)S(1)} %get-tuple-element.52.refs_0_, f32[12,32,128]{2,1,0:T(8,128)S(1)} %collective-permute-done.10.refs_1_, f32[12,32,128]{2,1,0:T(8,128)S(1)} %collective-permute-done.11.refs_2_, f32[12,32,128]{2,1,0:T(8,128)S(1)} %collective-permute-done.12.refs_3_), custom_call_target="tpu_custom_call" | custom-call | flops 100000000 | bytes 1000000 | tf_op jit(solution)/shard_map/gram/pallas_call | solution.py:410
  78.9 25.3 %all_to_all.9 = f32[256,1,128]{2,1,0:T(1,128)S(1)} all-to-all(f32[256,1,128]{2,1,0:T(1,128)S(1)} %bitcast.11), channel_id=1, replica_groups=mesh['grid'=64,'orb'=4] {'grid','orb'}, dimensions={0} | all-to-all | bytes 262144 | tf_op jit(solution)/shard_map/all_to_all | solution.py:420
  104.2 0.3 reduce_sum.9
  104.4 0.6 reshape.41
  (32 shorter events, 0.4 us)
Async XLA Ops:
  0.6 24.2 %collective-permute-start.2 = (f32[1536,128]{1,0:T(8,128)}, f32[1536,128]{1,0:T(8,128)S(1)}, u32[]{:S(2)}, u32[]{:S(2)}) collective-permute-start(f32[1536,128]{1,0:T(8,128)} %bitcast.16), channel_id=1, source_target_pairs={{0,4},{4,0},{8,12},{12,8},{16,20},{20,16},{24,28},{28,24},{32,36},... | collective-permute-start | bytes 2359304 | tf_op jit(solution)/shard_map/ppermute | solution.py:326
  4.0 33.6 %collective-permute-start.3 = (f32[1536,128]{1,0:T(8,128)}, f32[1536,128]{1,0:T(8,128)S(1)}, u32[]{:S(2)}, u32[]{:S(2)}) collective-permute-start(f32[1536,128]{1,0:T(8,128)} %bitcast.17), channel_id=1, source_target_pairs={{0,252},{4,8},{8,4},{12,16},{16,12},{20,24},{24,20},{28,32},{32,28... | collective-permute-start | bytes 2359304 | tf_op jit(solution)/shard_map/ppermute | solution.py:326
  5.0 0.7 copy-start
  5.8 0.7 copy-start.3
  6.5 1.1 %copy-start.4 = (f32[32,6,8,128]{3,2,1,0:T(8,128)S(1)}, f32[32,6,8,128]{3,2,1,0:T(8,128)}, u32[]{:S(2)}) copy-start(f32[32,6,8,128]{3,2,1,0:T(8,128)} %param.5) | copy-start | bytes 2359300
  7.6 14.9 %copy-start.1 = (f32[3,4,4,128]{3,2,1,0:T(4,128)S(1)}, f32[3,4,4,128]{3,2,1,0:T(4,128)}, u32[]{:S(2)}) copy-start(f32[3,4,4,128]{3,2,1,0:T(4,128)} %value_ref.1) | copy-start | bytes 73732
  7.6 14.9 %copy-start.2 = (f32[6,8,128]{2,1,0:T(8,128)S(1)}, f32[6,8,128]{2,1,0:T(8,128)}, u32[]{:S(2)}) copy-start(f32[6,8,128]{2,1,0:T(8,128)} %param.6) | copy-start | bytes 73732
  11.3 11.1 %collective-permute-start = (f32[32,128]{1,0:T(8,128)S(1)}, f32[32,128]{1,0:T(8,128)S(1)}, u32[]{:S(2)}, u32[]{:S(2)}) collective-permute-start(f32[32,128]{1,0:T(8,128)S(1)} %get-tuple-element.30), channel_id=1, source_target_pairs={{0,4},{4,0},{8,12},{12,8},{16,20},{20,16},{24,28},{28,24},{32,36},... | collective-permute-start | bytes 49160 | tf_op jit(solution)/shard_map/ppermute | solution.py:326
  22.5 4.2 %collective-permute-start.1 = (f32[140,128]{1,0:T(8,128)S(1)}, f32[140,128]{1,0:T(8,128)S(1)}, u32[]{:S(2)}, u32[]{:S(2)}) collective-permute-start(f32[140,128]{1,0:T(8,128)S(1)} %pad_maximum_fusion), channel_id=1, source_target_pairs={{0,252},{4,8},{8,4},{12,16},{16,12},{20,24},{24,20},{28,32},{32,28... | collective-permute-start | bytes 215048 | tf_op jit(solution)/shard_map/ppermute | solution.py:326
  22.6 1.1 %copy-start.5 = (f32[32,6,8,128]{3,2,1,0:T(8,128)S(1)}, f32[32,6,8,128]{3,2,1,0:T(8,128)}, u32[]{:S(2)}) copy-start(f32[32,6,8,128]{3,2,1,0:T(8,128)} %param.5) | copy-start | bytes 2359300
  24.9 32.6 %collective-permute-start.8 = (f32[1536,128]{1,0:T(8,128)S(1)}, f32[1536,128]{1,0:T(8,128)S(1)}, u32[]{:S(2)}, u32[]{:S(2)}) collective-permute-start(f32[1536,128]{1,0:T(8,128)S(1)} %collective-permute-done.2.mate_ref), channel_id=1, source_target_pairs={{0,252},{4,8},{8,4},{12,16},{16,12},{20,24},{24,20},{28,32},{32,28... | collective-permute-start | bytes 2359304 | tf_op jit(solution)/shard_map/ppermute | solution.py:326
  26.7 11.8 %collective-permute-start.4 = (f32[140,128]{1,0:T(8,128)S(1)}, f32[140,128]{1,0:T(8,128)S(1)}, u32[]{:S(2)}, u32[]{:S(2)}) collective-permute-start(f32[140,128]{1,0:T(8,128)S(1)} %collective-permute-done.1.far_msg.message_ref), channel_id=1, source_target_pairs={{0,4},{4,0},{8,12},{12,8},{16,20},{20,16},{24,28},{28,24},{32,36},... | collective-permute-start | bytes 215048 | tf_op jit(solution)/shard_map/ppermute | solution.py:326
  40.9 18.1 %collective-permute-start.7 = (f32[1536,128]{1,0:T(8,128)S(1)}, f32[1536,128]{1,0:T(8,128)S(1)}, u32[]{:S(2)}, u32[]{:S(2)}) collective-permute-start(f32[1536,128]{1,0:T(8,128)S(1)} %get-tuple-element.44.field_ref), channel_id=1, source_target_pairs={{0,4},{4,0},{8,12},{12,8},{16,20},{20,16},{24,28},{28,24},{32,36},... | collective-permute-start | bytes 2359304 | tf_op jit(solution)/shard_map/ppermute | solution.py:326
  41.3 2.0 %collective-permute-start.5 = (f32[32,128]{1,0:T(8,128)S(1)}, f32[32,128]{1,0:T(8,128)S(1)}, u32[]{:S(2)}, u32[]{:S(2)}) collective-permute-start(f32[32,128]{1,0:T(8,128)S(1)} %get-tuple-element.39), channel_id=1, source_target_pairs={{0,4},{4,0},{8,12},{12,8},{16,20},{20,16},{24,28},{28,24},{32,36},... | collective-permute-start | bytes 49160 | tf_op jit(solution)/shard_map/ppermute | solution.py:326
  43.3 4.7 %collective-permute-start.6 = (f32[32,128]{1,0:T(8,128)S(1)}, f32[32,128]{1,0:T(8,128)S(1)}, u32[]{:S(2)}, u32[]{:S(2)}) collective-permute-start(f32[32,128]{1,0:T(8,128)S(1)} %add.16.own_msg), channel_id=1, source_target_pairs={{0,252},{4,8},{8,4},{12,16},{16,12},{20,24},{24,20},{28,32},{32,28... | collective-permute-start | bytes 49160 | tf_op jit(solution)/shard_map/ppermute | solution.py:326
  43.3 2.4 %copy-start.6 = (f32[32,6,8,128]{3,2,1,0:T(8,128)S(1)}, f32[32,6,8,128]{3,2,1,0:T(8,128)}, u32[]{:S(2)}) copy-start(f32[32,6,8,128]{3,2,1,0:T(8,128)} %param.5) | copy-start | bytes 2359300
  48.1 11.0 %collective-permute-start.9 = (f32[32,128]{1,0:T(8,128)S(1)}, f32[32,128]{1,0:T(8,128)S(1)}, u32[]{:S(2)}, u32[]{:S(2)}) collective-permute-start(f32[32,128]{1,0:T(8,128)S(1)} %collective-permute-done.6.far_msg), channel_id=1, source_target_pairs={{0,4},{4,0},{8,12},{12,8},{16,20},{20,16},{24,28},{28,24},{32,36},... | collective-permute-start | bytes 49160 | tf_op jit(solution)/shard_map/ppermute | solution.py:326
  61.7 10.0 %collective-permute-start.10 = (f32[12,32,128]{2,1,0:T(8,128)S(1)}, f32[12,32,128]{2,1,0:T(8,128)S(1)}, u32[]{:S(2)}, u32[]{:S(2)}) collective-permute-start(f32[12,32,128]{2,1,0:T(8,128)S(1)} %get-tuple-element.53), channel_id=1, source_target_pairs={{0,1},{1,0},{2,3},{3,2},{4,5},{5,4},{6,7},{7,6},{8,9},{9,8},{10,11... | collective-permute-start | bytes 589832 | tf_op jit(solution)/shard_map/ppermute | solution.py:409
  61.7 15.9 %collective-permute-start.11 = (f32[12,32,128]{2,1,0:T(8,128)S(1)}, f32[12,32,128]{2,1,0:T(8,128)S(1)}, u32[]{:S(2)}, u32[]{:S(2)}) collective-permute-start(f32[12,32,128]{2,1,0:T(8,128)S(1)} %get-tuple-element.54), channel_id=1, source_target_pairs={{0,2},{1,3},{2,0},{3,1},{4,6},{5,7},{6,4},{7,5},{8,10},{9,11},{10,... | collective-permute-start | bytes 589832 | tf_op jit(solution)/shard_map/ppermute | solution.py:409
  63.6 14.1 %collective-permute-start.12 = (f32[12,32,128]{2,1,0:T(8,128)S(1)}, f32[12,32,128]{2,1,0:T(8,128)S(1)}, u32[]{:S(2)}, u32[]{:S(2)}) collective-permute-start(f32[12,32,128]{2,1,0:T(8,128)S(1)} %get-tuple-element.55), channel_id=1, source_target_pairs={{0,3},{1,2},{2,1},{3,0},{4,7},{5,6},{6,5},{7,4},{8,11},{9,10},{10,... | collective-permute-start | bytes 589832 | tf_op jit(solution)/shard_map/ppermute | solution.py:409
